TPU v7x, 256 devices: a whole 4x4x8 slice. The times are simulated.
256 devices in a mesh: mode: 64 (over y, x_lo, z), pencil: 4 (over x_hi, core).
Axes of the slice: x: 4 (x_hi: 2, x_lo: 2; x = x_hi * 2 + x_lo), y: 4, z: 8, core: 2. Of those that a mesh axis runs over, the one named last changes fastest.
Arguments:
- cotangent: bfloat16 [256, 8, 256, 512], P('mode', None, 'pencil'), may hold values from -6 to 6
- radial_ops: bfloat16 [256, 256, 256], P('mode'), may hold values from -0.375 to 0.375
- lengths: int32 [256], P('mode'), may hold values from 64 to 256, as said below
- couple_one: float32 [8, 8], replicated, may hold values from -1.5 to 1.5
- couple_two: float32 [8, 8], replicated, may hold values from -1.5 to 1.5
- axial_damping: float32 [256, 512], P('mode'), may hold values from 0.2 to 1
Outputs:
- sensitivity: bfloat16 [256, 8, 256, 512], P('mode', None, None, 'pencil')
Inputs may be any that keep to these rules, and one draw needn't show every extreme that they name: Mode m keeps its first lengths[m] radial coefficients; mode 0 keeps all 256 and mode 256 / 2 keeps 256 / 4.
All inputs are finite; a program needn't handle non-finite values.
Results may differ from a plain program's by a relative error of at most 0.01.
Values may be sent and summed in bfloat16 or wider, within the bound.
No kernel may reach another device: no remote copies, remote signals or barrier semaphores. Data moves between devices by JAX's collectives and lax.ppermute only.
A program may use at most 128 MiB of HBM per device.

v0:
```python
import functools
import math

import jax
import jax.numpy as jnp
import numpy as np
from jax import lax
from jax.experimental import pallas as pl
from jax.experimental.pallas import tpu as pltpu
from jax.sharding import PartitionSpec as P

BF = jnp.bfloat16
F32 = jnp.float32
SUB = 16
VMEM_LIMIT = 48 * 1024 * 1024


def cosine_table(count):
    points = np.arange(count, dtype=np.float32)
    scale = np.where(points == 0.0, np.float32(math.sqrt(1.0 / count)), np.float32(math.sqrt(2.0 / count)))
    angle = np.float32(math.pi) * (points[:, None] + np.float32(0.5)) * points[None, :] / np.float32(count)
    return (np.cos(angle).astype(np.float32) * scale[None, :].astype(np.float32)).astype(BF)


def vmem(count):
    return [pl.BlockSpec(memory_space=pltpu.VMEM)] * count


def call(kernel, name, args, outs, flops, scratch=(), smem=0):
    moved = sum(a.size * a.dtype.itemsize for a in args)
    moved += sum(math.prod(o.shape) * o.dtype.itemsize for o in outs)
    return pl.pallas_call(
        kernel,
        out_shape=outs,
        in_specs=[pl.BlockSpec(memory_space=pltpu.SMEM)] * smem + vmem(len(args) - smem),
        out_specs=vmem(len(outs)),
        scratch_shapes=list(scratch),
        compiler_params=pltpu.CompilerParams(vmem_limit_bytes=VMEM_LIMIT),
        cost_estimate=pl.CostEstimate(flops=flops, bytes_accessed=moved, transcendentals=0),
        name=name,
    )(*args)


def dot(a, b):
    return jnp.dot(a, b, preferred_element_type=F32)


def dot_nt(a, b):
    return lax.dot_general(a, b, (((1,), (1,)), ((), ())), preferred_element_type=F32)


def shape(*dims, dtype=BF):
    return jax.ShapeDtypeStruct(dims, dtype)


def prep_kernel(peers, me_ref, len_ref, q_ref, damp_ref, rad_ref, one_ref, two_ref, m1_ref, mpp_ref, rpp_ref, rp_ref, w_ref, qp_ref):
    me = me_ref[0]
    nz = q_ref.shape[0]
    block = nz // peers
    for k in range(peers):
        start = pl.multiple_of((me ^ k) * block, block)
        qp_ref[k * block : (k + 1) * block, :] = q_ref[pl.ds(start, block), :]
    qp = qp_ref[...]
    for m in range(damp_ref.shape[0]):
        factor = damp_ref[m : m + 1, :]
        for table, out in ((q_ref, m1_ref), (qp_ref, mpp_ref)):
            scaled = table[...].astype(F32) * factor
            high = scaled.astype(BF)
            low = (scaled - high.astype(F32)).astype(BF)
            out[m] = (dot_nt(high, qp) + dot_nt(low, qp)).astype(BF)
    nr = rad_ref.shape[1]
    rows = nr // peers
    for m in range(rad_ref.shape[0]):
        parts = []
        for k in range(peers):
            start = pl.multiple_of((me ^ k) * rows, rows)
            part = rad_ref[m, pl.ds(start, rows), :].astype(F32)
            index = start + lax.broadcasted_iota(jnp.int32, (rows, nr), 0)
            parts.append(jnp.where(index < len_ref[m], part, 0.0))
        turned = jnp.concatenate(parts, axis=0).T.astype(BF)
        rp_ref[m] = turned
        for k in range(peers):
            start = pl.multiple_of((me ^ k) * rows, rows)
            rpp_ref[m, k * rows : (k + 1) * rows, :] = rp_ref[m, pl.ds(start, rows), :]
    comp = one_ref.shape[0]
    wide = comp * SUB
    row = lax.broadcasted_iota(jnp.int32, (wide, comp), 0) // SUB
    spread = jnp.where(row == lax.broadcasted_iota(jnp.int32, (wide, comp), 1), 1.0, 0.0).astype(BF)
    i = lax.broadcasted_iota(jnp.int32, (wide, wide), 0) % SUB
    j = lax.broadcasted_iota(jnp.int32, (wide, wide), 1) % SUB
    for at, ref in enumerate((one_ref, two_ref)):
        turned = ref[...].astype(BF).astype(F32)
        half = lax.dot_general(spread, turned.astype(BF), (((1,), (1,)), ((), ())), preferred_element_type=F32)
        full = dot_nt(half.astype(BF), spread)
        full = jnp.where(i == j, full, 0.0).astype(BF)
        w_ref[:, (2 * at) * wide : (2 * at + 1) * wide] = full
        w_ref[:, (2 * at + 1) * wide : (2 * at + 2) * wide] = full


def prepare(peers, me, lengths, table, damping, radial, one, two):
    modes, nz = damping.shape
    nr = radial.shape[1]
    wide = one.shape[0] * SUB
    return call(
        functools.partial(prep_kernel, peers),
        "prepare",
        (me, lengths, table, damping, radial, one, two),
        [
            shape(modes, nz, nz),
            shape(modes, nz, nz),
            shape(modes, nr, nr),
            shape(modes, nr, nr),
            shape(wide, 4 * wide),
        ],
        8 * modes * nz**3,
        scratch=[pltpu.VMEM((nz, nz), BF)],
        smem=2,
    )


def around(own, before, after, m):
    count = len(own)

    def at(i):
        if i < 0:
            return before[-1 - i]
        return own[i] if i < count else after[i - count]

    return [at(m - 1), at(m + 1), at(m - 2), at(m + 2)]


def couple_axial_kernel(peers, modes, count, *refs):
    x_ref = refs[0]
    before, after = refs[1:3], refs[3:5]
    w_ref, m_ref = refs[5:7]
    outs, a_ref = refs[7 : 7 + peers], refs[7 + peers]
    own = [x_ref.at[i] for i in range(count)]
    comp, rows, nz = own[0].shape
    wide = comp * SUB
    block = nz // peers
    for at, m in enumerate(modes):
        near = around(own, before, after, m)
        for b in range(rows // SUB):
            part = slice(b * SUB, (b + 1) * SUB)
            field = jnp.concatenate([ref[:, part, :].reshape(wide, nz) for ref in near], axis=0)
            mixed = dot(w_ref[...], field) + own[m][:, part, :].reshape(wide, nz).astype(F32)
            a_ref[b * wide : (b + 1) * wide, :] = mixed.astype(BF)
        result = dot(a_ref[...], m_ref[m]).astype(BF)
        for b in range(rows // SUB):
            for k in range(peers):
                piece = result[b * wide : (b + 1) * wide, k * block : (k + 1) * block]
                outs[k][at, :, b * SUB : (b + 1) * SUB, :] = piece.reshape(comp, SUB, block)


def couple_axial(peers, modes, x, before, after, weights, matrices):
    count, comp, rows, nz = x.shape
    return call(
        functools.partial(couple_axial_kernel, peers, modes, count),
        "couple_axial",
        (x, *before, *after, weights, matrices),
        [shape(len(modes), comp, rows, nz // peers)] * peers,
        len(modes) * comp * rows * nz * 2 * (nz + 4 * comp * SUB),
        scratch=[pltpu.VMEM((comp * rows, nz), BF)],
    )


def radial_kernel(peers, modes, *refs):
    pieces, r_ref, outs = refs[:peers], refs[peers], refs[peers + 1 :]
    comp = pieces[0].shape[1]
    block = pieces[0].shape[3]
    for at, m in enumerate(modes):
        matrix = r_ref[m]
        for c in range(0, comp, 2):
            field = jnp.concatenate(
                [jnp.concatenate([p[at, c], p[at, c + 1]], axis=1) for p in pieces], axis=0
            )
            result = dot(matrix, field).astype(BF)
            out = outs[at] if len(outs) > 1 else outs[0].at[at]
            out[c] = result[:, :block]
            out[c + 1] = result[:, block:]


def radial(peers, modes, pieces, matrices, separate):
    count, comp, rows, block = pieces[0].shape
    nr = rows * peers
    outs = [shape(comp, nr, block)] * count if separate else [shape(count, comp, nr, block)]
    return call(
        functools.partial(radial_kernel, peers, modes),
        "radial",
        (*pieces, matrices),
        outs,
        count * comp * nr * nr * block * 2,
    )


def couple_kernel(peers, modes, count, *refs):
    own, before, after = refs[:count], refs[count : count + 2], refs[count + 2 : count + 4]
    w_ref = refs[count + 4]
    outs = refs[count + 5 :]
    comp, nr, block = own[0].shape
    rows = nr // peers
    wide = comp * SUB
    for at, m in enumerate(modes):
        near = around(own, before, after, m)

        def side(ref, k):
            parts = [
                ref[:, k * rows + b * SUB : k * rows + (b + 1) * SUB, :].reshape(wide, block)
                for b in range(rows // SUB)
            ]
            return jnp.concatenate(parts, axis=1)

        for k in range(peers):
            field = jnp.concatenate([side(ref, k) for ref in near], axis=0)
            mixed = (dot(w_ref[...], field) + side(own[m], k).astype(F32)).astype(BF)
            for b in range(rows // SUB):
                piece = mixed[:, b * block : (b + 1) * block]
                outs[k][at, :, b * SUB : (b + 1) * SUB, :] = piece.reshape(comp, SUB, block)


def couple(peers, modes, own, before, after, weights):
    comp, nr, block = own[0].shape
    return call(
        functools.partial(couple_kernel, peers, modes, len(own)),
        "couple",
        (*own, *before, *after, weights),
        [shape(len(modes), comp, nr // peers, block)] * peers,
        len(modes) * comp * nr * block * 2 * 4 * comp * SUB,
    )


def axial_kernel(peers, modes, *refs):
    pieces, m_ref, outs = refs[:peers], refs[peers], refs[peers + 1 :]
    comp, rows, block = pieces[0].shape[1:]
    for at, m in enumerate(modes):
        field = jnp.concatenate([p[at].reshape(comp * rows, block) for p in pieces], axis=1)
        result = dot(field, m_ref[m]).astype(BF)
        for k in range(peers):
            outs[k][at] = result[:, k * block : (k + 1) * block].reshape(comp, rows, block)


def axial(peers, modes, pieces, matrices):
    count, comp, rows, block = pieces[0].shape
    nz = block * peers
    return call(
        functools.partial(axial_kernel, peers, modes),
        "axial",
        (*pieces, matrices),
        [shape(count, comp, rows, block)] * peers,
        count * comp * rows * nz * nz * 2,
    )


def swap(pieces):
    peers = len(pieces)
    result = list(pieces)
    for k in sorted(range(1, peers), key=lambda k: k == 1):
        result[k] = lax.ppermute(pieces[k], "pencil", [(i, i ^ k) for i in range(peers)])
    return result


def local(cotangent, radial_ops, lengths, couple_one, couple_two, axial_damping):
    peers, ring = lax.axis_size("pencil"), lax.axis_size("mode")
    up = [(i, (i + 1) % ring) for i in range(ring)]
    down = [(j, i) for i, j in up]
    count = cotangent.shape[0]
    modes = tuple(range(count))

    def halos(planes):
        before = [lax.ppermute(planes[count - 1 - i], "mode", up) for i in range(2)]
        after = [lax.ppermute(planes[i], "mode", down) for i in range(2)]
        return before, after

    table = jnp.asarray(cosine_table(axial_damping.shape[1]))
    me = lax.axis_index("pencil").astype(jnp.int32).reshape(1)
    before, after = halos([cotangent[i] for i in modes])
    m1, mpp, rpp, rp, weights = prepare(
        peers, me, lengths, table, axial_damping, radial_ops, couple_one, couple_two
    )
    pieces = swap(couple_axial(peers, modes, cotangent, before, after, weights, m1))
    planes = radial(peers, modes, pieces, rpp, True)
    before, after = halos(planes)
    pieces = swap(couple(peers, modes, planes, before, after, weights))
    pieces = swap(axial(peers, modes, pieces, mpp))
    return radial(peers, modes, pieces, rp, False)[0]


def solution(mesh):
    return jax.shard_map(
        local,
        mesh=mesh,
        in_specs=(
            P("mode", None, "pencil", None),
            P("mode", None, None),
            P("mode"),
            P(),
            P(),
            P("mode", None),
        ),
        out_specs=P("mode", None, None, "pencil"),
        check_vma=False,
    )
```

profile of v0, /device:TPU:1, one launch (start us, length us, event | category | flops | bytes accessed | tf_op | source)
XLA Modules:
  0.0 166.3 jit_solution(11543946517989758951)
XLA Ops:
  0.0 0.0 copy-start.5
  0.0 0.0 copy-start.1
  0.0 0.0 copy-start.3
  0.0 0.0 copy-start.2
  0.0 0.0 copy-start.4
  0.0 0.0 copy-start
  0.0 2.9 %slice_bitcast_fusion = (bf16[8,64,512]{2,1,0:T(8,128)(2,1)}, bf16[8,64,512]{2,1,0:T(8,128)(2,1)}, bf16[8,64,512]{2,1,0:T(8,128)(2,1)}, bf16[8,64,512]{2,1,0:T(8,128)(2,1)}) fusion(bf16[4,8,64,512]{3,2,1,0:T(8,128)(2,1)} %refs_0_.1), kind=kLoop, calls=%fused_computation | loop fusion | bytes 4194304 | tf_op jit(solution)/shard_map/squeeze | solution.py:276
  3.0 9.8 %collective-permute-start.3 = (bf16[8,64,512]{2,1,0:T(8,128)(2,1)}, bf16[8,64,512]{2,1,0:T(8,128)(2,1)S(1)}, u32[]{:S(2)}, u32[]{:S(2)}) collective-permute-start(bf16[8,64,512]{2,1,0:T(8,128)(2,1)} %get-tuple-element.47), channel_id=1, source_target_pairs={{4,0},{8,4},{12,8},{16,12},{20,16},{24,20},{28,24},{32,28},{36,32}... | collective-permute-start | bytes 1572872 | tf_op jit(solution)/shard_map/ppermute | solution.py:271
  12.8 0.7 collective-permute-start.2
  13.5 0.7 collective-permute-start.1
  14.2 0.0 collective-permute-start
  14.3 0.0 copy-done.5
  14.3 0.0 copy-done.1
  14.3 0.0 copy-done.3
  14.3 0.0 copy-done.2
  14.3 0.0 copy-done.4
  14.3 0.0 copy-done
  14.3 6.5 %prepare.1 = (bf16[4,512,512]{2,1,0:T(8,128)(2,1)S(1)}, bf16[4,512,512]{2,1,0:T(8,128)(2,1)}, bf16[4,256,256]{2,1,0:T(8,128)(2,1)S(1)}, bf16[4,256,256]{2,1,0:T(8,128)(2,1)S(1)}, bf16[128,512]{1,0:T(8,128)(2,1)S(1)}) custom-call(s32[1]{0:T(128)} %bitcast.4.me_ref, s32[4]{0:T(128)S(1)} %copy-done.4, bf16[512,512]{1,0:T(8,128)(2,1)S(1)} %copy-done.5, ...), custom_call_target="tpu_custom_call" | custom-call | flops 4294967296 | bytes 6431252 | tf_op jit(solution)/shard_map/prepare/pallas_call | solution.py:32
  20.7 0.0 copy-start.6
  20.8 1.4 copy-done.6
  22.1 1.6 collective-permute-done.3.refs_4_
  23.7 11.2 %collective-permute-done.2.refs_3_ = bf16[8,64,512]{2,1,0:T(8,128)(2,1)S(1)} collective-permute-done((bf16[8,64,512]{2,1,0:T(8,128)(2,1)}, bf16[8,64,512]{2,1,0:T(8,128)(2,1)S(1)}, u32[]{:S(2)}, u32[]{:S(2)}) %collective-permute-start.2) | collective-permute-done | bytes 524320 | tf_op jit(solution)/shard_map/ppermute | solution.py:271
  34.9 0.0 collective-permute-done.1.refs_2_
  34.9 6.4 %collective-permute-done.refs_1_ = bf16[8,64,512]{2,1,0:T(8,128)(2,1)S(1)} collective-permute-done((bf16[8,64,512]{2,1,0:T(8,128)(2,1)}, bf16[8,64,512]{2,1,0:T(8,128)(2,1)S(1)}, u32[]{:S(2)}, u32[]{:S(2)}) %collective-permute-start) | collective-permute-done | bytes 524320 | tf_op jit(solution)/shard_map/ppermute | solution.py:270
  41.3 4.6 %couple_axial.1 = (bf16[4,8,64,128]{3,2,1,0:T(8,128)(2,1)S(1)}, bf16[4,8,64,128]{3,2,1,0:T(8,128)(2,1)S(1)}, bf16[4,8,64,128]{3,2,1,0:T(8,128)(2,1)S(1)}, bf16[4,8,64,128]{3,2,1,0:T(8,128)(2,1)S(1)}) custom-call(bf16[4,8,64,512]{3,2,1,0:T(8,128)(2,1)} %refs_0_.1, bf16[8,64,512]{2,1,0:T(8,128)(2,1)S(1)} %collective-permute-done.refs_1_, ...), custom_call_target="tpu_custom_call" | custom-call | flops 2147483648 | bytes 8519680 | tf_op jit(solution)/shard_map/couple_axial/pallas_call | solution.py:32
  45.9 2.2 %collective-permute-start.4 = (bf16[4,8,64,128]{3,2,1,0:T(8,128)(2,1)S(1)}, bf16[4,8,64,128]{3,2,1,0:T(8,128)(2,1)S(1)}, u32[]{:S(2)}, u32[]{:S(2)}) collective-permute-start(bf16[4,8,64,128]{3,2,1,0:T(8,128)(2,1)S(1)} %get-tuple-element.29), channel_id=1, source_target_pairs={{0,1},{1,0},{2,3},{3,2},{4,5},{5,4},{6,7},{7,6},{8,9},{9,8},{10,11... | collective-permute-start | bytes 1572872 | tf_op jit(solution)/shard_map/ppermute | solution.py:258
  48.2 2.5 %collective-permute-start.5 = (bf16[4,8,64,128]{3,2,1,0:T(8,128)(2,1)S(1)}, bf16[4,8,64,128]{3,2,1,0:T(8,128)(2,1)S(1)}, u32[]{:S(2)}, u32[]{:S(2)}) collective-permute-start(bf16[4,8,64,128]{3,2,1,0:T(8,128)(2,1)S(1)} %get-tuple-element.30), channel_id=1, source_target_pairs={{0,2},{1,3},{2,0},{3,1},{4,6},{5,7},{6,4},{7,5},{8,10},{9,11},{10,... | collective-permute-start | bytes 1572872 | tf_op jit(solution)/shard_map/ppermute | solution.py:258
  50.6 0.8 collective-permute-start.6
  51.4 0.0 collective-permute-done.4.refs_1_
  51.4 11.8 %collective-permute-done.5.refs_2_ = bf16[4,8,64,128]{3,2,1,0:T(8,128)(2,1)S(1)} collective-permute-done((bf16[4,8,64,128]{3,2,1,0:T(8,128)(2,1)S(1)}, bf16[4,8,64,128]{3,2,1,0:T(8,128)(2,1)S(1)}, u32[]{:S(2)}, u32[]{:S(2)}) %collective-permute-start.5) | collective-permute-done | bytes 524320 | tf_op jit(solution)/shard_map/ppermute | solution.py:258
  63.1 11.4 %collective-permute-done.6.refs_3_ = bf16[4,8,64,128]{3,2,1,0:T(8,128)(2,1)S(1)} collective-permute-done((bf16[4,8,64,128]{3,2,1,0:T(8,128)(2,1)S(1)}, bf16[4,8,64,128]{3,2,1,0:T(8,128)(2,1)S(1)}, u32[]{:S(2)}, u32[]{:S(2)}) %collective-permute-start.6) | collective-permute-done | bytes 524320 | tf_op jit(solution)/shard_map/ppermute | solution.py:258
  74.6 0.7 radial.2
  75.3 0.3 collective-permute-start.9
  75.6 0.1 collective-permute-start.10
  75.6 1.5 collective-permute-start.8
  77.1 1.4 collective-permute-start.7
  78.5 10.4 %collective-permute-done.9.refs_6_ = bf16[8,256,128]{2,1,0:T(8,128)(2,1)S(1)} collective-permute-done((bf16[8,256,128]{2,1,0:T(8,128)(2,1)S(1)}, bf16[8,256,128]{2,1,0:T(8,128)(2,1)S(1)}, u32[]{:S(2)}, u32[]{:S(2)}) %collective-permute-start.9) | collective-permute-done | bytes 524320 | tf_op jit(solution)/shard_map/ppermute | solution.py:271
  88.8 11.2 %collective-permute-done.10.refs_7_ = bf16[8,256,128]{2,1,0:T(8,128)(2,1)S(1)} collective-permute-done((bf16[8,256,128]{2,1,0:T(8,128)(2,1)S(1)}, bf16[8,256,128]{2,1,0:T(8,128)(2,1)S(1)}, u32[]{:S(2)}, u32[]{:S(2)}) %collective-permute-start.10) | collective-permute-done | bytes 524320 | tf_op jit(solution)/shard_map/ppermute | solution.py:271
  100.1 0.0 copy-start.7
  100.1 0.0 collective-permute-done.8.refs_5_
  100.1 4.4 %collective-permute-done.7.refs_4_ = bf16[8,256,128]{2,1,0:T(8,128)(2,1)S(1)} collective-permute-done((bf16[8,256,128]{2,1,0:T(8,128)(2,1)S(1)}, bf16[8,256,128]{2,1,0:T(8,128)(2,1)S(1)}, u32[]{:S(2)}, u32[]{:S(2)}) %collective-permute-start.7) | collective-permute-done | bytes 524320 | tf_op jit(solution)/shard_map/ppermute | solution.py:270
  104.5 0.0 copy-done.7
  104.5 2.7 %couple.1 = (bf16[4,8,64,128]{3,2,1,0:T(8,128)(2,1)S(1)}, bf16[4,8,64,128]{3,2,1,0:T(8,128)(2,1)S(1)}, bf16[4,8,64,128]{3,2,1,0:T(8,128)(2,1)S(1)}, bf16[4,8,64,128]{3,2,1,0:T(8,128)(2,1)S(1)}) custom-call(bf16[8,256,128]{2,1,0:T(8,128)(2,1)S(1)} %get-tuple-element.33.refs_0_, bf16[8,256,128]{2,1,0:T(8,128)(2,1)S(1)} %get-tuple-element.34.refs_1_, ...), custom_call_target="tpu_custom_call" | custom-call | flops 1073741824 | bytes 6422528 | tf_op jit(solution)/shard_map/couple/pallas_call | solution.py:32
  107.2 1.1 collective-permute-start.11
  108.3 2.5 %collective-permute-start.12 = (bf16[4,8,64,128]{3,2,1,0:T(8,128)(2,1)S(1)}, bf16[4,8,64,128]{3,2,1,0:T(8,128)(2,1)S(1)}, u32[]{:S(2)}, u32[]{:S(2)}) collective-permute-start(bf16[4,8,64,128]{3,2,1,0:T(8,128)(2,1)S(1)} %get-tuple-element.39), channel_id=1, source_target_pairs={{0,2},{1,3},{2,0},{3,1},{4,6},{5,7},{6,4},{7,5},{8,10},{9,11},{10,... | collective-permute-start | bytes 1572872 | tf_op jit(solution)/shard_map/ppermute | solution.py:258
  110.8 0.8 collective-permute-start.13
  111.5 0.0 collective-permute-done.11.refs_1_
  111.5 11.8 %collective-permute-done.12.refs_2_ = bf16[4,8,64,128]{3,2,1,0:T(8,128)(2,1)S(1)} collective-permute-done((bf16[4,8,64,128]{3,2,1,0:T(8,128)(2,1)S(1)}, bf16[4,8,64,128]{3,2,1,0:T(8,128)(2,1)S(1)}, u32[]{:S(2)}, u32[]{:S(2)}) %collective-permute-start.12) | collective-permute-done | bytes 524320 | tf_op jit(solution)/shard_map/ppermute | solution.py:258
  123.3 11.4 %collective-permute-done.13.refs_3_ = bf16[4,8,64,128]{3,2,1,0:T(8,128)(2,1)S(1)} collective-permute-done((bf16[4,8,64,128]{3,2,1,0:T(8,128)(2,1)S(1)}, bf16[4,8,64,128]{3,2,1,0:T(8,128)(2,1)S(1)}, u32[]{:S(2)}, u32[]{:S(2)}) %collective-permute-start.13) | collective-permute-done | bytes 524320 | tf_op jit(solution)/shard_map/ppermute | solution.py:258
  134.7 2.8 %axial.1 = (bf16[4,8,64,128]{3,2,1,0:T(8,128)(2,1)S(1)}, bf16[4,8,64,128]{3,2,1,0:T(8,128)(2,1)S(1)}, bf16[4,8,64,128]{3,2,1,0:T(8,128)(2,1)S(1)}, bf16[4,8,64,128]{3,2,1,0:T(8,128)(2,1)S(1)}) custom-call(bf16[4,8,64,128]{3,2,1,0:T(8,128)(2,1)S(1)} %get-tuple-element.37.refs_0_, bf16[4,8,64,128]{3,2,1,0:T(8,128)(2,1)S(1)} %collective-permute-done.11.refs_1_, ...), custom_call_target="tpu_custom_call" | custom-call | flops 1073741824 | bytes 6291456 | tf_op jit(solution)/shard_map/axial/pallas_call | solution.py:32
  137.6 0.3 collective-permute-start.14
  137.9 2.4 %collective-permute-start.15 = (bf16[4,8,64,128]{3,2,1,0:T(8,128)(2,1)S(1)}, bf16[4,8,64,128]{3,2,1,0:T(8,128)(2,1)S(1)}, u32[]{:S(2)}, u32[]{:S(2)}) collective-permute-start(bf16[4,8,64,128]{3,2,1,0:T(8,128)(2,1)S(1)} %get-tuple-element.44), channel_id=1, source_target_pairs={{0,2},{1,3},{2,0},{3,1},{4,6},{5,7},{6,4},{7,5},{8,10},{9,11},{10,... | collective-permute-start | bytes 1572872 | tf_op jit(solution)/shard_map/ppermute | solution.py:258
  140.3 1.0 collective-permute-start.16
  141.3 0.0 collective-permute-done.14.refs_1_
  141.3 11.3 %collective-permute-done.15.refs_2_ = bf16[4,8,64,128]{3,2,1,0:T(8,128)(2,1)S(1)} collective-permute-done((bf16[4,8,64,128]{3,2,1,0:T(8,128)(2,1)S(1)}, bf16[4,8,64,128]{3,2,1,0:T(8,128)(2,1)S(1)}, u32[]{:S(2)}, u32[]{:S(2)}) %collective-permute-start.15) | collective-permute-done | bytes 524320 | tf_op jit(solution)/shard_map/ppermute | solution.py:258
  152.6 11.7 %collective-permute-done.16.refs_3_ = bf16[4,8,64,128]{3,2,1,0:T(8,128)(2,1)S(1)} collective-permute-done((bf16[4,8,64,128]{3,2,1,0:T(8,128)(2,1)S(1)}, bf16[4,8,64,128]{3,2,1,0:T(8,128)(2,1)S(1)}, u32[]{:S(2)}, u32[]{:S(2)}) %collective-permute-start.16) | collective-permute-done | bytes 524320 | tf_op jit(solution)/shard_map/ppermute | solution.py:258
  164.2 2.0 %radial.3 = bf16[4,8,256,128]{3,2,1,0:T(8,128)(2,1)} custom-call(bf16[4,8,64,128]{3,2,1,0:T(8,128)(2,1)S(1)} %get-tuple-element.42.refs_0_, bf16[4,8,64,128]{3,2,1,0:T(8,128)(2,1)S(1)} %collective-permute-done.14.refs_1_, bf16[4,8,64,128]{3,2,1,0:T(8,128)(2,1)S(1)} %collective-permute-done.15.refs_2_, ...), custom_call_target="tpu_custom_call" | custom-call | flops 536870912 | bytes 4718592 | tf_op jit(solution)/shard_map/radial/pallas_call | solution.py:32
Async XLA Ops:
  0.0 14.3 %copy-start.5 = (bf16[512,512]{1,0:T(8,128)(2,1)S(1)}, bf16[512,512]{1,0:T(8,128)(2,1)}, u32[]{:S(2)}) copy-start(bf16[512,512]{1,0:T(8,128)(2,1)} %constant.6.clone.q_ref) | copy-start | bytes 1572868
  0.0 14.3 %copy-start.1 = (f32[4,512]{1,0:T(4,128)S(1)}, f32[4,512]{1,0:T(4,128)}, u32[]{:S(2)}) copy-start(f32[4,512]{1,0:T(4,128)} %damp_ref.1) | copy-start | bytes 24580
  0.0 14.3 %copy-start.3 = (f32[8,8]{1,0:T(8,128)S(1)}, f32[8,8]{1,0:T(8,128)}, u32[]{:S(2)}) copy-start(f32[8,8]{1,0:T(8,128)} %two_ref.1) | copy-start | bytes 772
  0.0 14.3 %copy-start.2 = (f32[8,8]{1,0:T(8,128)S(1)}, f32[8,8]{1,0:T(8,128)}, u32[]{:S(2)}) copy-start(f32[8,8]{1,0:T(8,128)} %one_ref.1) | copy-start | bytes 772
  0.0 14.3 %copy-start.4 = (s32[4]{0:T(128)S(1)}, s32[4]{0:T(128)}, u32[]{:S(2)}) copy-start(s32[4]{0:T(128)} %len_ref.1) | copy-start | bytes 52
  0.0 14.3 %copy-start = (bf16[4,256,256]{2,1,0:T(8,128)(2,1)S(1)}, bf16[4,256,256]{2,1,0:T(8,128)(2,1)}, u32[]{:S(2)}) copy-start(bf16[4,256,256]{2,1,0:T(8,128)(2,1)} %rad_ref.1) | copy-start | bytes 1572868
  3.0 20.7 %collective-permute-start.3 = (bf16[8,64,512]{2,1,0:T(8,128)(2,1)}, bf16[8,64,512]{2,1,0:T(8,128)(2,1)S(1)}, u32[]{:S(2)}, u32[]{:S(2)}) collective-permute-start(bf16[8,64,512]{2,1,0:T(8,128)(2,1)} %get-tuple-element.47), channel_id=1, source_target_pairs={{4,0},{8,4},{12,8},{16,12},{20,16},{24,20},{28,24},{32,28},{36,32}... | collective-permute-start | bytes 1572872 | tf_op jit(solution)/shard_map/ppermute | solution.py:271
  12.8 22.1 %collective-permute-start.2 = (bf16[8,64,512]{2,1,0:T(8,128)(2,1)}, bf16[8,64,512]{2,1,0:T(8,128)(2,1)S(1)}, u32[]{:S(2)}, u32[]{:S(2)}) collective-permute-start(bf16[8,64,512]{2,1,0:T(8,128)(2,1)} %get-tuple-element.48), channel_id=1, source_target_pairs={{4,0},{8,4},{12,8},{16,12},{20,16},{24,20},{28,24},{32,28},{36,32}... | collective-permute-start | bytes 1572872 | tf_op jit(solution)/shard_map/ppermute | solution.py:271
  13.5 21.4 %collective-permute-start.1 = (bf16[8,64,512]{2,1,0:T(8,128)(2,1)}, bf16[8,64,512]{2,1,0:T(8,128)(2,1)S(1)}, u32[]{:S(2)}, u32[]{:S(2)}) collective-permute-start(bf16[8,64,512]{2,1,0:T(8,128)(2,1)} %get-tuple-element.49), channel_id=1, source_target_pairs={{0,4},{4,8},{8,12},{12,16},{16,20},{20,24},{24,28},{28,32},{32,36}... | collective-permute-start | bytes 1572872 | tf_op jit(solution)/shard_map/ppermute | solution.py:270
  14.2 27.1 %collective-permute-start = (bf16[8,64,512]{2,1,0:T(8,128)(2,1)}, bf16[8,64,512]{2,1,0:T(8,128)(2,1)S(1)}, u32[]{:S(2)}, u32[]{:S(2)}) collective-permute-start(bf16[8,64,512]{2,1,0:T(8,128)(2,1)} %get-tuple-element.50), channel_id=1, source_target_pairs={{0,4},{4,8},{8,12},{12,16},{16,20},{20,24},{24,28},{28,32},{32,36}... | collective-permute-start | bytes 1572872 | tf_op jit(solution)/shard_map/ppermute | solution.py:270
  20.7 1.4 copy-start.6
  45.9 5.5 %collective-permute-start.4 = (bf16[4,8,64,128]{3,2,1,0:T(8,128)(2,1)S(1)}, bf16[4,8,64,128]{3,2,1,0:T(8,128)(2,1)S(1)}, u32[]{:S(2)}, u32[]{:S(2)}) collective-permute-start(bf16[4,8,64,128]{3,2,1,0:T(8,128)(2,1)S(1)} %get-tuple-element.29), channel_id=1, source_target_pairs={{0,1},{1,0},{2,3},{3,2},{4,5},{5,4},{6,7},{7,6},{8,9},{9,8},{10,11... | collective-permute-start | bytes 1572872 | tf_op jit(solution)/shard_map/ppermute | solution.py:258
  48.2 15.0 %collective-permute-start.5 = (bf16[4,8,64,128]{3,2,1,0:T(8,128)(2,1)S(1)}, bf16[4,8,64,128]{3,2,1,0:T(8,128)(2,1)S(1)}, u32[]{:S(2)}, u32[]{:S(2)}) collective-permute-start(bf16[4,8,64,128]{3,2,1,0:T(8,128)(2,1)S(1)} %get-tuple-element.30), channel_id=1, source_target_pairs={{0,2},{1,3},{2,0},{3,1},{4,6},{5,7},{6,4},{7,5},{8,10},{9,11},{10,... | collective-permute-start | bytes 1572872 | tf_op jit(solution)/shard_map/ppermute | solution.py:258
  50.6 23.9 %collective-permute-start.6 = (bf16[4,8,64,128]{3,2,1,0:T(8,128)(2,1)S(1)}, bf16[4,8,64,128]{3,2,1,0:T(8,128)(2,1)S(1)}, u32[]{:S(2)}, u32[]{:S(2)}) collective-permute-start(bf16[4,8,64,128]{3,2,1,0:T(8,128)(2,1)S(1)} %get-tuple-element.31), channel_id=1, source_target_pairs={{0,3},{1,2},{2,1},{3,0},{4,7},{5,6},{6,5},{7,4},{8,11},{9,10},{10,... | collective-permute-start | bytes 1572872 | tf_op jit(solution)/shard_map/ppermute | solution.py:258
  75.3 13.5 %collective-permute-start.9 = (bf16[8,256,128]{2,1,0:T(8,128)(2,1)S(1)}, bf16[8,256,128]{2,1,0:T(8,128)(2,1)S(1)}, u32[]{:S(2)}, u32[]{:S(2)}) collective-permute-start(bf16[8,256,128]{2,1,0:T(8,128)(2,1)S(1)} %get-tuple-element.33.refs_0_), channel_id=1, source_target_pairs={{4,0},{8,4},{12,8},{16,12},{20,16},{24,20},{28,24},{32,28},{36,32}... | collective-permute-start | bytes 1572872 | tf_op jit(solution)/shard_map/ppermute | solution.py:271
  75.6 24.5 %collective-permute-start.10 = (bf16[8,256,128]{2,1,0:T(8,128)(2,1)S(1)}, bf16[8,256,128]{2,1,0:T(8,128)(2,1)S(1)}, u32[]{:S(2)}, u32[]{:S(2)}) collective-permute-start(bf16[8,256,128]{2,1,0:T(8,128)(2,1)S(1)} %get-tuple-element.34.refs_1_), channel_id=1, source_target_pairs={{4,0},{8,4},{12,8},{16,12},{20,16},{24,20},{28,24},{32,28},{36,32}... | collective-permute-start | bytes 1572872 | tf_op jit(solution)/shard_map/ppermute | solution.py:271
  75.6 24.4 %collective-permute-start.8 = (bf16[8,256,128]{2,1,0:T(8,128)(2,1)S(1)}, bf16[8,256,128]{2,1,0:T(8,128)(2,1)S(1)}, u32[]{:S(2)}, u32[]{:S(2)}) collective-permute-start(bf16[8,256,128]{2,1,0:T(8,128)(2,1)S(1)} %get-tuple-element.35.refs_2_), channel_id=1, source_target_pairs={{0,4},{4,8},{8,12},{12,16},{16,20},{20,24},{24,28},{28,32},{32,36}... | collective-permute-start | bytes 1572872 | tf_op jit(solution)/shard_map/ppermute | solution.py:270
  77.1 27.4 %collective-permute-start.7 = (bf16[8,256,128]{2,1,0:T(8,128)(2,1)S(1)}, bf16[8,256,128]{2,1,0:T(8,128)(2,1)S(1)}, u32[]{:S(2)}, u32[]{:S(2)}) collective-permute-start(bf16[8,256,128]{2,1,0:T(8,128)(2,1)S(1)} %get-tuple-element.36.refs_3_), channel_id=1, source_target_pairs={{0,4},{4,8},{8,12},{12,16},{16,20},{20,24},{24,28},{28,32},{32,36}... | collective-permute-start | bytes 1572872 | tf_op jit(solution)/shard_map/ppermute | solution.py:270
  100.1 4.4 %copy-start.7 = (bf16[8,256,128]{2,1,0:T(8,128)(2,1)}, bf16[8,256,128]{2,1,0:T(8,128)(2,1)S(1)}, u32[]{:S(2)}) copy-start(bf16[8,256,128]{2,1,0:T(8,128)(2,1)S(1)} %collective-permute-done.10.refs_7_) | copy-start | bytes 1572868
  107.2 4.4 %collective-permute-start.11 = (bf16[4,8,64,128]{3,2,1,0:T(8,128)(2,1)S(1)}, bf16[4,8,64,128]{3,2,1,0:T(8,128)(2,1)S(1)}, u32[]{:S(2)}, u32[]{:S(2)}) collective-permute-start(bf16[4,8,64,128]{3,2,1,0:T(8,128)(2,1)S(1)} %get-tuple-element.38), channel_id=1, source_target_pairs={{0,1},{1,0},{2,3},{3,2},{4,5},{5,4},{6,7},{7,6},{8,9},{9,8},{10,11... | collective-permute-start | bytes 1572872 | tf_op jit(solution)/shard_map/ppermute | solution.py:258
  108.3 15.0 %collective-permute-start.12 = (bf16[4,8,64,128]{3,2,1,0:T(8,128)(2,1)S(1)}, bf16[4,8,64,128]{3,2,1,0:T(8,128)(2,1)S(1)}, u32[]{:S(2)}, u32[]{:S(2)}) collective-permute-start(bf16[4,8,64,128]{3,2,1,0:T(8,128)(2,1)S(1)} %get-tuple-element.39), channel_id=1, source_target_pairs={{0,2},{1,3},{2,0},{3,1},{4,6},{5,7},{6,4},{7,5},{8,10},{9,11},{10,... | collective-permute-start | bytes 1572872 | tf_op jit(solution)/shard_map/ppermute | solution.py:258
  110.8 23.9 %collective-permute-start.13 = (bf16[4,8,64,128]{3,2,1,0:T(8,128)(2,1)S(1)}, bf16[4,8,64,128]{3,2,1,0:T(8,128)(2,1)S(1)}, u32[]{:S(2)}, u32[]{:S(2)}) collective-permute-start(bf16[4,8,64,128]{3,2,1,0:T(8,128)(2,1)S(1)} %get-tuple-element.40), channel_id=1, source_target_pairs={{0,3},{1,2},{2,1},{3,0},{4,7},{5,6},{6,5},{7,4},{8,11},{9,10},{10,... | collective-permute-start | bytes 1572872 | tf_op jit(solution)/shard_map/ppermute | solution.py:258
  137.6 3.7 %collective-permute-start.14 = (bf16[4,8,64,128]{3,2,1,0:T(8,128)(2,1)S(1)}, bf16[4,8,64,128]{3,2,1,0:T(8,128)(2,1)S(1)}, u32[]{:S(2)}, u32[]{:S(2)}) collective-permute-start(bf16[4,8,64,128]{3,2,1,0:T(8,128)(2,1)S(1)} %get-tuple-element.43), channel_id=1, source_target_pairs={{0,1},{1,0},{2,3},{3,2},{4,5},{5,4},{6,7},{7,6},{8,9},{9,8},{10,11... | collective-permute-start | bytes 1572872 | tf_op jit(solution)/shard_map/ppermute | solution.py:258
  137.9 14.7 %collective-permute-start.15 = (bf16[4,8,64,128]{3,2,1,0:T(8,128)(2,1)S(1)}, bf16[4,8,64,128]{3,2,1,0:T(8,128)(2,1)S(1)}, u32[]{:S(2)}, u32[]{:S(2)}) collective-permute-start(bf16[4,8,64,128]{3,2,1,0:T(8,128)(2,1)S(1)} %get-tuple-element.44), channel_id=1, source_target_pairs={{0,2},{1,3},{2,0},{3,1},{4,6},{5,7},{6,4},{7,5},{8,10},{9,11},{10,... | collective-permute-start | bytes 1572872 | tf_op jit(solution)/shard_map/ppermute | solution.py:258
  140.3 23.9 %collective-permute-start.16 = (bf16[4,8,64,128]{3,2,1,0:T(8,128)(2,1)S(1)}, bf16[4,8,64,128]{3,2,1,0:T(8,128)(2,1)S(1)}, u32[]{:S(2)}, u32[]{:S(2)}) collective-permute-start(bf16[4,8,64,128]{3,2,1,0:T(8,128)(2,1)S(1)} %get-tuple-element.45), channel_id=1, source_target_pairs={{0,3},{1,2},{2,1},{3,0},{4,7},{5,6},{6,5},{7,4},{8,11},{9,10},{10,... | collective-permute-start | bytes 1572872 | tf_op jit(solution)/shard_map/ppermute | solution.py:258
where the time goes:
time: 166 us
  waiting for transfers between devices  115 us (69%)
  starting transfers between devices  28 us (17%)
  Pallas kernels  19.3 us (12%)
  local copies, waits for them, and re-layouts  4.31 us (3%)
    ppermute x9, waiting for transfers between devices, swap(): lax.ppermute(pieces[k], 'pencil', [(i, i ^ k) for i in range(peers)])  69.3 us
    ppermute x4, waiting for transfers between devices, halos(): after = [lax.ppermute(planes[i], 'mode', down) for i in range(2)]  34.4 us
    pallas_call x6, Pallas kernels, call(): pl.pallas_call(kernel, out_shape=outs, in_specs=[pl.BlockSpec(memory_spac...  19.3 us
    ppermute x9, starting transfers between devices, swap(): lax.ppermute(pieces[k], 'pencil', [(i, i ^ k) for i in range(peers)])  13.6 us
    ppermute x4, starting transfers between devices, halos(): after = [lax.ppermute(planes[i], 'mode', down) for i in range(2)]  10.9 us
    ppermute x4, waiting for transfers between devices, halos(): before = [lax.ppermute(planes[count - 1 - i], 'mode', up) for i in range(2)]  10.9 us
    ppermute x4, starting transfers between devices, halos(): before = [lax.ppermute(planes[count - 1 - i], 'mode', up) for i in range(2)]  3.6 us
  transfers between devices with their start and end apart: 17, of which 12 were waited for; matrix products, arithmetic and copies ran while one was open for 0% of the time, Pallas kernels for 4%

commit v1 on v0

--- a/solution.py
+++ b/solution.py
@@ -129,11 +129,11 @@
     return [at(m - 1), at(m + 1), at(m - 2), at(m + 2)]
 
 
-def couple_axial_kernel(peers, modes, count, *refs):
-    x_ref = refs[0]
-    before, after = refs[1:3], refs[3:5]
-    w_ref, m_ref = refs[5:7]
-    outs, a_ref = refs[7 : 7 + peers], refs[7 + peers]
+def couple_axial_kernel(peers, modes, count, depth, *refs):
+    x_ref, refs = refs[0], refs[1:]
+    before, after, refs = refs[:depth], refs[depth : 2 * depth], refs[2 * depth :]
+    w_ref, m_ref = refs[:2]
+    outs, a_ref = refs[2 : 2 + peers], refs[2 + peers]
     own = [x_ref.at[i] for i in range(count)]
     comp, rows, nz = own[0].shape
     wide = comp * SUB
@@ -155,7 +155,7 @@
 def couple_axial(peers, modes, x, before, after, weights, matrices):
     count, comp, rows, nz = x.shape
     return call(
-        functools.partial(couple_axial_kernel, peers, modes, count),
+        functools.partial(couple_axial_kernel, peers, modes, count, len(before)),
         "couple_axial",
         (x, *before, *after, weights, matrices),
         [shape(len(modes), comp, rows, nz // peers)] * peers,
@@ -164,33 +164,63 @@
     )
 
 
+def radial_one(pieces, matrix, out):
+    comp, _, block = pieces[0].shape
+    for c in range(0, comp, 2):
+        field = jnp.concatenate([jnp.concatenate([p[c], p[c + 1]], axis=1) for p in pieces], axis=0)
+        result = dot(matrix, field).astype(BF)
+        out[c] = result[:, :block]
+        out[c + 1] = result[:, block:]
+
+
 def radial_kernel(peers, modes, *refs):
     pieces, r_ref, outs = refs[:peers], refs[peers], refs[peers + 1 :]
-    comp = pieces[0].shape[1]
-    block = pieces[0].shape[3]
     for at, m in enumerate(modes):
-        matrix = r_ref[m]
-        for c in range(0, comp, 2):
-            field = jnp.concatenate(
-                [jnp.concatenate([p[at, c], p[at, c + 1]], axis=1) for p in pieces], axis=0
-            )
-            result = dot(matrix, field).astype(BF)
-            out = outs[at] if len(outs) > 1 else outs[0].at[at]
-            out[c] = result[:, :block]
-            out[c + 1] = result[:, block:]
-
-
-def radial(peers, modes, pieces, matrices, separate):
+        radial_one([p.at[at] for p in pieces], r_ref[m], outs[at])
+
+
+def radial(peers, modes, pieces, matrices):
     count, comp, rows, block = pieces[0].shape
     nr = rows * peers
-    outs = [shape(comp, nr, block)] * count if separate else [shape(count, comp, nr, block)]
     return call(
         functools.partial(radial_kernel, peers, modes),
         "radial",
         (*pieces, matrices),
-        outs,
+        [shape(comp, nr, block)] * count,
         count * comp * nr * nr * block * 2,
     )
+
+
+def radial_last_kernel(peers, *refs):
+    radial_one([p.at[0] for p in refs[:peers]], refs[peers][0], refs[-1].at[0])
+
+
+def radial_last(peers, first, total, pieces, matrices, partial_result):
+    count, comp, rows, block = pieces[0].shape
+    nr = rows * peers
+    specs = [pl.BlockSpec((1, comp, rows, block), lambda i: (i, 0, 0, 0))] * peers
+    specs.append(pl.BlockSpec((1, nr, nr), lambda i: (first + i, 0, 0)))
+    args = [*pieces, matrices]
+    aliases = {}
+    if partial_result is not None:
+        specs.append(pl.BlockSpec(memory_space=pl.ANY))
+        aliases = {len(args): 0}
+        args.append(partial_result)
+    return pl.pallas_call(
+        functools.partial(radial_last_kernel, peers),
+        grid=(count,),
+        out_shape=shape(total, comp, nr, block),
+        in_specs=specs,
+        out_specs=pl.BlockSpec((1, comp, nr, block), lambda i: (first + i, 0, 0, 0)),
+        input_output_aliases=aliases,
+        compiler_params=pltpu.CompilerParams(vmem_limit_bytes=VMEM_LIMIT),
+        cost_estimate=pl.CostEstimate(
+            flops=count * comp * nr * nr * block * 2,
+            bytes_accessed=count * comp * nr * block * 4,
+            transcendentals=0,
+        ),
+        name="radial_last",
+    )(*args)
 
 
 def couple_kernel(peers, modes, count, *refs):
@@ -266,23 +296,37 @@
     count = cotangent.shape[0]
     modes = tuple(range(count))
 
-    def halos(planes):
-        before = [lax.ppermute(planes[count - 1 - i], "mode", up) for i in range(2)]
-        after = [lax.ppermute(planes[i], "mode", down) for i in range(2)]
-        return before, after
+    def send(plane, way):
+        return lax.ppermute(plane, "mode", way)
 
     table = jnp.asarray(cosine_table(axial_damping.shape[1]))
     me = lax.axis_index("pencil").astype(jnp.int32).reshape(1)
-    before, after = halos([cotangent[i] for i in modes])
+    last = count - 1
+    inner, outer = modes[1:last], (0, last)
+
+    before = [send(cotangent[last], up)]
+    after = [send(cotangent[0], down)]
+    before.append(send(cotangent[last - 1], up))
+    after.append(send(cotangent[1], down))
     m1, mpp, rpp, rp, weights = prepare(
         peers, me, lengths, table, axial_damping, radial_ops, couple_one, couple_two
     )
-    pieces = swap(couple_axial(peers, modes, cotangent, before, after, weights, m1))
-    planes = radial(peers, modes, pieces, rpp, True)
-    before, after = halos(planes)
-    pieces = swap(couple(peers, modes, planes, before, after, weights))
-    pieces = swap(axial(peers, modes, pieces, mpp))
-    return radial(peers, modes, pieces, rp, False)[0]
+    inner_pieces = swap(couple_axial(peers, inner, cotangent, before[:1], after[:1], weights, m1))
+    outer_pieces = swap(couple_axial(peers, outer, cotangent, before, after, weights, m1))
+    planes = dict(zip(inner, radial(peers, inner, inner_pieces, rpp)))
+    far_before, far_after = send(planes[last - 1], up), send(planes[1], down)
+    planes.update(zip(outer, radial(peers, outer, outer_pieces, rpp)))
+    before = [send(planes[last], up), far_before]
+    after = [send(planes[0], down), far_after]
+    planes = [planes[m] for m in modes]
+
+    halves = (modes[: count // 2], modes[count // 2 :])
+    pieces = [swap(couple(peers, half, planes, before, after, weights)) for half in halves]
+    pieces = [swap(axial(peers, half, p, mpp)) for half, p in zip(halves, pieces)]
+    result = None
+    for half, p in zip(halves, pieces):
+        result = radial_last(peers, half[0], count, p, rp, result)
+    return result
 
 
 def solution(mesh):

time: 166 us -> 145 us (0.87)
  waiting for transfers between devices: 115 us -> 75 us
  starting transfers between devices: 28 us -> 46.5 us
    ppermute x8, waiting for transfers between devices: 45.2 us -> 21.7 us  [send(): return lax.ppermute(plane, 'mode', way)]
    ppermute x9 -> x18, waiting for transfers between devices: 69.3 us -> 53.3 us  [swap(): lax.ppermute(pieces[k], 'pencil', [(i, i ^ k) for i in range(peers)])]
    ppermute x9 -> x18, starting transfers between devices: 13.6 us -> 27.9 us  [swap(): lax.ppermute(pieces[k], 'pencil', [(i, i ^ k) for i in range(peers)])]
    ppermute x8, starting transfers between devices: 14.5 us -> 18.6 us  [send(): return lax.ppermute(plane, 'mode', way)]
    pallas_call x6 -> x9, Pallas kernels: 19.3 us -> 16.2 us  [call(): pl.pallas_call(kernel, out_shape=outs, in_specs=[pl.BlockSpec(memory_spac...]
    pallas_call x0 -> x2, Pallas kernels: none -> 2.83 us  [radial_last(): pl.pallas_call(functools.partial(radial_last_kernel, peers), grid=(count,...]
  transfers between devices with their start and end apart: 17 -> 26, of which waited for: 12 -> 15; matrix products, arithmetic and copies ran while one was open for 0% -> 0% of each run, Pallas kernels for 4% -> 12%
where the time goes in v1:
time: 145 us
  waiting for transfers between devices  75 us (52%)
  starting transfers between devices  46.5 us (32%)
  Pallas kernels  19 us (13%)
  local copies, waits for them, and re-layouts  4.34 us (3%)
    ppermute x18, waiting for transfers between devices, swap(): lax.ppermute(pieces[k], 'pencil', [(i, i ^ k) for i in range(peers)])  53.3 us
    ppermute x18, starting transfers between devices, swap(): lax.ppermute(pieces[k], 'pencil', [(i, i ^ k) for i in range(peers)])  27.9 us
    ppermute x8, waiting for transfers between devices, send(): return lax.ppermute(plane, 'mode', way)  21.7 us
    ppermute x8, starting transfers between devices, send(): return lax.ppermute(plane, 'mode', way)  18.6 us
    pallas_call x9, Pallas kernels, call(): pl.pallas_call(kernel, out_shape=outs, in_specs=[pl.BlockSpec(memory_spac...  16.2 us
    squeeze x1, local copies, waits for them, and re-layouts, local(): after.append(send(cotangent[1], down))  2.96 us
  transfers between devices with their start and end apart: 26, of which 15 were waited for; matrix products, arithmetic and copies ran while one was open for 0% of the time, Pallas kernels for 12%

profile of v1, /device:TPU:1, one launch (start us, length us, event | category | flops | bytes accessed | tf_op | source)
XLA Modules:
  0.0 145.0 jit_solution(2816061104016822386)
XLA Ops:
  0.0 3.0 %slice_bitcast_fusion = (bf16[8,64,512]{2,1,0:T(8,128)(2,1)}, bf16[8,64,512]{2,1,0:T(8,128)(2,1)}, bf16[8,64,512]{2,1,0:T(8,128)(2,1)}, bf16[8,64,512]{2,1,0:T(8,128)(2,1)}) fusion(bf16[4,8,64,512]{3,2,1,0:T(8,128)(2,1)} %refs_0_.3), kind=kLoop, calls=%fused_computation | loop fusion | bytes 4194304 | tf_op jit(solution)/shard_map/squeeze | solution.py:310
  3.0 9.8 %collective-permute-start.2 = (bf16[8,64,512]{2,1,0:T(8,128)(2,1)}, bf16[8,64,512]{2,1,0:T(8,128)(2,1)S(1)}, u32[]{:S(2)}, u32[]{:S(2)}) collective-permute-start(bf16[8,64,512]{2,1,0:T(8,128)(2,1)} %get-tuple-element.72), channel_id=1, source_target_pairs={{4,0},{8,4},{12,8},{16,12},{20,16},{24,20},{28,24},{32,28},{36,32}... | collective-permute-start | bytes 1572872 | tf_op jit(solution)/shard_map/ppermute | solution.py:300
  12.8 0.0 collective-permute-start
  12.8 5.7 %collective-permute-start.3 = (bf16[8,64,512]{2,1,0:T(8,128)(2,1)}, bf16[8,64,512]{2,1,0:T(8,128)(2,1)S(1)}, u32[]{:S(2)}, u32[]{:S(2)}) collective-permute-start(bf16[8,64,512]{2,1,0:T(8,128)(2,1)} %get-tuple-element.71), channel_id=1, source_target_pairs={{4,0},{8,4},{12,8},{16,12},{20,16},{24,20},{28,24},{32,28},{36,32}... | collective-permute-start | bytes 1572872 | tf_op jit(solution)/shard_map/ppermute | solution.py:300
  18.5 0.0 collective-permute-start.1
  18.5 0.0 copy-start
  18.5 6.5 %prepare.1 = (bf16[4,512,512]{2,1,0:T(8,128)(2,1)S(1)}, bf16[4,512,512]{2,1,0:T(8,128)(2,1)}, bf16[4,256,256]{2,1,0:T(8,128)(2,1)S(1)}, bf16[4,256,256]{2,1,0:T(8,128)(2,1)S(1)}, bf16[128,512]{1,0:T(8,128)(2,1)S(1)}) custom-call(s32[1]{0:T(128)} %bitcast.4.me_ref, s32[4]{0:T(128)S(1)} %copy-done.7, bf16[512,512]{1,0:T(8,128)(2,1)S(1)} %copy-done.8, ...), custom_call_target="tpu_custom_call" | custom-call | flops 4294967296 | bytes 6431252 | tf_op jit(solution)/shard_map/prepare/pallas_call | solution.py:32
  25.0 1.4 copy-done.2
  26.3 0.0 collective-permute-done.2.refs_3_.refs_2_
  26.4 3.3 %collective-permute-done.refs_1_ = bf16[8,64,512]{2,1,0:T(8,128)(2,1)S(1)} collective-permute-done((bf16[8,64,512]{2,1,0:T(8,128)(2,1)}, bf16[8,64,512]{2,1,0:T(8,128)(2,1)S(1)}, u32[]{:S(2)}, u32[]{:S(2)}) %collective-permute-start) | collective-permute-done | bytes 524320 | tf_op jit(solution)/shard_map/ppermute | solution.py:300
  29.7 2.8 %couple_axial.3 = (bf16[2,8,64,128]{3,2,1,0:T(8,128)(2,1)S(1)}, bf16[2,8,64,128]{3,2,1,0:T(8,128)(2,1)S(1)}, bf16[2,8,64,128]{3,2,1,0:T(8,128)(2,1)S(1)}, bf16[2,8,64,128]{3,2,1,0:T(8,128)(2,1)S(1)}) custom-call(bf16[4,8,64,512]{3,2,1,0:T(8,128)(2,1)S(1)} %copy-done, bf16[8,64,512]{2,1,0:T(8,128)(2,1)S(1)} %collective-permute-done.refs_1_, ...), custom_call_target="tpu_custom_call" | custom-call | flops 1073741824 | bytes 6422528 | tf_op jit(solution)/shard_map/couple_axial/pallas_call | solution.py:32
  32.5 3.4 %collective-permute-start.7 = (bf16[2,8,64,128]{3,2,1,0:T(8,128)(2,1)S(1)}, bf16[2,8,64,128]{3,2,1,0:T(8,128)(2,1)S(1)}, u32[]{:S(2)}, u32[]{:S(2)}) collective-permute-start(bf16[2,8,64,128]{3,2,1,0:T(8,128)(2,1)S(1)} %get-tuple-element.47), channel_id=1, source_target_pairs={{0,1},{1,0},{2,3},{3,2},{4,5},{5,4},{6,7},{7,6},{8,9},{9,8},{10,11... | collective-permute-start | bytes 786440 | tf_op jit(solution)/shard_map/ppermute | solution.py:288
  36.0 2.5 %collective-permute-start.8 = (bf16[2,8,64,128]{3,2,1,0:T(8,128)(2,1)S(1)}, bf16[2,8,64,128]{3,2,1,0:T(8,128)(2,1)S(1)}, u32[]{:S(2)}, u32[]{:S(2)}) collective-permute-start(bf16[2,8,64,128]{3,2,1,0:T(8,128)(2,1)S(1)} %get-tuple-element.48), channel_id=1, source_target_pairs={{0,2},{1,3},{2,0},{3,1},{4,6},{5,7},{6,4},{7,5},{8,10},{9,11},{10,... | collective-permute-start | bytes 786440 | tf_op jit(solution)/shard_map/ppermute | solution.py:288
  38.4 0.8 collective-permute-start.9
  39.2 0.0 collective-permute-done.3.refs_4_
  39.2 1.8 %collective-permute-done.1.refs_2_ = bf16[8,64,512]{2,1,0:T(8,128)(2,1)S(1)} collective-permute-done((bf16[8,64,512]{2,1,0:T(8,128)(2,1)}, bf16[8,64,512]{2,1,0:T(8,128)(2,1)S(1)}, u32[]{:S(2)}, u32[]{:S(2)}) %collective-permute-start.1) | collective-permute-done | bytes 524320 | tf_op jit(solution)/shard_map/ppermute | solution.py:300
  41.0 2.9 %couple_axial.2 = (bf16[2,8,64,128]{3,2,1,0:T(8,128)(2,1)S(1)}, bf16[2,8,64,128]{3,2,1,0:T(8,128)(2,1)S(1)}, bf16[2,8,64,128]{3,2,1,0:T(8,128)(2,1)S(1)}, bf16[2,8,64,128]{3,2,1,0:T(8,128)(2,1)S(1)}) custom-call(bf16[4,8,64,512]{3,2,1,0:T(8,128)(2,1)S(1)} %copy-done, bf16[8,64,512]{2,1,0:T(8,128)(2,1)S(1)} %collective-permute-done.refs_1_, ...), custom_call_target="tpu_custom_call" | custom-call | flops 1073741824 | bytes 7471104 | tf_op jit(solution)/shard_map/couple_axial/pallas_call | solution.py:32
  43.8 2.0 %collective-permute-start.4 = (bf16[2,8,64,128]{3,2,1,0:T(8,128)(2,1)S(1)}, bf16[2,8,64,128]{3,2,1,0:T(8,128)(2,1)S(1)}, u32[]{:S(2)}, u32[]{:S(2)}) collective-permute-start(bf16[2,8,64,128]{3,2,1,0:T(8,128)(2,1)S(1)} %get-tuple-element.41), channel_id=1, source_target_pairs={{0,1},{1,0},{2,3},{3,2},{4,5},{5,4},{6,7},{7,6},{8,9},{9,8},{10,11... | collective-permute-start | bytes 786440 | tf_op jit(solution)/shard_map/ppermute | solution.py:288
  45.8 2.5 %collective-permute-start.5 = (bf16[2,8,64,128]{3,2,1,0:T(8,128)(2,1)S(1)}, bf16[2,8,64,128]{3,2,1,0:T(8,128)(2,1)S(1)}, u32[]{:S(2)}, u32[]{:S(2)}) collective-permute-start(bf16[2,8,64,128]{3,2,1,0:T(8,128)(2,1)S(1)} %get-tuple-element.42), channel_id=1, source_target_pairs={{0,2},{1,3},{2,0},{3,1},{4,6},{5,7},{6,4},{7,5},{8,10},{9,11},{10,... | collective-permute-start | bytes 786440 | tf_op jit(solution)/shard_map/ppermute | solution.py:288
  48.3 0.0 collective-permute-done.7.refs_1_
  48.3 0.8 collective-permute-start.6
  49.1 0.0 collective-permute-done.8.refs_2_
  49.1 2.5 %collective-permute-done.9.refs_3_ = bf16[2,8,64,128]{3,2,1,0:T(8,128)(2,1)S(1)} collective-permute-done((bf16[2,8,64,128]{3,2,1,0:T(8,128)(2,1)S(1)}, bf16[2,8,64,128]{3,2,1,0:T(8,128)(2,1)S(1)}, u32[]{:S(2)}, u32[]{:S(2)}) %collective-permute-start.9) | collective-permute-done | bytes 262176 | tf_op jit(solution)/shard_map/ppermute | solution.py:288
  51.6 0.4 radial.3
  52.0 0.9 collective-permute-start.13
  53.0 0.6 collective-permute-start.11
  53.6 0.0 collective-permute-done.4.refs_1_
  53.6 3.0 %collective-permute-done.5.refs_2_ = bf16[2,8,64,128]{3,2,1,0:T(8,128)(2,1)S(1)} collective-permute-done((bf16[2,8,64,128]{3,2,1,0:T(8,128)(2,1)S(1)}, bf16[2,8,64,128]{3,2,1,0:T(8,128)(2,1)S(1)}, u32[]{:S(2)}, u32[]{:S(2)}) %collective-permute-start.5) | collective-permute-done | bytes 262176 | tf_op jit(solution)/shard_map/ppermute | solution.py:288
  56.6 17.0 %collective-permute-done.6.refs_3_ = bf16[2,8,64,128]{3,2,1,0:T(8,128)(2,1)S(1)} collective-permute-done((bf16[2,8,64,128]{3,2,1,0:T(8,128)(2,1)S(1)}, bf16[2,8,64,128]{3,2,1,0:T(8,128)(2,1)S(1)}, u32[]{:S(2)}, u32[]{:S(2)}) %collective-permute-start.6) | collective-permute-done | bytes 262176 | tf_op jit(solution)/shard_map/ppermute | solution.py:288
  73.6 0.4 radial.2
  74.0 1.1 collective-permute-start.12
  75.1 0.5 collective-permute-start.10
  75.6 0.0 collective-permute-done.13.refs_7_
  75.6 0.0 collective-permute-done.11.refs_5_
  75.6 11.8 %collective-permute-done.12.refs_6_ = bf16[8,256,128]{2,1,0:T(8,128)(2,1)S(1)} collective-permute-done((bf16[8,256,128]{2,1,0:T(8,128)(2,1)S(1)}, bf16[8,256,128]{2,1,0:T(8,128)(2,1)S(1)}, u32[]{:S(2)}, u32[]{:S(2)}) %collective-permute-start.12) | collective-permute-done | bytes 524320 | tf_op jit(solution)/shard_map/ppermute | solution.py:300
  87.4 4.8 %collective-permute-done.10.refs_4_ = bf16[8,256,128]{2,1,0:T(8,128)(2,1)S(1)} collective-permute-done((bf16[8,256,128]{2,1,0:T(8,128)(2,1)S(1)}, bf16[8,256,128]{2,1,0:T(8,128)(2,1)S(1)}, u32[]{:S(2)}, u32[]{:S(2)}) %collective-permute-start.10) | collective-permute-done | bytes 524320 | tf_op jit(solution)/shard_map/ppermute | solution.py:300
  92.2 0.9 couple.3
  93.1 1.6 %collective-permute-start.20 = (bf16[2,8,64,128]{3,2,1,0:T(8,128)(2,1)S(1)}, bf16[2,8,64,128]{3,2,1,0:T(8,128)(2,1)S(1)}, u32[]{:S(2)}, u32[]{:S(2)}) collective-permute-start(bf16[2,8,64,128]{3,2,1,0:T(8,128)(2,1)S(1)} %get-tuple-element.64), channel_id=1, source_target_pairs={{0,1},{1,0},{2,3},{3,2},{4,5},{5,4},{6,7},{7,6},{8,9},{9,8},{10,11... | collective-permute-start | bytes 786440 | tf_op jit(solution)/shard_map/ppermute | solution.py:288
  94.7 2.2 %collective-permute-start.21 = (bf16[2,8,64,128]{3,2,1,0:T(8,128)(2,1)S(1)}, bf16[2,8,64,128]{3,2,1,0:T(8,128)(2,1)S(1)}, u32[]{:S(2)}, u32[]{:S(2)}) collective-permute-start(bf16[2,8,64,128]{3,2,1,0:T(8,128)(2,1)S(1)} %get-tuple-element.65), channel_id=1, source_target_pairs={{0,2},{1,3},{2,0},{3,1},{4,6},{5,7},{6,4},{7,5},{8,10},{9,11},{10,... | collective-permute-start | bytes 786440 | tf_op jit(solution)/shard_map/ppermute | solution.py:288
  96.9 1.0 collective-permute-start.22
  97.9 0.9 couple.2
  98.8 0.2 collective-permute-start.14
  99.0 2.2 %collective-permute-start.15 = (bf16[2,8,64,128]{3,2,1,0:T(8,128)(2,1)S(1)}, bf16[2,8,64,128]{3,2,1,0:T(8,128)(2,1)S(1)}, u32[]{:S(2)}, u32[]{:S(2)}) collective-permute-start(bf16[2,8,64,128]{3,2,1,0:T(8,128)(2,1)S(1)} %get-tuple-element.55), channel_id=1, source_target_pairs={{0,2},{1,3},{2,0},{3,1},{4,6},{5,7},{6,4},{7,5},{8,10},{9,11},{10,... | collective-permute-start | bytes 786440 | tf_op jit(solution)/shard_map/ppermute | solution.py:288
  101.3 0.0 collective-permute-done.20.refs_1_
  101.3 1.3 collective-permute-start.16
  102.5 1.5 %collective-permute-done.21.refs_2_ = bf16[2,8,64,128]{3,2,1,0:T(8,128)(2,1)S(1)} collective-permute-done((bf16[2,8,64,128]{3,2,1,0:T(8,128)(2,1)S(1)}, bf16[2,8,64,128]{3,2,1,0:T(8,128)(2,1)S(1)}, u32[]{:S(2)}, u32[]{:S(2)}) %collective-permute-start.21) | collective-permute-done | bytes 262176 | tf_op jit(solution)/shard_map/ppermute | solution.py:288
  104.0 6.3 %collective-permute-done.22.refs_3_ = bf16[2,8,64,128]{3,2,1,0:T(8,128)(2,1)S(1)} collective-permute-done((bf16[2,8,64,128]{3,2,1,0:T(8,128)(2,1)S(1)}, bf16[2,8,64,128]{3,2,1,0:T(8,128)(2,1)S(1)}, u32[]{:S(2)}, u32[]{:S(2)}) %collective-permute-start.22) | collective-permute-done | bytes 262176 | tf_op jit(solution)/shard_map/ppermute | solution.py:288
  110.3 0.7 axial.3
  111.0 0.1 collective-permute-start.23
  111.1 2.3 %collective-permute-start.24 = (bf16[2,8,64,128]{3,2,1,0:T(8,128)(2,1)S(1)}, bf16[2,8,64,128]{3,2,1,0:T(8,128)(2,1)S(1)}, u32[]{:S(2)}, u32[]{:S(2)}) collective-permute-start(bf16[2,8,64,128]{3,2,1,0:T(8,128)(2,1)S(1)} %get-tuple-element.69), channel_id=1, source_target_pairs={{0,2},{1,3},{2,0},{3,1},{4,6},{5,7},{6,4},{7,5},{8,10},{9,11},{10,... | collective-permute-start | bytes 786440 | tf_op jit(solution)/shard_map/ppermute | solution.py:288
  113.4 0.0 collective-permute-done.14.refs_1_
  113.5 1.3 collective-permute-start.25
  114.8 0.5 collective-permute-done.15.refs_2_
  115.3 6.3 %collective-permute-done.16.refs_3_ = bf16[2,8,64,128]{3,2,1,0:T(8,128)(2,1)S(1)} collective-permute-done((bf16[2,8,64,128]{3,2,1,0:T(8,128)(2,1)S(1)}, bf16[2,8,64,128]{3,2,1,0:T(8,128)(2,1)S(1)}, u32[]{:S(2)}, u32[]{:S(2)}) %collective-permute-start.16) | collective-permute-done | bytes 262176 | tf_op jit(solution)/shard_map/ppermute | solution.py:288
  121.6 0.7 axial.2
  122.3 0.1 collective-permute-start.17
  122.4 2.3 %collective-permute-start.18 = (bf16[2,8,64,128]{3,2,1,0:T(8,128)(2,1)S(1)}, bf16[2,8,64,128]{3,2,1,0:T(8,128)(2,1)S(1)}, u32[]{:S(2)}, u32[]{:S(2)}) collective-permute-start(bf16[2,8,64,128]{3,2,1,0:T(8,128)(2,1)S(1)} %get-tuple-element.60), channel_id=1, source_target_pairs={{0,2},{1,3},{2,0},{3,1},{4,6},{5,7},{6,4},{7,5},{8,10},{9,11},{10,... | collective-permute-start | bytes 786440 | tf_op jit(solution)/shard_map/ppermute | solution.py:288
  124.7 1.3 collective-permute-start.19
  126.0 0.5 collective-permute-done.24.refs_2_
  126.5 6.3 %collective-permute-done.25.refs_3_ = bf16[2,8,64,128]{3,2,1,0:T(8,128)(2,1)S(1)} collective-permute-done((bf16[2,8,64,128]{3,2,1,0:T(8,128)(2,1)S(1)}, bf16[2,8,64,128]{3,2,1,0:T(8,128)(2,1)S(1)}, u32[]{:S(2)}, u32[]{:S(2)}) %collective-permute-start.25) | collective-permute-done | bytes 262176 | tf_op jit(solution)/shard_map/ppermute | solution.py:288
  132.8 1.4 radial_last.2.refs_5_
  134.2 3.5 %collective-permute-done.18.refs_2_ = bf16[2,8,64,128]{3,2,1,0:T(8,128)(2,1)S(1)} collective-permute-done((bf16[2,8,64,128]{3,2,1,0:T(8,128)(2,1)S(1)}, bf16[2,8,64,128]{3,2,1,0:T(8,128)(2,1)S(1)}, u32[]{:S(2)}, u32[]{:S(2)}) %collective-permute-start.18) | collective-permute-done | bytes 262176 | tf_op jit(solution)/shard_map/ppermute | solution.py:288
  137.8 5.8 %collective-permute-done.19.refs_3_ = bf16[2,8,64,128]{3,2,1,0:T(8,128)(2,1)S(1)} collective-permute-done((bf16[2,8,64,128]{3,2,1,0:T(8,128)(2,1)S(1)}, bf16[2,8,64,128]{3,2,1,0:T(8,128)(2,1)S(1)}, u32[]{:S(2)}, u32[]{:S(2)}) %collective-permute-start.19) | collective-permute-done | bytes 262176 | tf_op jit(solution)/shard_map/ppermute | solution.py:288
  143.6 1.4 radial_last.3
  (18 shorter events, 0.0 us)
Async XLA Ops:
  0.0 18.5 %copy-start.8 = (bf16[512,512]{1,0:T(8,128)(2,1)S(1)}, bf16[512,512]{1,0:T(8,128)(2,1)}, u32[]{:S(2)}) copy-start(bf16[512,512]{1,0:T(8,128)(2,1)} %constant.6.clone.q_ref) | copy-start | bytes 1572868
  0.0 18.5 %copy-start.4 = (f32[4,512]{1,0:T(4,128)S(1)}, f32[4,512]{1,0:T(4,128)}, u32[]{:S(2)}) copy-start(f32[4,512]{1,0:T(4,128)} %damp_ref.1) | copy-start | bytes 24580
  0.0 18.5 %copy-start.6 = (f32[8,8]{1,0:T(8,128)S(1)}, f32[8,8]{1,0:T(8,128)}, u32[]{:S(2)}) copy-start(f32[8,8]{1,0:T(8,128)} %two_ref.1) | copy-start | bytes 772
  0.0 18.5 %copy-start.5 = (f32[8,8]{1,0:T(8,128)S(1)}, f32[8,8]{1,0:T(8,128)}, u32[]{:S(2)}) copy-start(f32[8,8]{1,0:T(8,128)} %one_ref.1) | copy-start | bytes 772
  0.0 18.5 %copy-start.7 = (s32[4]{0:T(128)S(1)}, s32[4]{0:T(128)}, u32[]{:S(2)}) copy-start(s32[4]{0:T(128)} %len_ref.1) | copy-start | bytes 52
  0.0 18.5 %copy-start.3 = (bf16[4,256,256]{2,1,0:T(8,128)(2,1)S(1)}, bf16[4,256,256]{2,1,0:T(8,128)(2,1)}, u32[]{:S(2)}) copy-start(bf16[4,256,256]{2,1,0:T(8,128)(2,1)} %rad_ref.1) | copy-start | bytes 1572868
  3.0 23.4 %collective-permute-start.2 = (bf16[8,64,512]{2,1,0:T(8,128)(2,1)}, bf16[8,64,512]{2,1,0:T(8,128)(2,1)S(1)}, u32[]{:S(2)}, u32[]{:S(2)}) collective-permute-start(bf16[8,64,512]{2,1,0:T(8,128)(2,1)} %get-tuple-element.72), channel_id=1, source_target_pairs={{4,0},{8,4},{12,8},{16,12},{20,16},{24,20},{28,24},{32,28},{36,32}... | collective-permute-start | bytes 1572872 | tf_op jit(solution)/shard_map/ppermute | solution.py:300
  12.8 16.9 %collective-permute-start = (bf16[8,64,512]{2,1,0:T(8,128)(2,1)}, bf16[8,64,512]{2,1,0:T(8,128)(2,1)S(1)}, u32[]{:S(2)}, u32[]{:S(2)}) collective-permute-start(bf16[8,64,512]{2,1,0:T(8,128)(2,1)} %get-tuple-element.74), channel_id=1, source_target_pairs={{0,4},{4,8},{8,12},{12,16},{16,20},{20,24},{24,28},{28,32},{32,36}... | collective-permute-start | bytes 1572872 | tf_op jit(solution)/shard_map/ppermute | solution.py:300
  12.8 26.4 %collective-permute-start.3 = (bf16[8,64,512]{2,1,0:T(8,128)(2,1)}, bf16[8,64,512]{2,1,0:T(8,128)(2,1)S(1)}, u32[]{:S(2)}, u32[]{:S(2)}) collective-permute-start(bf16[8,64,512]{2,1,0:T(8,128)(2,1)} %get-tuple-element.71), channel_id=1, source_target_pairs={{4,0},{8,4},{12,8},{16,12},{20,16},{24,20},{28,24},{32,28},{36,32}... | collective-permute-start | bytes 1572872 | tf_op jit(solution)/shard_map/ppermute | solution.py:300
  18.5 22.5 %collective-permute-start.1 = (bf16[8,64,512]{2,1,0:T(8,128)(2,1)}, bf16[8,64,512]{2,1,0:T(8,128)(2,1)S(1)}, u32[]{:S(2)}, u32[]{:S(2)}) collective-permute-start(bf16[8,64,512]{2,1,0:T(8,128)(2,1)} %get-tuple-element.73), channel_id=1, source_target_pairs={{0,4},{4,8},{8,12},{12,16},{16,20},{20,24},{24,28},{28,32},{32,36}... | collective-permute-start | bytes 1572872 | tf_op jit(solution)/shard_map/ppermute | solution.py:300
  18.5 11.2 %copy-start = (bf16[4,8,64,512]{3,2,1,0:T(8,128)(2,1)S(1)}, bf16[4,8,64,512]{3,2,1,0:T(8,128)(2,1)}, u32[]{:S(2)}) copy-start(bf16[4,8,64,512]{3,2,1,0:T(8,128)(2,1)} %refs_0_.3) | copy-start | bytes 6291460
  25.0 1.4 copy-start.2
  32.5 15.8 %collective-permute-start.7 = (bf16[2,8,64,128]{3,2,1,0:T(8,128)(2,1)S(1)}, bf16[2,8,64,128]{3,2,1,0:T(8,128)(2,1)S(1)}, u32[]{:S(2)}, u32[]{:S(2)}) collective-permute-start(bf16[2,8,64,128]{3,2,1,0:T(8,128)(2,1)S(1)} %get-tuple-element.47), channel_id=1, source_target_pairs={{0,1},{1,0},{2,3},{3,2},{4,5},{5,4},{6,7},{7,6},{8,9},{9,8},{10,11... | collective-permute-start | bytes 786440 | tf_op jit(solution)/shard_map/ppermute | solution.py:288
  36.0 13.1 %collective-permute-start.8 = (bf16[2,8,64,128]{3,2,1,0:T(8,128)(2,1)S(1)}, bf16[2,8,64,128]{3,2,1,0:T(8,128)(2,1)S(1)}, u32[]{:S(2)}, u32[]{:S(2)}) collective-permute-start(bf16[2,8,64,128]{3,2,1,0:T(8,128)(2,1)S(1)} %get-tuple-element.48), channel_id=1, source_target_pairs={{0,2},{1,3},{2,0},{3,1},{4,6},{5,7},{6,4},{7,5},{8,10},{9,11},{10,... | collective-permute-start | bytes 786440 | tf_op jit(solution)/shard_map/ppermute | solution.py:288
  38.4 13.2 %collective-permute-start.9 = (bf16[2,8,64,128]{3,2,1,0:T(8,128)(2,1)S(1)}, bf16[2,8,64,128]{3,2,1,0:T(8,128)(2,1)S(1)}, u32[]{:S(2)}, u32[]{:S(2)}) collective-permute-start(bf16[2,8,64,128]{3,2,1,0:T(8,128)(2,1)S(1)} %get-tuple-element.49), channel_id=1, source_target_pairs={{0,3},{1,2},{2,1},{3,0},{4,7},{5,6},{6,5},{7,4},{8,11},{9,10},{10,... | collective-permute-start | bytes 786440 | tf_op jit(solution)/shard_map/ppermute | solution.py:288
  43.8 9.8 %collective-permute-start.4 = (bf16[2,8,64,128]{3,2,1,0:T(8,128)(2,1)S(1)}, bf16[2,8,64,128]{3,2,1,0:T(8,128)(2,1)S(1)}, u32[]{:S(2)}, u32[]{:S(2)}) collective-permute-start(bf16[2,8,64,128]{3,2,1,0:T(8,128)(2,1)S(1)} %get-tuple-element.41), channel_id=1, source_target_pairs={{0,1},{1,0},{2,3},{3,2},{4,5},{5,4},{6,7},{7,6},{8,9},{9,8},{10,11... | collective-permute-start | bytes 786440 | tf_op jit(solution)/shard_map/ppermute | solution.py:288
  45.8 10.7 %collective-permute-start.5 = (bf16[2,8,64,128]{3,2,1,0:T(8,128)(2,1)S(1)}, bf16[2,8,64,128]{3,2,1,0:T(8,128)(2,1)S(1)}, u32[]{:S(2)}, u32[]{:S(2)}) collective-permute-start(bf16[2,8,64,128]{3,2,1,0:T(8,128)(2,1)S(1)} %get-tuple-element.42), channel_id=1, source_target_pairs={{0,2},{1,3},{2,0},{3,1},{4,6},{5,7},{6,4},{7,5},{8,10},{9,11},{10,... | collective-permute-start | bytes 786440 | tf_op jit(solution)/shard_map/ppermute | solution.py:288
  48.3 25.3 %collective-permute-start.6 = (bf16[2,8,64,128]{3,2,1,0:T(8,128)(2,1)S(1)}, bf16[2,8,64,128]{3,2,1,0:T(8,128)(2,1)S(1)}, u32[]{:S(2)}, u32[]{:S(2)}) collective-permute-start(bf16[2,8,64,128]{3,2,1,0:T(8,128)(2,1)S(1)} %get-tuple-element.43), channel_id=1, source_target_pairs={{0,3},{1,2},{2,1},{3,0},{4,7},{5,6},{6,5},{7,4},{8,11},{9,10},{10,... | collective-permute-start | bytes 786440 | tf_op jit(solution)/shard_map/ppermute | solution.py:288
  52.0 23.5 %collective-permute-start.13 = (bf16[8,256,128]{2,1,0:T(8,128)(2,1)S(1)}, bf16[8,256,128]{2,1,0:T(8,128)(2,1)S(1)}, u32[]{:S(2)}, u32[]{:S(2)}) collective-permute-start(bf16[8,256,128]{2,1,0:T(8,128)(2,1)S(1)} %get-tuple-element.50.refs_1_), channel_id=1, source_target_pairs={{4,0},{8,4},{12,8},{16,12},{20,16},{24,20},{28,24},{32,28},{36,32}... | collective-permute-start | bytes 1572872 | tf_op jit(solution)/shard_map/ppermute | solution.py:300
  53.0 22.6 %collective-permute-start.11 = (bf16[8,256,128]{2,1,0:T(8,128)(2,1)S(1)}, bf16[8,256,128]{2,1,0:T(8,128)(2,1)S(1)}, u32[]{:S(2)}, u32[]{:S(2)}) collective-permute-start(bf16[8,256,128]{2,1,0:T(8,128)(2,1)S(1)} %get-tuple-element.51.refs_2_), channel_id=1, source_target_pairs={{0,4},{4,8},{8,12},{12,16},{16,20},{20,24},{24,28},{28,32},{32,36}... | collective-permute-start | bytes 1572872 | tf_op jit(solution)/shard_map/ppermute | solution.py:300
  74.0 13.4 %collective-permute-start.12 = (bf16[8,256,128]{2,1,0:T(8,128)(2,1)S(1)}, bf16[8,256,128]{2,1,0:T(8,128)(2,1)S(1)}, u32[]{:S(2)}, u32[]{:S(2)}) collective-permute-start(bf16[8,256,128]{2,1,0:T(8,128)(2,1)S(1)} %get-tuple-element.45.refs_0_), channel_id=1, source_target_pairs={{4,0},{8,4},{12,8},{16,12},{20,16},{24,20},{28,24},{32,28},{36,32}... | collective-permute-start | bytes 1572872 | tf_op jit(solution)/shard_map/ppermute | solution.py:300
  75.1 17.1 %collective-permute-start.10 = (bf16[8,256,128]{2,1,0:T(8,128)(2,1)S(1)}, bf16[8,256,128]{2,1,0:T(8,128)(2,1)S(1)}, u32[]{:S(2)}, u32[]{:S(2)}) collective-permute-start(bf16[8,256,128]{2,1,0:T(8,128)(2,1)S(1)} %get-tuple-element.52.refs_3_), channel_id=1, source_target_pairs={{0,4},{4,8},{8,12},{12,16},{16,20},{20,24},{24,28},{28,32},{32,36}... | collective-permute-start | bytes 1572872 | tf_op jit(solution)/shard_map/ppermute | solution.py:300
  93.1 8.2 %collective-permute-start.20 = (bf16[2,8,64,128]{3,2,1,0:T(8,128)(2,1)S(1)}, bf16[2,8,64,128]{3,2,1,0:T(8,128)(2,1)S(1)}, u32[]{:S(2)}, u32[]{:S(2)}) collective-permute-start(bf16[2,8,64,128]{3,2,1,0:T(8,128)(2,1)S(1)} %get-tuple-element.64), channel_id=1, source_target_pairs={{0,1},{1,0},{2,3},{3,2},{4,5},{5,4},{6,7},{7,6},{8,9},{9,8},{10,11... | collective-permute-start | bytes 786440 | tf_op jit(solution)/shard_map/ppermute | solution.py:288
  94.7 9.4 %collective-permute-start.21 = (bf16[2,8,64,128]{3,2,1,0:T(8,128)(2,1)S(1)}, bf16[2,8,64,128]{3,2,1,0:T(8,128)(2,1)S(1)}, u32[]{:S(2)}, u32[]{:S(2)}) collective-permute-start(bf16[2,8,64,128]{3,2,1,0:T(8,128)(2,1)S(1)} %get-tuple-element.65), channel_id=1, source_target_pairs={{0,2},{1,3},{2,0},{3,1},{4,6},{5,7},{6,4},{7,5},{8,10},{9,11},{10,... | collective-permute-start | bytes 786440 | tf_op jit(solution)/shard_map/ppermute | solution.py:288
  96.9 13.4 %copy-start.1 = (bf16[4,512,512]{2,1,0:T(8,128)(2,1)S(1)}, bf16[4,512,512]{2,1,0:T(8,128)(2,1)}, u32[]{:S(2)}) copy-start(bf16[4,512,512]{2,1,0:T(8,128)(2,1)} %get-tuple-element.57.refs_4_) | copy-start | bytes 6291460
  96.9 13.4 %collective-permute-start.22 = (bf16[2,8,64,128]{3,2,1,0:T(8,128)(2,1)S(1)}, bf16[2,8,64,128]{3,2,1,0:T(8,128)(2,1)S(1)}, u32[]{:S(2)}, u32[]{:S(2)}) collective-permute-start(bf16[2,8,64,128]{3,2,1,0:T(8,128)(2,1)S(1)} %get-tuple-element.66), channel_id=1, source_target_pairs={{0,3},{1,2},{2,1},{3,0},{4,7},{5,6},{6,5},{7,4},{8,11},{9,10},{10,... | collective-permute-start | bytes 786440 | tf_op jit(solution)/shard_map/ppermute | solution.py:288
  98.8 14.7 %collective-permute-start.14 = (bf16[2,8,64,128]{3,2,1,0:T(8,128)(2,1)S(1)}, bf16[2,8,64,128]{3,2,1,0:T(8,128)(2,1)S(1)}, u32[]{:S(2)}, u32[]{:S(2)}) collective-permute-start(bf16[2,8,64,128]{3,2,1,0:T(8,128)(2,1)S(1)} %get-tuple-element.54), channel_id=1, source_target_pairs={{0,1},{1,0},{2,3},{3,2},{4,5},{5,4},{6,7},{7,6},{8,9},{9,8},{10,11... | collective-permute-start | bytes 786440 | tf_op jit(solution)/shard_map/ppermute | solution.py:288
  99.0 16.3 %collective-permute-start.15 = (bf16[2,8,64,128]{3,2,1,0:T(8,128)(2,1)S(1)}, bf16[2,8,64,128]{3,2,1,0:T(8,128)(2,1)S(1)}, u32[]{:S(2)}, u32[]{:S(2)}) collective-permute-start(bf16[2,8,64,128]{3,2,1,0:T(8,128)(2,1)S(1)} %get-tuple-element.55), channel_id=1, source_target_pairs={{0,2},{1,3},{2,0},{3,1},{4,6},{5,7},{6,4},{7,5},{8,10},{9,11},{10,... | collective-permute-start | bytes 786440 | tf_op jit(solution)/shard_map/ppermute | solution.py:288
  101.3 20.3 %collective-permute-start.16 = (bf16[2,8,64,128]{3,2,1,0:T(8,128)(2,1)S(1)}, bf16[2,8,64,128]{3,2,1,0:T(8,128)(2,1)S(1)}, u32[]{:S(2)}, u32[]{:S(2)}) collective-permute-start(bf16[2,8,64,128]{3,2,1,0:T(8,128)(2,1)S(1)} %get-tuple-element.56), channel_id=1, source_target_pairs={{0,3},{1,2},{2,1},{3,0},{4,7},{5,6},{6,5},{7,4},{8,11},{9,10},{10,... | collective-permute-start | bytes 786440 | tf_op jit(solution)/shard_map/ppermute | solution.py:288
  111.0 13.6 %collective-permute-start.23 = (bf16[2,8,64,128]{3,2,1,0:T(8,128)(2,1)S(1)}, bf16[2,8,64,128]{3,2,1,0:T(8,128)(2,1)S(1)}, u32[]{:S(2)}, u32[]{:S(2)}) collective-permute-start(bf16[2,8,64,128]{3,2,1,0:T(8,128)(2,1)S(1)} %get-tuple-element.68), channel_id=1, source_target_pairs={{0,1},{1,0},{2,3},{3,2},{4,5},{5,4},{6,7},{7,6},{8,9},{9,8},{10,11... | collective-permute-start | bytes 786440 | tf_op jit(solution)/shard_map/ppermute | solution.py:288
  111.1 15.4 %collective-permute-start.24 = (bf16[2,8,64,128]{3,2,1,0:T(8,128)(2,1)S(1)}, bf16[2,8,64,128]{3,2,1,0:T(8,128)(2,1)S(1)}, u32[]{:S(2)}, u32[]{:S(2)}) collective-permute-start(bf16[2,8,64,128]{3,2,1,0:T(8,128)(2,1)S(1)} %get-tuple-element.69), channel_id=1, source_target_pairs={{0,2},{1,3},{2,0},{3,1},{4,6},{5,7},{6,4},{7,5},{8,10},{9,11},{10,... | collective-permute-start | bytes 786440 | tf_op jit(solution)/shard_map/ppermute | solution.py:288
  113.5 19.3 %collective-permute-start.25 = (bf16[2,8,64,128]{3,2,1,0:T(8,128)(2,1)S(1)}, bf16[2,8,64,128]{3,2,1,0:T(8,128)(2,1)S(1)}, u32[]{:S(2)}, u32[]{:S(2)}) collective-permute-start(bf16[2,8,64,128]{3,2,1,0:T(8,128)(2,1)S(1)} %get-tuple-element.70), channel_id=1, source_target_pairs={{0,3},{1,2},{2,1},{3,0},{4,7},{5,6},{6,5},{7,4},{8,11},{9,10},{10,... | collective-permute-start | bytes 786440 | tf_op jit(solution)/shard_map/ppermute | solution.py:288
  122.3 11.9 %collective-permute-start.17 = (bf16[2,8,64,128]{3,2,1,0:T(8,128)(2,1)S(1)}, bf16[2,8,64,128]{3,2,1,0:T(8,128)(2,1)S(1)}, u32[]{:S(2)}, u32[]{:S(2)}) collective-permute-start(bf16[2,8,64,128]{3,2,1,0:T(8,128)(2,1)S(1)} %get-tuple-element.59), channel_id=1, source_target_pairs={{0,1},{1,0},{2,3},{3,2},{4,5},{5,4},{6,7},{7,6},{8,9},{9,8},{10,11... | collective-permute-start | bytes 786440 | tf_op jit(solution)/shard_map/ppermute | solution.py:288
  122.4 15.4 %collective-permute-start.18 = (bf16[2,8,64,128]{3,2,1,0:T(8,128)(2,1)S(1)}, bf16[2,8,64,128]{3,2,1,0:T(8,128)(2,1)S(1)}, u32[]{:S(2)}, u32[]{:S(2)}) collective-permute-start(bf16[2,8,64,128]{3,2,1,0:T(8,128)(2,1)S(1)} %get-tuple-element.60), channel_id=1, source_target_pairs={{0,2},{1,3},{2,0},{3,1},{4,6},{5,7},{6,4},{7,5},{8,10},{9,11},{10,... | collective-permute-start | bytes 786440 | tf_op jit(solution)/shard_map/ppermute | solution.py:288
  124.7 18.9 %collective-permute-start.19 = (bf16[2,8,64,128]{3,2,1,0:T(8,128)(2,1)S(1)}, bf16[2,8,64,128]{3,2,1,0:T(8,128)(2,1)S(1)}, u32[]{:S(2)}, u32[]{:S(2)}) collective-permute-start(bf16[2,8,64,128]{3,2,1,0:T(8,128)(2,1)S(1)} %get-tuple-element.61), channel_id=1, source_target_pairs={{0,3},{1,2},{2,1},{3,0},{4,7},{5,6},{6,5},{7,4},{8,11},{9,10},{10,... | collective-permute-start | bytes 786440 | tf_op jit(solution)/shard_map/ppermute | solution.py:288

commit v2 on v1

--- a/solution.py
+++ b/solution.py
@@ -53,35 +53,33 @@
     return jax.ShapeDtypeStruct(dims, dtype)
 
 
-def prep_kernel(peers, me_ref, len_ref, q_ref, damp_ref, rad_ref, one_ref, two_ref, m1_ref, mpp_ref, rpp_ref, rp_ref, w_ref, qp_ref):
-    me = me_ref[0]
+def prep_kernel(peers, order_ref, len_ref, q_ref, damp_ref, rad_ref, one_ref, two_ref, in_ref, out_ref, rin_ref, rout_ref, w_ref, qh_ref, qp_ref, turned_ref):
     nz = q_ref.shape[0]
     block = nz // peers
     for k in range(peers):
-        start = pl.multiple_of((me ^ k) * block, block)
-        qp_ref[k * block : (k + 1) * block, :] = q_ref[pl.ds(start, block), :]
-    qp = qp_ref[...]
+        for at, table in ((k, qh_ref), (peers + k, qp_ref)):
+            start = pl.multiple_of(order_ref[at] * block, block)
+            table[k * block : (k + 1) * block, :] = q_ref[pl.ds(start, block), :]
     for m in range(damp_ref.shape[0]):
         factor = damp_ref[m : m + 1, :]
-        for table, out in ((q_ref, m1_ref), (qp_ref, mpp_ref)):
-            scaled = table[...].astype(F32) * factor
+        for left, right, out in ((qh_ref, q_ref, in_ref), (q_ref, qp_ref, out_ref)):
+            scaled = left[...].astype(F32) * factor
             high = scaled.astype(BF)
             low = (scaled - high.astype(F32)).astype(BF)
-            out[m] = (dot_nt(high, qp) + dot_nt(low, qp)).astype(BF)
+            out[m] = (dot_nt(high, right[...]) + dot_nt(low, right[...])).astype(BF)
     nr = rad_ref.shape[1]
     rows = nr // peers
     for m in range(rad_ref.shape[0]):
+        index = lax.broadcasted_iota(jnp.int32, (nr, nr), 0)
+        turned_ref[...] = jnp.where(index < len_ref[m], rad_ref[m].astype(F32), 0.0).T.astype(BF)
         parts = []
         for k in range(peers):
-            start = pl.multiple_of((me ^ k) * rows, rows)
+            start = pl.multiple_of(order_ref[k] * rows, rows)
+            rin_ref[m, k * rows : (k + 1) * rows, :] = turned_ref[pl.ds(start, rows), :]
             part = rad_ref[m, pl.ds(start, rows), :].astype(F32)
             index = start + lax.broadcasted_iota(jnp.int32, (rows, nr), 0)
             parts.append(jnp.where(index < len_ref[m], part, 0.0))
-        turned = jnp.concatenate(parts, axis=0).T.astype(BF)
-        rp_ref[m] = turned
-        for k in range(peers):
-            start = pl.multiple_of((me ^ k) * rows, rows)
-            rpp_ref[m, k * rows : (k + 1) * rows, :] = rp_ref[m, pl.ds(start, rows), :]
+        rout_ref[m] = jnp.concatenate(parts, axis=0).T.astype(BF)
     comp = one_ref.shape[0]
     wide = comp * SUB
     row = lax.broadcasted_iota(jnp.int32, (wide, comp), 0) // SUB
@@ -97,14 +95,14 @@
         w_ref[:, (2 * at + 1) * wide : (2 * at + 2) * wide] = full
 
 
-def prepare(peers, me, lengths, table, damping, radial, one, two):
+def prepare(peers, order, lengths, table, damping, radial, one, two):
     modes, nz = damping.shape
     nr = radial.shape[1]
     wide = one.shape[0] * SUB
     return call(
         functools.partial(prep_kernel, peers),
         "prepare",
-        (me, lengths, table, damping, radial, one, two),
+        (order, lengths, table, damping, radial, one, two),
         [
             shape(modes, nz, nz),
             shape(modes, nz, nz),
@@ -113,8 +111,73 @@
             shape(wide, 4 * wide),
         ],
         8 * modes * nz**3,
-        scratch=[pltpu.VMEM((nz, nz), BF)],
+        scratch=[pltpu.VMEM((nz, nz), BF), pltpu.VMEM((nz, nz), BF), pltpu.VMEM((nr, nr), BF)],
         smem=2,
+    )
+
+
+def split_kernel(peers, order_ref, *refs):
+    for k in range(peers):
+        refs[peers + k][...] = refs[k][...]
+
+
+def split(peers, order, x, first, step, number):
+    _, comp, rows, nz = x.shape
+    block = nz // peers
+    return pl.pallas_call(
+        functools.partial(split_kernel, peers),
+        grid_spec=pltpu.PrefetchScalarGridSpec(
+            num_scalar_prefetch=1,
+            grid=(number,),
+            in_specs=[
+                pl.BlockSpec(
+                    (1, comp, rows, block),
+                    functools.partial(lambda k, i, order: (first + step * i, 0, 0, order[k]), k),
+                )
+                for k in range(peers)
+            ],
+            out_specs=[pl.BlockSpec((1, comp, rows, block), lambda i, order: (i, 0, 0, 0))] * peers,
+        ),
+        out_shape=[shape(number, comp, rows, block)] * peers,
+        compiler_params=pltpu.CompilerParams(vmem_limit_bytes=VMEM_LIMIT),
+        cost_estimate=pl.CostEstimate(
+            flops=0, bytes_accessed=4 * number * comp * rows * nz, transcendentals=0
+        ),
+        name="split",
+    )(order, *[x] * peers)
+
+
+def by_parity(odd, given, taken):
+    @pl.when(odd == 1)
+    def _():
+        taken[0][...] = given[0][...]
+        taken[1][...] = given[1][...]
+
+    @pl.when(odd == 0)
+    def _():
+        taken[0][...] = given[1][...]
+        taken[1][...] = given[0][...]
+
+
+def assemble_kernel(peers, order_ref, *refs):
+    pieces, outs = refs[:peers], refs[peers:]
+    rows = pieces[0].shape[2]
+    for k in range(peers):
+        start = pl.multiple_of(order_ref[peers + k] * rows, rows)
+        for at, out in enumerate(outs[:2]):
+            out[:, pl.ds(start, rows), :] = pieces[k][at]
+    by_parity(order_ref[2 * peers], outs[:2], outs[2:])
+
+
+def assemble(peers, order, pieces):
+    count, comp, rows, block = pieces[0].shape
+    return call(
+        functools.partial(assemble_kernel, peers),
+        "assemble",
+        (order, *pieces),
+        [shape(comp, rows * peers, block)] * 4,
+        0,
+        smem=1,
     )
 
 
@@ -129,12 +192,15 @@
     return [at(m - 1), at(m + 1), at(m - 2), at(m + 2)]
 
 
-def couple_axial_kernel(peers, modes, count, depth, *refs):
-    x_ref, refs = refs[0], refs[1:]
-    before, after, refs = refs[:depth], refs[depth : 2 * depth], refs[2 * depth :]
+def couple_axial_kernel(peers, modes, count, depth, order_ref, *refs):
+    own, refs = refs[:count], refs[count:]
+    halos, refs = refs[: 2 * depth], refs[2 * depth :]
+    sides = refs[3 + peers :]
+    for i in range(0, 2 * depth, 2):
+        by_parity(order_ref[2 * peers], halos[i : i + 2], sides[i : i + 2])
+    before, after = sides[0::2], sides[1::2]
     w_ref, m_ref = refs[:2]
     outs, a_ref = refs[2 : 2 + peers], refs[2 + peers]
-    own = [x_ref.at[i] for i in range(count)]
     comp, rows, nz = own[0].shape
     wide = comp * SUB
     block = nz // peers
@@ -152,15 +218,17 @@
                 outs[k][at, :, b * SUB : (b + 1) * SUB, :] = piece.reshape(comp, SUB, block)
 
 
-def couple_axial(peers, modes, x, before, after, weights, matrices):
-    count, comp, rows, nz = x.shape
+def couple_axial(peers, order, modes, own, halos, weights, matrices):
+    count = len(own)
+    comp, rows, nz = own[0].shape
     return call(
-        functools.partial(couple_axial_kernel, peers, modes, count, len(before)),
+        functools.partial(couple_axial_kernel, peers, modes, count, len(halos) // 2),
         "couple_axial",
-        (x, *before, *after, weights, matrices),
+        (order, *own, *halos, weights, matrices),
         [shape(len(modes), comp, rows, nz // peers)] * peers,
         len(modes) * comp * rows * nz * 2 * (nz + 4 * comp * SUB),
-        scratch=[pltpu.VMEM((comp * rows, nz), BF)],
+        scratch=[pltpu.VMEM((comp * rows, nz), BF)] + [pltpu.VMEM((comp, rows, nz), BF)] * len(halos),
+        smem=1,
     )
 
 
@@ -171,24 +239,6 @@
         result = dot(matrix, field).astype(BF)
         out[c] = result[:, :block]
         out[c + 1] = result[:, block:]
-
-
-def radial_kernel(peers, modes, *refs):
-    pieces, r_ref, outs = refs[:peers], refs[peers], refs[peers + 1 :]
-    for at, m in enumerate(modes):
-        radial_one([p.at[at] for p in pieces], r_ref[m], outs[at])
-
-
-def radial(peers, modes, pieces, matrices):
-    count, comp, rows, block = pieces[0].shape
-    nr = rows * peers
-    return call(
-        functools.partial(radial_kernel, peers, modes),
-        "radial",
-        (*pieces, matrices),
-        [shape(comp, nr, block)] * count,
-        count * comp * nr * nr * block * 2,
-    )
 
 
 def radial_last_kernel(peers, *refs):
@@ -223,10 +273,15 @@
     )(*args)
 
 
-def couple_kernel(peers, modes, count, *refs):
-    own, before, after = refs[:count], refs[count : count + 2], refs[count + 2 : count + 4]
-    w_ref = refs[count + 4]
-    outs = refs[count + 5 :]
+def couple_radial_kernel(peers, modes, count, depth, order_ref, *refs):
+    own, refs = refs[:count], refs[count:]
+    halos, refs = refs[: 2 * depth], refs[2 * depth :]
+    sides = refs[3 + peers :]
+    for i in range(0, 2 * depth, 2):
+        by_parity(order_ref[2 * peers], halos[i : i + 2], sides[i : i + 2])
+    before, after = sides[0::2], sides[1::2]
+    w_ref, r_ref = refs[:2]
+    outs, a_ref = refs[2 : 2 + peers], refs[2 + peers]
     comp, nr, block = own[0].shape
     rows = nr // peers
     wide = comp * SUB
@@ -245,39 +300,48 @@
             mixed = (dot(w_ref[...], field) + side(own[m], k).astype(F32)).astype(BF)
             for b in range(rows // SUB):
                 piece = mixed[:, b * block : (b + 1) * block]
-                outs[k][at, :, b * SUB : (b + 1) * SUB, :] = piece.reshape(comp, SUB, block)
-
-
-def couple(peers, modes, own, before, after, weights):
+                a_ref[:, k * rows + b * SUB : k * rows + (b + 1) * SUB, :] = piece.reshape(comp, SUB, block)
+        for c in range(0, comp, 2):
+            field = jnp.concatenate([a_ref[c], a_ref[c + 1]], axis=1)
+            result = dot(r_ref[m], field).astype(BF)
+            for k in range(peers):
+                part = slice(k * rows, (k + 1) * rows)
+                outs[k][at, c] = result[part, :block]
+                outs[k][at, c + 1] = result[part, block:]
+
+
+def couple_radial(peers, order, modes, own, halos, weights, matrices):
     comp, nr, block = own[0].shape
     return call(
-        functools.partial(couple_kernel, peers, modes, len(own)),
-        "couple",
-        (*own, *before, *after, weights),
+        functools.partial(couple_radial_kernel, peers, modes, len(own), len(halos) // 2),
+        "couple_radial",
+        (order, *own, *halos, weights, matrices),
         [shape(len(modes), comp, nr // peers, block)] * peers,
-        len(modes) * comp * nr * block * 2 * 4 * comp * SUB,
-    )
-
-
-def axial_kernel(peers, modes, *refs):
+        len(modes) * comp * nr * block * 2 * (4 * comp * SUB + nr),
+        scratch=[pltpu.VMEM((comp, nr, block), BF)] * (1 + len(halos)),
+        smem=1,
+    )
+
+
+def axial_kernel(peers, modes, order_ref, *refs):
     pieces, m_ref, outs = refs[:peers], refs[peers], refs[peers + 1 :]
     comp, rows, block = pieces[0].shape[1:]
     for at, m in enumerate(modes):
         field = jnp.concatenate([p[at].reshape(comp * rows, block) for p in pieces], axis=1)
-        result = dot(field, m_ref[m]).astype(BF)
-        for k in range(peers):
-            outs[k][at] = result[:, k * block : (k + 1) * block].reshape(comp, rows, block)
-
-
-def axial(peers, modes, pieces, matrices):
+        outs[at][...] = dot(field, m_ref[m]).astype(BF).reshape(comp, rows, peers * block)
+    by_parity(order_ref[2 * peers], outs[:2], outs[2:])
+
+
+def axial(peers, order, modes, pieces, matrices):
     count, comp, rows, block = pieces[0].shape
     nz = block * peers
     return call(
         functools.partial(axial_kernel, peers, modes),
         "axial",
-        (*pieces, matrices),
-        [shape(count, comp, rows, block)] * peers,
+        (order, *pieces, matrices),
+        [shape(comp, rows, nz)] * 4,
         count * comp * rows * nz * nz * 2,
+        smem=1,
     )
 
 
@@ -289,43 +353,62 @@
     return result
 
 
+RUN = 8
+
+
+def held(mode, peer):
+    turned = (mode // RUN) % 2 * (peer % 2)
+    return peer ^ (2 * turned)
+
+
 def local(cotangent, radial_ops, lengths, couple_one, couple_two, axial_damping):
     peers, ring = lax.axis_size("pencil"), lax.axis_size("mode")
-    up = [(i, (i + 1) % ring) for i in range(ring)]
-    down = [(j, i) for i, j in up]
+    pairs = ([], [])
+    for mode in range(ring):
+        beyond = (mode + 1) % ring
+        for peer in range(peers):
+            one, other = mode * peers + peer, beyond * peers + held(beyond, held(mode, peer))
+            pairs[mode % 2].extend([(one, other), (other, one)])
     count = cotangent.shape[0]
     modes = tuple(range(count))
 
-    def send(plane, way):
-        return lax.ppermute(plane, "mode", way)
+    def exchange(planes):
+        return tuple(lax.ppermute(p, ("mode", "pencil"), pair) for p, pair in zip(planes, pairs))
 
     table = jnp.asarray(cosine_table(axial_damping.shape[1]))
-    me = lax.axis_index("pencil").astype(jnp.int32).reshape(1)
+    mode, me = lax.axis_index("mode"), lax.axis_index("pencil")
+    others = me ^ jnp.arange(peers, dtype=jnp.int32)
+    order = jnp.concatenate([held(mode, others), others, (mode % 2).reshape(1)]).astype(jnp.int32)
     last = count - 1
-    inner, outer = modes[1:last], (0, last)
-
-    before = [send(cotangent[last], up)]
-    after = [send(cotangent[0], down)]
-    before.append(send(cotangent[last - 1], up))
-    after.append(send(cotangent[1], down))
-    m1, mpp, rpp, rp, weights = prepare(
-        peers, me, lengths, table, axial_damping, radial_ops, couple_one, couple_two
-    )
-    inner_pieces = swap(couple_axial(peers, inner, cotangent, before[:1], after[:1], weights, m1))
-    outer_pieces = swap(couple_axial(peers, outer, cotangent, before, after, weights, m1))
-    planes = dict(zip(inner, radial(peers, inner, inner_pieces, rpp)))
-    far_before, far_after = send(planes[last - 1], up), send(planes[1], down)
-    planes.update(zip(outer, radial(peers, outer, outer_pieces, rpp)))
-    before = [send(planes[last], up), far_before]
-    after = [send(planes[0], down), far_after]
-    planes = [planes[m] for m in modes]
+    inner, outer = (1, last - 1), (0, last)
+
+    pieces_outer = swap(split(peers, order, cotangent, 0, last, 2))
+    pieces_inner = split(peers, order, cotangent, 1, last - 2, 2)
+    in_m, out_m, in_r, out_r, weights = prepare(
+        peers, order, lengths, table, axial_damping, radial_ops, couple_one, couple_two
+    )
+    order, weights, pieces_inner, pieces_outer[2] = lax.optimization_barrier(
+        (order, weights, pieces_inner, pieces_outer[2])
+    )
+    pieces_inner = swap(pieces_inner)
+    low, high, *sent = assemble(peers, order, pieces_outer)
+    near = exchange(sent)
+    own = [low, *assemble(peers, order, pieces_inner), high]
+    far = exchange(own[3:5])
+    own = own[:3] + own[5:]
+    pieces_inner = swap(couple_radial(peers, order, inner, own, near, weights, in_r))
+    pieces_outer = swap(couple_radial(peers, order, outer, own, near + far, weights, in_r))
+    low, high, *sent = axial(peers, order, inner, pieces_inner, in_m)
+    far = exchange(sent)
+    first, final, *sent = axial(peers, order, outer, pieces_outer, in_m)
+    near = exchange(sent)
+    own = [first, low, high, final]
 
     halves = (modes[: count // 2], modes[count // 2 :])
-    pieces = [swap(couple(peers, half, planes, before, after, weights)) for half in halves]
-    pieces = [swap(axial(peers, half, p, mpp)) for half, p in zip(halves, pieces)]
+    pieces = [swap(couple_axial(peers, order, half, own, near + far, weights, out_m)) for half in halves]
     result = None
     for half, p in zip(halves, pieces):
-        result = radial_last(peers, half[0], count, p, rp, result)
+        result = radial_last(peers, half[0], count, p, out_r, result)
     return result
 
 

time: 145 us -> 135 us (0.931)
  waiting for transfers between devices: 75 us -> 49.2 us
  starting transfers between devices: 46.5 us -> 58.6 us
  Pallas kernels: 19 us -> 25.2 us
  local copies, waits for them, and re-layouts: 4.34 us -> 1.62 us
    ppermute x18, waiting for transfers between devices: 53.3 us -> 30.9 us  [swap(): lax.ppermute(pieces[k], 'pencil', [(i, i ^ k) for i in range(peers)])]
    ppermute x8, starting transfers between devices: 18.6 us -> 33.1 us  [exchange(): lax.ppermute(p, ('mode', 'pencil'), pair)]
    pallas_call x9, Pallas kernels: 16.2 us -> 20.5 us  [call(): pl.pallas_call(kernel, out_shape=outs, in_specs=[pl.BlockSpec(memory_spac...]
    ppermute x8, waiting for transfers between devices: 21.7 us -> 18.2 us  [exchange(): lax.ppermute(p, ('mode', 'pencil'), pair)]
    squeeze x1 -> x0, local copies, waits for them, and re-layouts: 2.96 us -> none  [local(): after.append(send(cotangent[1], down))]
    ppermute x18, starting transfers between devices: 27.9 us -> 25.6 us  [swap(): lax.ppermute(pieces[k], 'pencil', [(i, i ^ k) for i in range(peers)])]
    pallas_call x0 -> x2, Pallas kernels: none -> 1.86 us  [split(): pl.pallas_call(functools.partial(split_kernel, peers), grid_spec=pltpu.Pr...]
  transfers between devices with their start and end apart: 26 -> 26, of which waited for: 15 -> 9; matrix products, arithmetic and copies ran while one was open for 0% -> 0% of each run, Pallas kernels for 12% -> 15%
where the time goes in v2:
time: 135 us
  starting transfers between devices  58.6 us (43%)
  waiting for transfers between devices  49.2 us (36%)
  Pallas kernels  25.2 us (19%)
  local copies, waits for them, and re-layouts  1.62 us (1%)
    ppermute x8, starting transfers between devices, exchange(): lax.ppermute(p, ('mode', 'pencil'), pair)  33.1 us
    ppermute x18, waiting for transfers between devices, swap(): lax.ppermute(pieces[k], 'pencil', [(i, i ^ k) for i in range(peers)])  30.9 us
    ppermute x18, starting transfers between devices, swap(): lax.ppermute(pieces[k], 'pencil', [(i, i ^ k) for i in range(peers)])  25.6 us
    pallas_call x9, Pallas kernels, call(): pl.pallas_call(kernel, out_shape=outs, in_specs=[pl.BlockSpec(memory_spac...  20.5 us
    ppermute x8, waiting for transfers between devices, exchange(): lax.ppermute(p, ('mode', 'pencil'), pair)  18.2 us
    pallas_call x2, Pallas kernels, radial_last(): pl.pallas_call(functools.partial(radial_last_kernel, peers), grid=(count,...  2.84 us
  transfers between devices with their start and end apart: 26, of which 9 were waited for; matrix products, arithmetic and copies ran while one was open for 0% of the time, Pallas kernels for 15%

profile of v2, /device:TPU:1, one launch (start us, length us, event | category | flops | bytes accessed | tf_op | source)
XLA Modules:
  0.0 135.0 jit_solution(12433038097226050489)
XLA Ops:
  0.0 0.1 pad_add_fusion.order_ref
  0.1 1.6 %copy-done = bf16[4,8,64,512]{3,2,1,0:T(8,128)(2,1)S(1)} copy-done((bf16[4,8,64,512]{3,2,1,0:T(8,128)(2,1)S(1)}, bf16[4,8,64,512]{3,2,1,0:T(8,128)(2,1)}, u32[]{:S(2)}) %copy-start) | copy-done | bytes 2097176
  1.7 0.9 split.3
  2.6 3.7 %collective-permute-start = (bf16[2,8,64,128]{3,2,1,0:T(8,128)(2,1)S(1)}, bf16[2,8,64,128]{3,2,1,0:T(8,128)(2,1)S(1)}, u32[]{:S(2)}, u32[]{:S(2)}) collective-permute-start(bf16[2,8,64,128]{3,2,1,0:T(8,128)(2,1)S(1)} %get-tuple-element.62), channel_id=1, source_target_pairs={{0,2},{1,3},{2,0},{3,1},{4,6},{5,7},{6,4},{7,5},{8,10},{9,11},{10,... | collective-permute-start | bytes 786440 | tf_op jit(solution)/shard_map/ppermute | solution.py:352
  6.3 1.0 collective-permute-start.1
  7.3 0.0 copy-start.5
  7.3 0.0 copy-start.6
  7.3 1.9 %collective-permute-start.2 = (bf16[2,8,64,128]{3,2,1,0:T(8,128)(2,1)S(1)}, bf16[2,8,64,128]{3,2,1,0:T(8,128)(2,1)S(1)}, u32[]{:S(2)}, u32[]{:S(2)}) collective-permute-start(bf16[2,8,64,128]{3,2,1,0:T(8,128)(2,1)S(1)} %get-tuple-element.67), channel_id=1, source_target_pairs={{0,3},{1,2},{2,1},{3,0},{4,7},{5,6},{6,5},{7,4},{8,11},{9,10},{10,... | collective-permute-start | bytes 786440 | tf_op jit(solution)/shard_map/ppermute | solution.py:352
  9.2 0.9 split.2
  10.2 6.6 %prepare.1 = (bf16[4,512,512]{2,1,0:T(8,128)(2,1)S(1)}, bf16[4,512,512]{2,1,0:T(8,128)(2,1)}, bf16[4,256,256]{2,1,0:T(8,128)(2,1)S(1)}, bf16[4,256,256]{2,1,0:T(8,128)(2,1)S(1)}, bf16[128,512]{1,0:T(8,128)(2,1)S(1)}) custom-call(s32[9]{0:T(128)S(1)} %pad_add_fusion.order_ref, s32[4]{0:T(128)S(1)} %copy-done.5, bf16[512,512]{1,0:T(8,128)(2,1)S(1)} %copy-done.6, ...), custom_call_target="tpu_custom_call" | custom-call | flops 4294967296 | bytes 6431284 | tf_op jit(solution)/shard_map/prepare/pallas_call | solution.py:32
  16.8 0.0 collective-permute-done.refs_2_
  16.8 0.5 collective-permute-start.3
  17.3 1.0 collective-permute-start.4
  18.3 2.1 %collective-permute-start.5 = (bf16[2,8,64,128]{3,2,1,0:T(8,128)(2,1)S(1)}, bf16[2,8,64,128]{3,2,1,0:T(8,128)(2,1)S(1)}, u32[]{:S(2)}, u32[]{:S(2)}) collective-permute-start(bf16[2,8,64,128]{3,2,1,0:T(8,128)(2,1)S(1)} %get-tuple-element.72), channel_id=1, source_target_pairs={{0,3},{1,2},{2,1},{3,0},{4,7},{5,6},{6,5},{7,4},{8,11},{9,10},{10,... | collective-permute-start | bytes 786440 | tf_op jit(solution)/shard_map/ppermute | solution.py:352
  20.5 0.0 collective-permute-done.1.refs_1_
  20.5 0.0 collective-permute-done.2.refs_3_
  20.5 0.7 assemble.2
  21.2 0.1 collective-permute-start.6
  21.3 9.2 %collective-permute-start.7 = (bf16[8,256,128]{2,1,0:T(8,128)(2,1)S(1)}, bf16[8,256,128]{2,1,0:T(8,128)(2,1)S(1)}, u32[]{:S(2)}, u32[]{:S(2)}) collective-permute-start(bf16[8,256,128]{2,1,0:T(8,128)(2,1)S(1)} %get-tuple-element.77), channel_id=1, source_target_pairs={{4,8},{8,4},{5,9},{9,5},{6,10},{10,6},{7,11},{11,7},{12,16},{16,12... | collective-permute-start | bytes 1572872 | tf_op jit(solution)/shard_map/ppermute | solution.py:376
  30.5 0.0 collective-permute-done.3.refs_1_
  30.5 0.0 collective-permute-done.4.refs_2_
  30.5 5.4 %collective-permute-done.5.refs_3_ = bf16[2,8,64,128]{3,2,1,0:T(8,128)(2,1)S(1)} collective-permute-done((bf16[2,8,64,128]{3,2,1,0:T(8,128)(2,1)S(1)}, bf16[2,8,64,128]{3,2,1,0:T(8,128)(2,1)S(1)}, u32[]{:S(2)}, u32[]{:S(2)}) %collective-permute-start.5) | collective-permute-done | bytes 262176 | tf_op jit(solution)/shard_map/ppermute | solution.py:352
  35.8 0.7 assemble.3
  36.5 0.1 collective-permute-start.8
  36.6 10.6 %collective-permute-start.9 = (bf16[8,256,128]{2,1,0:T(8,128)(2,1)S(1)}, bf16[8,256,128]{2,1,0:T(8,128)(2,1)S(1)}, u32[]{:S(2)}, u32[]{:S(2)}) collective-permute-start(bf16[8,256,128]{2,1,0:T(8,128)(2,1)S(1)} %get-tuple-element.79), channel_id=1, source_target_pairs={{4,8},{8,4},{5,9},{9,5},{6,10},{10,6},{7,11},{11,7},{12,16},{16,12... | collective-permute-start | bytes 1572872 | tf_op jit(solution)/shard_map/ppermute | solution.py:376
  47.2 0.0 collective-permute-done.6.refs_4_
  47.2 0.0 collective-permute-done.7.refs_5_
  47.2 2.0 %couple_radial.3 = (bf16[2,8,64,128]{3,2,1,0:T(8,128)(2,1)S(1)}, bf16[2,8,64,128]{3,2,1,0:T(8,128)(2,1)S(1)}, bf16[2,8,64,128]{3,2,1,0:T(8,128)(2,1)S(1)}, bf16[2,8,64,128]{3,2,1,0:T(8,128)(2,1)S(1)}) custom-call(s32[9]{0:T(128)S(1)} %pad_add_fusion.order_ref, bf16[8,256,128]{2,1,0:T(8,128)(2,1)S(1)} %get-tuple-element.68.refs_0_, ...), custom_call_target="tpu_custom_call" | custom-call | flops 805306368 | bytes 4849700 | tf_op jit(solution)/shard_map/couple_radial/pallas_call | solution.py:32
  49.2 0.3 collective-permute-start.13
  49.5 1.8 %collective-permute-start.14 = (bf16[2,8,64,128]{3,2,1,0:T(8,128)(2,1)S(1)}, bf16[2,8,64,128]{3,2,1,0:T(8,128)(2,1)S(1)}, u32[]{:S(2)}, u32[]{:S(2)}) collective-permute-start(bf16[2,8,64,128]{3,2,1,0:T(8,128)(2,1)S(1)} %get-tuple-element.90), channel_id=1, source_target_pairs={{0,2},{1,3},{2,0},{3,1},{4,6},{5,7},{6,4},{7,5},{8,10},{9,11},{10,... | collective-permute-start | bytes 786440 | tf_op jit(solution)/shard_map/ppermute | solution.py:352
  51.3 1.6 %collective-permute-start.15 = (bf16[2,8,64,128]{3,2,1,0:T(8,128)(2,1)S(1)}, bf16[2,8,64,128]{3,2,1,0:T(8,128)(2,1)S(1)}, u32[]{:S(2)}, u32[]{:S(2)}) collective-permute-start(bf16[2,8,64,128]{3,2,1,0:T(8,128)(2,1)S(1)} %get-tuple-element.91), channel_id=1, source_target_pairs={{0,3},{1,2},{2,1},{3,0},{4,7},{5,6},{6,5},{7,4},{8,11},{9,10},{10,... | collective-permute-start | bytes 786440 | tf_op jit(solution)/shard_map/ppermute | solution.py:352
  52.9 0.0 collective-permute-done.8.refs_6_
  52.9 6.4 %collective-permute-done.9.refs_7_ = bf16[8,256,128]{2,1,0:T(8,128)(2,1)S(1)} collective-permute-done((bf16[8,256,128]{2,1,0:T(8,128)(2,1)S(1)}, bf16[8,256,128]{2,1,0:T(8,128)(2,1)S(1)}, u32[]{:S(2)}, u32[]{:S(2)}) %collective-permute-start.9) | collective-permute-done | bytes 524320 | tf_op jit(solution)/shard_map/ppermute | solution.py:376
  59.3 2.0 %couple_radial.2 = (bf16[2,8,64,128]{3,2,1,0:T(8,128)(2,1)S(1)}, bf16[2,8,64,128]{3,2,1,0:T(8,128)(2,1)S(1)}, bf16[2,8,64,128]{3,2,1,0:T(8,128)(2,1)S(1)}, bf16[2,8,64,128]{3,2,1,0:T(8,128)(2,1)S(1)}) custom-call(s32[9]{0:T(128)S(1)} %pad_add_fusion.order_ref, bf16[8,256,128]{2,1,0:T(8,128)(2,1)S(1)} %get-tuple-element.68.refs_0_, ...), custom_call_target="tpu_custom_call" | custom-call | flops 805306368 | bytes 5898276 | tf_op jit(solution)/shard_map/couple_radial/pallas_call | solution.py:32
  61.4 0.9 collective-permute-start.10
  62.3 1.5 %collective-permute-start.11 = (bf16[2,8,64,128]{3,2,1,0:T(8,128)(2,1)S(1)}, bf16[2,8,64,128]{3,2,1,0:T(8,128)(2,1)S(1)}, u32[]{:S(2)}, u32[]{:S(2)}) collective-permute-start(bf16[2,8,64,128]{3,2,1,0:T(8,128)(2,1)S(1)} %get-tuple-element.84), channel_id=1, source_target_pairs={{0,2},{1,3},{2,0},{3,1},{4,6},{5,7},{6,4},{7,5},{8,10},{9,11},{10,... | collective-permute-start | bytes 786440 | tf_op jit(solution)/shard_map/ppermute | solution.py:352
  63.8 0.0 collective-permute-done.13.refs_1_
  63.8 1.7 %collective-permute-start.12 = (bf16[2,8,64,128]{3,2,1,0:T(8,128)(2,1)S(1)}, bf16[2,8,64,128]{3,2,1,0:T(8,128)(2,1)S(1)}, u32[]{:S(2)}, u32[]{:S(2)}) collective-permute-start(bf16[2,8,64,128]{3,2,1,0:T(8,128)(2,1)S(1)} %get-tuple-element.85), channel_id=1, source_target_pairs={{0,3},{1,2},{2,1},{3,0},{4,7},{5,6},{6,5},{7,4},{8,11},{9,10},{10,... | collective-permute-start | bytes 786440 | tf_op jit(solution)/shard_map/ppermute | solution.py:352
  65.5 1.3 collective-permute-done.15.refs_3_
  66.8 1.3 axial.3
  68.2 0.1 collective-permute-start.18
  68.3 5.9 %collective-permute-start.19 = (bf16[8,64,512]{2,1,0:T(8,128)(2,1)S(1)}, bf16[8,64,512]{2,1,0:T(8,128)(2,1)S(1)}, u32[]{:S(2)}, u32[]{:S(2)}) collective-permute-start(bf16[8,64,512]{2,1,0:T(8,128)(2,1)S(1)} %get-tuple-element.98), channel_id=1, source_target_pairs={{4,8},{8,4},{5,9},{9,5},{6,10},{10,6},{7,11},{11,7},{12,16},{16,12... | collective-permute-start | bytes 1572872 | tf_op jit(solution)/shard_map/ppermute | solution.py:376
  74.2 0.0 collective-permute-done.11.refs_2_
  74.2 9.5 %collective-permute-done.12.refs_3_ = bf16[2,8,64,128]{3,2,1,0:T(8,128)(2,1)S(1)} collective-permute-done((bf16[2,8,64,128]{3,2,1,0:T(8,128)(2,1)S(1)}, bf16[2,8,64,128]{3,2,1,0:T(8,128)(2,1)S(1)}, u32[]{:S(2)}, u32[]{:S(2)}) %collective-permute-start.12) | collective-permute-done | bytes 262176 | tf_op jit(solution)/shard_map/ppermute | solution.py:352
  83.7 1.3 axial.2
  85.0 0.1 collective-permute-start.16
  85.1 7.0 %collective-permute-start.17 = (bf16[8,64,512]{2,1,0:T(8,128)(2,1)S(1)}, bf16[8,64,512]{2,1,0:T(8,128)(2,1)S(1)}, u32[]{:S(2)}, u32[]{:S(2)}) collective-permute-start(bf16[8,64,512]{2,1,0:T(8,128)(2,1)S(1)} %get-tuple-element.96), channel_id=1, source_target_pairs={{4,8},{8,4},{5,9},{9,5},{6,10},{10,6},{7,11},{11,7},{12,16},{16,12... | collective-permute-start | bytes 1572872 | tf_op jit(solution)/shard_map/ppermute | solution.py:376
  92.1 6.4 %collective-permute-done.16.refs_4_ = bf16[8,64,512]{2,1,0:T(8,128)(2,1)S(1)} collective-permute-done((bf16[8,64,512]{2,1,0:T(8,128)(2,1)S(1)}, bf16[8,64,512]{2,1,0:T(8,128)(2,1)S(1)}, u32[]{:S(2)}, u32[]{:S(2)}) %collective-permute-start.16) | collective-permute-done | bytes 524320 | tf_op jit(solution)/shard_map/ppermute | solution.py:376
  98.5 5.5 %collective-permute-done.17.refs_5_ = bf16[8,64,512]{2,1,0:T(8,128)(2,1)S(1)} collective-permute-done((bf16[8,64,512]{2,1,0:T(8,128)(2,1)S(1)}, bf16[8,64,512]{2,1,0:T(8,128)(2,1)S(1)}, u32[]{:S(2)}, u32[]{:S(2)}) %collective-permute-start.17) | collective-permute-done | bytes 524320 | tf_op jit(solution)/shard_map/ppermute | solution.py:376
  104.0 3.0 %couple_axial.3 = (bf16[2,8,64,128]{3,2,1,0:T(8,128)(2,1)S(1)}, bf16[2,8,64,128]{3,2,1,0:T(8,128)(2,1)S(1)}, bf16[2,8,64,128]{3,2,1,0:T(8,128)(2,1)S(1)}, bf16[2,8,64,128]{3,2,1,0:T(8,128)(2,1)S(1)}) custom-call(s32[9]{0:T(128)S(1)} %pad_add_fusion.order_ref, bf16[8,64,512]{2,1,0:T(8,128)(2,1)S(1)} %get-tuple-element.87.refs_0_, ...), custom_call_target="tpu_custom_call" | custom-call | flops 1073741824 | bytes 7471140 | tf_op jit(solution)/shard_map/couple_axial/pallas_call | solution.py:32
  107.0 0.2 collective-permute-start.23
  107.1 1.6 %collective-permute-start.24 = (bf16[2,8,64,128]{3,2,1,0:T(8,128)(2,1)S(1)}, bf16[2,8,64,128]{3,2,1,0:T(8,128)(2,1)S(1)}, u32[]{:S(2)}, u32[]{:S(2)}) collective-permute-start(bf16[2,8,64,128]{3,2,1,0:T(8,128)(2,1)S(1)} %get-tuple-element.107), channel_id=1, source_target_pairs={{0,2},{1,3},{2,0},{3,1},{4,6},{5,7},{6,4},{7,5},{8,10},{9,11},{10,... | collective-permute-start | bytes 786440 | tf_op jit(solution)/shard_map/ppermute | solution.py:352
  108.7 2.0 %collective-permute-start.25 = (bf16[2,8,64,128]{3,2,1,0:T(8,128)(2,1)S(1)}, bf16[2,8,64,128]{3,2,1,0:T(8,128)(2,1)S(1)}, u32[]{:S(2)}, u32[]{:S(2)}) collective-permute-start(bf16[2,8,64,128]{3,2,1,0:T(8,128)(2,1)S(1)} %get-tuple-element.108), channel_id=1, source_target_pairs={{0,3},{1,2},{2,1},{3,0},{4,7},{5,6},{6,5},{7,4},{8,11},{9,10},{10,... | collective-permute-start | bytes 786440 | tf_op jit(solution)/shard_map/ppermute | solution.py:352
  110.7 3.0 %couple_axial.2 = (bf16[2,8,64,128]{3,2,1,0:T(8,128)(2,1)S(1)}, bf16[2,8,64,128]{3,2,1,0:T(8,128)(2,1)S(1)}, bf16[2,8,64,128]{3,2,1,0:T(8,128)(2,1)S(1)}, bf16[2,8,64,128]{3,2,1,0:T(8,128)(2,1)S(1)}) custom-call(s32[9]{0:T(128)S(1)} %pad_add_fusion.order_ref, bf16[8,64,512]{2,1,0:T(8,128)(2,1)S(1)} %get-tuple-element.87.refs_0_, ...), custom_call_target="tpu_custom_call" | custom-call | flops 1073741824 | bytes 7471140 | tf_op jit(solution)/shard_map/couple_axial/pallas_call | solution.py:32
  113.7 0.1 collective-permute-start.20
  113.8 1.4 %collective-permute-start.21 = (bf16[2,8,64,128]{3,2,1,0:T(8,128)(2,1)S(1)}, bf16[2,8,64,128]{3,2,1,0:T(8,128)(2,1)S(1)}, u32[]{:S(2)}, u32[]{:S(2)}) collective-permute-start(bf16[2,8,64,128]{3,2,1,0:T(8,128)(2,1)S(1)} %get-tuple-element.102), channel_id=1, source_target_pairs={{0,2},{1,3},{2,0},{3,1},{4,6},{5,7},{6,4},{7,5},{8,10},{9,11},{10,... | collective-permute-start | bytes 786440 | tf_op jit(solution)/shard_map/ppermute | solution.py:352
  115.1 0.0 collective-permute-done.23.refs_1_
  115.1 2.3 %collective-permute-start.22 = (bf16[2,8,64,128]{3,2,1,0:T(8,128)(2,1)S(1)}, bf16[2,8,64,128]{3,2,1,0:T(8,128)(2,1)S(1)}, u32[]{:S(2)}, u32[]{:S(2)}) collective-permute-start(bf16[2,8,64,128]{3,2,1,0:T(8,128)(2,1)S(1)} %get-tuple-element.103), channel_id=1, source_target_pairs={{0,3},{1,2},{2,1},{3,0},{4,7},{5,6},{6,5},{7,4},{8,11},{9,10},{10,... | collective-permute-start | bytes 786440 | tf_op jit(solution)/shard_map/ppermute | solution.py:352
  117.4 5.7 %collective-permute-done.25.refs_3_ = bf16[2,8,64,128]{3,2,1,0:T(8,128)(2,1)S(1)} collective-permute-done((bf16[2,8,64,128]{3,2,1,0:T(8,128)(2,1)S(1)}, bf16[2,8,64,128]{3,2,1,0:T(8,128)(2,1)S(1)}, u32[]{:S(2)}, u32[]{:S(2)}) %collective-permute-start.25) | collective-permute-done | bytes 262176 | tf_op jit(solution)/shard_map/ppermute | solution.py:352
  123.1 1.4 %radial_last.2.refs_5_ = bf16[4,8,256,128]{3,2,1,0:T(8,128)(2,1)} custom-call(bf16[2,8,64,128]{3,2,1,0:T(8,128)(2,1)S(1)} %get-tuple-element.105.refs_0_, bf16[2,8,64,128]{3,2,1,0:T(8,128)(2,1)S(1)} %collective-permute-done.23.refs_1_, bf16[2,8,64,128]{3,2,1,0:T(8,128)(2,1)S(1)} %collective-permute-done.24.refs_2_, ...), custom_call_target="tpu_custom_call" | custom-call | flops 268435456 | bytes 2097152 | tf_op jit(solution)/shard_map/radial_last/pallas_call | solution.py:259
  124.6 0.0 collective-permute-done.20.refs_1_
  124.6 2.8 %collective-permute-done.21.refs_2_ = bf16[2,8,64,128]{3,2,1,0:T(8,128)(2,1)S(1)} collective-permute-done((bf16[2,8,64,128]{3,2,1,0:T(8,128)(2,1)S(1)}, bf16[2,8,64,128]{3,2,1,0:T(8,128)(2,1)S(1)}, u32[]{:S(2)}, u32[]{:S(2)}) %collective-permute-start.21) | collective-permute-done | bytes 262176 | tf_op jit(solution)/shard_map/ppermute | solution.py:352
  127.4 6.2 %collective-permute-done.22.refs_3_ = bf16[2,8,64,128]{3,2,1,0:T(8,128)(2,1)S(1)} collective-permute-done((bf16[2,8,64,128]{3,2,1,0:T(8,128)(2,1)S(1)}, bf16[2,8,64,128]{3,2,1,0:T(8,128)(2,1)S(1)}, u32[]{:S(2)}, u32[]{:S(2)}) %collective-permute-start.22) | collective-permute-done | bytes 262176 | tf_op jit(solution)/shard_map/ppermute | solution.py:352
  133.5 1.4 %radial_last.3 = bf16[4,8,256,128]{3,2,1,0:T(8,128)(2,1)} custom-call(bf16[2,8,64,128]{3,2,1,0:T(8,128)(2,1)S(1)} %get-tuple-element.100.refs_0_, bf16[2,8,64,128]{3,2,1,0:T(8,128)(2,1)S(1)} %collective-permute-done.20.refs_1_, bf16[2,8,64,128]{3,2,1,0:T(8,128)(2,1)S(1)} %collective-permute-done.21.refs_2_, ...), custom_call_target="tpu_custom_call", output_to_operand_aliasing={{}: (5, {})} | custom-call | flops 268435456 | bytes 2097152 | tf_op jit(solution)/shard_map/radial_last/pallas_call | solution.py:259
  (17 shorter events, 0.0 us)
Async XLA Ops:
  0.1 1.6 %copy-start = (bf16[4,8,64,512]{3,2,1,0:T(8,128)(2,1)S(1)}, bf16[4,8,64,512]{3,2,1,0:T(8,128)(2,1)}, u32[]{:S(2)}) copy-start(bf16[4,8,64,512]{3,2,1,0:T(8,128)(2,1)} %refs_3_.3) | copy-start | bytes 6291460
  2.6 14.2 %collective-permute-start = (bf16[2,8,64,128]{3,2,1,0:T(8,128)(2,1)S(1)}, bf16[2,8,64,128]{3,2,1,0:T(8,128)(2,1)S(1)}, u32[]{:S(2)}, u32[]{:S(2)}) collective-permute-start(bf16[2,8,64,128]{3,2,1,0:T(8,128)(2,1)S(1)} %get-tuple-element.62), channel_id=1, source_target_pairs={{0,2},{1,3},{2,0},{3,1},{4,6},{5,7},{6,4},{7,5},{8,10},{9,11},{10,... | collective-permute-start | bytes 786440 | tf_op jit(solution)/shard_map/ppermute | solution.py:352
  6.3 14.2 %collective-permute-start.1 = (bf16[2,8,64,128]{3,2,1,0:T(8,128)(2,1)S(1)}, bf16[2,8,64,128]{3,2,1,0:T(8,128)(2,1)S(1)}, u32[]{:S(2)}, u32[]{:S(2)}) collective-permute-start(bf16[2,8,64,128]{3,2,1,0:T(8,128)(2,1)S(1)} %get-tuple-element.65), channel_id=1, source_target_pairs={{0,1},{1,0},{2,3},{3,2},{4,5},{5,4},{6,7},{7,6},{8,9},{9,8},{10,11... | collective-permute-start | bytes 786440 | tf_op jit(solution)/shard_map/ppermute | solution.py:352
  7.2 2.9 %copy-start.1 = (bf16[4,256,256]{2,1,0:T(8,128)(2,1)S(1)}, bf16[4,256,256]{2,1,0:T(8,128)(2,1)}, u32[]{:S(2)}) copy-start(bf16[4,256,256]{2,1,0:T(8,128)(2,1)} %rad_ref.1) | copy-start | bytes 1572868
  7.2 2.9 %copy-start.2 = (f32[4,512]{1,0:T(4,128)S(1)}, f32[4,512]{1,0:T(4,128)}, u32[]{:S(2)}) copy-start(f32[4,512]{1,0:T(4,128)} %damp_ref.1) | copy-start | bytes 24580
  7.2 2.9 %copy-start.3 = (f32[8,8]{1,0:T(8,128)S(1)}, f32[8,8]{1,0:T(8,128)}, u32[]{:S(2)}) copy-start(f32[8,8]{1,0:T(8,128)} %one_ref.1) | copy-start | bytes 772
  7.2 3.0 %copy-start.4 = (f32[8,8]{1,0:T(8,128)S(1)}, f32[8,8]{1,0:T(8,128)}, u32[]{:S(2)}) copy-start(f32[8,8]{1,0:T(8,128)} %two_ref.1) | copy-start | bytes 772
  7.3 3.0 %copy-start.5 = (s32[4]{0:T(128)S(1)}, s32[4]{0:T(128)}, u32[]{:S(2)}) copy-start(s32[4]{0:T(128)} %len_ref.1) | copy-start | bytes 52
  7.3 3.0 %copy-start.6 = (bf16[512,512]{1,0:T(8,128)(2,1)S(1)}, bf16[512,512]{1,0:T(8,128)(2,1)}, u32[]{:S(2)}) copy-start(bf16[512,512]{1,0:T(8,128)(2,1)} %constant.51.clone.q_ref) | copy-start | bytes 1572868
  7.3 13.2 %collective-permute-start.2 = (bf16[2,8,64,128]{3,2,1,0:T(8,128)(2,1)S(1)}, bf16[2,8,64,128]{3,2,1,0:T(8,128)(2,1)S(1)}, u32[]{:S(2)}, u32[]{:S(2)}) collective-permute-start(bf16[2,8,64,128]{3,2,1,0:T(8,128)(2,1)S(1)} %get-tuple-element.67), channel_id=1, source_target_pairs={{0,3},{1,2},{2,1},{3,0},{4,7},{5,6},{6,5},{7,4},{8,11},{9,10},{10,... | collective-permute-start | bytes 786440 | tf_op jit(solution)/shard_map/ppermute | solution.py:352
  16.8 13.7 %collective-permute-start.3 = (bf16[2,8,64,128]{3,2,1,0:T(8,128)(2,1)S(1)}, bf16[2,8,64,128]{3,2,1,0:T(8,128)(2,1)S(1)}, u32[]{:S(2)}, u32[]{:S(2)}) collective-permute-start(bf16[2,8,64,128]{3,2,1,0:T(8,128)(2,1)S(1)} %get-tuple-element.70), channel_id=1, source_target_pairs={{0,1},{1,0},{2,3},{3,2},{4,5},{5,4},{6,7},{7,6},{8,9},{9,8},{10,11... | collective-permute-start | bytes 786440 | tf_op jit(solution)/shard_map/ppermute | solution.py:352
  17.3 13.2 %collective-permute-start.4 = (bf16[2,8,64,128]{3,2,1,0:T(8,128)(2,1)S(1)}, bf16[2,8,64,128]{3,2,1,0:T(8,128)(2,1)S(1)}, u32[]{:S(2)}, u32[]{:S(2)}) collective-permute-start(bf16[2,8,64,128]{3,2,1,0:T(8,128)(2,1)S(1)} %get-tuple-element.71), channel_id=1, source_target_pairs={{0,2},{1,3},{2,0},{3,1},{4,6},{5,7},{6,4},{7,5},{8,10},{9,11},{10,... | collective-permute-start | bytes 786440 | tf_op jit(solution)/shard_map/ppermute | solution.py:352
  18.3 17.5 %collective-permute-start.5 = (bf16[2,8,64,128]{3,2,1,0:T(8,128)(2,1)S(1)}, bf16[2,8,64,128]{3,2,1,0:T(8,128)(2,1)S(1)}, u32[]{:S(2)}, u32[]{:S(2)}) collective-permute-start(bf16[2,8,64,128]{3,2,1,0:T(8,128)(2,1)S(1)} %get-tuple-element.72), channel_id=1, source_target_pairs={{0,3},{1,2},{2,1},{3,0},{4,7},{5,6},{6,5},{7,4},{8,11},{9,10},{10,... | collective-permute-start | bytes 786440 | tf_op jit(solution)/shard_map/ppermute | solution.py:352
  21.2 26.0 %collective-permute-start.6 = (bf16[8,256,128]{2,1,0:T(8,128)(2,1)S(1)}, bf16[8,256,128]{2,1,0:T(8,128)(2,1)S(1)}, u32[]{:S(2)}, u32[]{:S(2)}) collective-permute-start(bf16[8,256,128]{2,1,0:T(8,128)(2,1)S(1)} %get-tuple-element.76), channel_id=1, source_target_pairs={{0,4},{4,0},{1,5},{5,1},{2,6},{6,2},{3,7},{7,3},{8,12},{12,8},{9,1... | collective-permute-start | bytes 1572872 | tf_op jit(solution)/shard_map/ppermute | solution.py:376
  21.3 26.0 %collective-permute-start.7 = (bf16[8,256,128]{2,1,0:T(8,128)(2,1)S(1)}, bf16[8,256,128]{2,1,0:T(8,128)(2,1)S(1)}, u32[]{:S(2)}, u32[]{:S(2)}) collective-permute-start(bf16[8,256,128]{2,1,0:T(8,128)(2,1)S(1)} %get-tuple-element.77), channel_id=1, source_target_pairs={{4,8},{8,4},{5,9},{9,5},{6,10},{10,6},{7,11},{11,7},{12,16},{16,12... | collective-permute-start | bytes 1572872 | tf_op jit(solution)/shard_map/ppermute | solution.py:376
  36.5 16.4 %collective-permute-start.8 = (bf16[8,256,128]{2,1,0:T(8,128)(2,1)S(1)}, bf16[8,256,128]{2,1,0:T(8,128)(2,1)S(1)}, u32[]{:S(2)}, u32[]{:S(2)}) collective-permute-start(bf16[8,256,128]{2,1,0:T(8,128)(2,1)S(1)} %get-tuple-element.78), channel_id=1, source_target_pairs={{0,4},{4,0},{1,5},{5,1},{2,6},{6,2},{3,7},{7,3},{8,12},{12,8},{9,1... | collective-permute-start | bytes 1572872 | tf_op jit(solution)/shard_map/ppermute | solution.py:376
  36.6 22.7 %collective-permute-start.9 = (bf16[8,256,128]{2,1,0:T(8,128)(2,1)S(1)}, bf16[8,256,128]{2,1,0:T(8,128)(2,1)S(1)}, u32[]{:S(2)}, u32[]{:S(2)}) collective-permute-start(bf16[8,256,128]{2,1,0:T(8,128)(2,1)S(1)} %get-tuple-element.79), channel_id=1, source_target_pairs={{4,8},{8,4},{5,9},{9,5},{6,10},{10,6},{7,11},{11,7},{12,16},{16,12... | collective-permute-start | bytes 1572872 | tf_op jit(solution)/shard_map/ppermute | solution.py:376
  49.2 14.6 %collective-permute-start.13 = (bf16[2,8,64,128]{3,2,1,0:T(8,128)(2,1)S(1)}, bf16[2,8,64,128]{3,2,1,0:T(8,128)(2,1)S(1)}, u32[]{:S(2)}, u32[]{:S(2)}) collective-permute-start(bf16[2,8,64,128]{3,2,1,0:T(8,128)(2,1)S(1)} %get-tuple-element.89), channel_id=1, source_target_pairs={{0,1},{1,0},{2,3},{3,2},{4,5},{5,4},{6,7},{7,6},{8,9},{9,8},{10,11... | collective-permute-start | bytes 786440 | tf_op jit(solution)/shard_map/ppermute | solution.py:352
  49.5 16.0 %collective-permute-start.14 = (bf16[2,8,64,128]{3,2,1,0:T(8,128)(2,1)S(1)}, bf16[2,8,64,128]{3,2,1,0:T(8,128)(2,1)S(1)}, u32[]{:S(2)}, u32[]{:S(2)}) collective-permute-start(bf16[2,8,64,128]{3,2,1,0:T(8,128)(2,1)S(1)} %get-tuple-element.90), channel_id=1, source_target_pairs={{0,2},{1,3},{2,0},{3,1},{4,6},{5,7},{6,4},{7,5},{8,10},{9,11},{10,... | collective-permute-start | bytes 786440 | tf_op jit(solution)/shard_map/ppermute | solution.py:352
  51.3 15.6 %collective-permute-start.15 = (bf16[2,8,64,128]{3,2,1,0:T(8,128)(2,1)S(1)}, bf16[2,8,64,128]{3,2,1,0:T(8,128)(2,1)S(1)}, u32[]{:S(2)}, u32[]{:S(2)}) collective-permute-start(bf16[2,8,64,128]{3,2,1,0:T(8,128)(2,1)S(1)} %get-tuple-element.91), channel_id=1, source_target_pairs={{0,3},{1,2},{2,1},{3,0},{4,7},{5,6},{6,5},{7,4},{8,11},{9,10},{10,... | collective-permute-start | bytes 786440 | tf_op jit(solution)/shard_map/ppermute | solution.py:352
  61.4 12.8 %collective-permute-start.10 = (bf16[2,8,64,128]{3,2,1,0:T(8,128)(2,1)S(1)}, bf16[2,8,64,128]{3,2,1,0:T(8,128)(2,1)S(1)}, u32[]{:S(2)}, u32[]{:S(2)}) collective-permute-start(bf16[2,8,64,128]{3,2,1,0:T(8,128)(2,1)S(1)} %get-tuple-element.83), channel_id=1, source_target_pairs={{0,1},{1,0},{2,3},{3,2},{4,5},{5,4},{6,7},{7,6},{8,9},{9,8},{10,11... | collective-permute-start | bytes 786440 | tf_op jit(solution)/shard_map/ppermute | solution.py:352
  62.3 11.9 %collective-permute-start.11 = (bf16[2,8,64,128]{3,2,1,0:T(8,128)(2,1)S(1)}, bf16[2,8,64,128]{3,2,1,0:T(8,128)(2,1)S(1)}, u32[]{:S(2)}, u32[]{:S(2)}) collective-permute-start(bf16[2,8,64,128]{3,2,1,0:T(8,128)(2,1)S(1)} %get-tuple-element.84), channel_id=1, source_target_pairs={{0,2},{1,3},{2,0},{3,1},{4,6},{5,7},{6,4},{7,5},{8,10},{9,11},{10,... | collective-permute-start | bytes 786440 | tf_op jit(solution)/shard_map/ppermute | solution.py:352
  63.8 19.9 %collective-permute-start.12 = (bf16[2,8,64,128]{3,2,1,0:T(8,128)(2,1)S(1)}, bf16[2,8,64,128]{3,2,1,0:T(8,128)(2,1)S(1)}, u32[]{:S(2)}, u32[]{:S(2)}) collective-permute-start(bf16[2,8,64,128]{3,2,1,0:T(8,128)(2,1)S(1)} %get-tuple-element.85), channel_id=1, source_target_pairs={{0,3},{1,2},{2,1},{3,0},{4,7},{5,6},{6,5},{7,4},{8,11},{9,10},{10,... | collective-permute-start | bytes 786440 | tf_op jit(solution)/shard_map/ppermute | solution.py:352
  68.2 24.0 %collective-permute-start.18 = (bf16[8,64,512]{2,1,0:T(8,128)(2,1)S(1)}, bf16[8,64,512]{2,1,0:T(8,128)(2,1)S(1)}, u32[]{:S(2)}, u32[]{:S(2)}) collective-permute-start(bf16[8,64,512]{2,1,0:T(8,128)(2,1)S(1)} %get-tuple-element.97), channel_id=1, source_target_pairs={{0,4},{4,0},{1,5},{5,1},{2,6},{6,2},{3,7},{7,3},{8,12},{12,8},{9,1... | collective-permute-start | bytes 1572872 | tf_op jit(solution)/shard_map/ppermute | solution.py:376
  68.3 23.9 %collective-permute-start.19 = (bf16[8,64,512]{2,1,0:T(8,128)(2,1)S(1)}, bf16[8,64,512]{2,1,0:T(8,128)(2,1)S(1)}, u32[]{:S(2)}, u32[]{:S(2)}) collective-permute-start(bf16[8,64,512]{2,1,0:T(8,128)(2,1)S(1)} %get-tuple-element.98), channel_id=1, source_target_pairs={{4,8},{8,4},{5,9},{9,5},{6,10},{10,6},{7,11},{11,7},{12,16},{16,12... | collective-permute-start | bytes 1572872 | tf_op jit(solution)/shard_map/ppermute | solution.py:376
  85.0 13.5 %collective-permute-start.16 = (bf16[8,64,512]{2,1,0:T(8,128)(2,1)S(1)}, bf16[8,64,512]{2,1,0:T(8,128)(2,1)S(1)}, u32[]{:S(2)}, u32[]{:S(2)}) collective-permute-start(bf16[8,64,512]{2,1,0:T(8,128)(2,1)S(1)} %get-tuple-element.95), channel_id=1, source_target_pairs={{0,4},{4,0},{1,5},{5,1},{2,6},{6,2},{3,7},{7,3},{8,12},{12,8},{9,1... | collective-permute-start | bytes 1572872 | tf_op jit(solution)/shard_map/ppermute | solution.py:376
  85.1 18.8 %collective-permute-start.17 = (bf16[8,64,512]{2,1,0:T(8,128)(2,1)S(1)}, bf16[8,64,512]{2,1,0:T(8,128)(2,1)S(1)}, u32[]{:S(2)}, u32[]{:S(2)}) collective-permute-start(bf16[8,64,512]{2,1,0:T(8,128)(2,1)S(1)} %get-tuple-element.96), channel_id=1, source_target_pairs={{4,8},{8,4},{5,9},{9,5},{6,10},{10,6},{7,11},{11,7},{12,16},{16,12... | collective-permute-start | bytes 1572872 | tf_op jit(solution)/shard_map/ppermute | solution.py:376
  107.0 8.2 %collective-permute-start.23 = (bf16[2,8,64,128]{3,2,1,0:T(8,128)(2,1)S(1)}, bf16[2,8,64,128]{3,2,1,0:T(8,128)(2,1)S(1)}, u32[]{:S(2)}, u32[]{:S(2)}) collective-permute-start(bf16[2,8,64,128]{3,2,1,0:T(8,128)(2,1)S(1)} %get-tuple-element.106), channel_id=1, source_target_pairs={{0,1},{1,0},{2,3},{3,2},{4,5},{5,4},{6,7},{7,6},{8,9},{9,8},{10,11... | collective-permute-start | bytes 786440 | tf_op jit(solution)/shard_map/ppermute | solution.py:352
  107.1 10.3 %collective-permute-start.24 = (bf16[2,8,64,128]{3,2,1,0:T(8,128)(2,1)S(1)}, bf16[2,8,64,128]{3,2,1,0:T(8,128)(2,1)S(1)}, u32[]{:S(2)}, u32[]{:S(2)}) collective-permute-start(bf16[2,8,64,128]{3,2,1,0:T(8,128)(2,1)S(1)} %get-tuple-element.107), channel_id=1, source_target_pairs={{0,2},{1,3},{2,0},{3,1},{4,6},{5,7},{6,4},{7,5},{8,10},{9,11},{10,... | collective-permute-start | bytes 786440 | tf_op jit(solution)/shard_map/ppermute | solution.py:352
  108.7 14.4 %collective-permute-start.25 = (bf16[2,8,64,128]{3,2,1,0:T(8,128)(2,1)S(1)}, bf16[2,8,64,128]{3,2,1,0:T(8,128)(2,1)S(1)}, u32[]{:S(2)}, u32[]{:S(2)}) collective-permute-start(bf16[2,8,64,128]{3,2,1,0:T(8,128)(2,1)S(1)} %get-tuple-element.108), channel_id=1, source_target_pairs={{0,3},{1,2},{2,1},{3,0},{4,7},{5,6},{6,5},{7,4},{8,11},{9,10},{10,... | collective-permute-start | bytes 786440 | tf_op jit(solution)/shard_map/ppermute | solution.py:352
  113.7 10.9 %collective-permute-start.20 = (bf16[2,8,64,128]{3,2,1,0:T(8,128)(2,1)S(1)}, bf16[2,8,64,128]{3,2,1,0:T(8,128)(2,1)S(1)}, u32[]{:S(2)}, u32[]{:S(2)}) collective-permute-start(bf16[2,8,64,128]{3,2,1,0:T(8,128)(2,1)S(1)} %get-tuple-element.101), channel_id=1, source_target_pairs={{0,1},{1,0},{2,3},{3,2},{4,5},{5,4},{6,7},{7,6},{8,9},{9,8},{10,11... | collective-permute-start | bytes 786440 | tf_op jit(solution)/shard_map/ppermute | solution.py:352
  113.8 13.6 %collective-permute-start.21 = (bf16[2,8,64,128]{3,2,1,0:T(8,128)(2,1)S(1)}, bf16[2,8,64,128]{3,2,1,0:T(8,128)(2,1)S(1)}, u32[]{:S(2)}, u32[]{:S(2)}) collective-permute-start(bf16[2,8,64,128]{3,2,1,0:T(8,128)(2,1)S(1)} %get-tuple-element.102), channel_id=1, source_target_pairs={{0,2},{1,3},{2,0},{3,1},{4,6},{5,7},{6,4},{7,5},{8,10},{9,11},{10,... | collective-permute-start | bytes 786440 | tf_op jit(solution)/shard_map/ppermute | solution.py:352
  115.1 18.4 %collective-permute-start.22 = (bf16[2,8,64,128]{3,2,1,0:T(8,128)(2,1)S(1)}, bf16[2,8,64,128]{3,2,1,0:T(8,128)(2,1)S(1)}, u32[]{:S(2)}, u32[]{:S(2)}) collective-permute-start(bf16[2,8,64,128]{3,2,1,0:T(8,128)(2,1)S(1)} %get-tuple-element.103), channel_id=1, source_target_pairs={{0,3},{1,2},{2,1},{3,0},{4,7},{5,6},{6,5},{7,4},{8,11},{9,10},{10,... | collective-permute-start | bytes 786440 | tf_op jit(solution)/shard_map/ppermute | solution.py:352

commit v3 on v2

--- a/solution.py
+++ b/solution.py
@@ -245,11 +245,12 @@
     radial_one([p.at[0] for p in refs[:peers]], refs[peers][0], refs[-1].at[0])
 
 
-def radial_last(peers, first, total, pieces, matrices, partial_result):
+def radial_last(peers, modes, total, pieces, matrices, partial_result):
     count, comp, rows, block = pieces[0].shape
+    first, step = modes[0], modes[1] - modes[0]
     nr = rows * peers
     specs = [pl.BlockSpec((1, comp, rows, block), lambda i: (i, 0, 0, 0))] * peers
-    specs.append(pl.BlockSpec((1, nr, nr), lambda i: (first + i, 0, 0)))
+    specs.append(pl.BlockSpec((1, nr, nr), lambda i: (first + step * i, 0, 0)))
     args = [*pieces, matrices]
     aliases = {}
     if partial_result is not None:
@@ -261,7 +262,7 @@
         grid=(count,),
         out_shape=shape(total, comp, nr, block),
         in_specs=specs,
-        out_specs=pl.BlockSpec((1, comp, nr, block), lambda i: (first + i, 0, 0, 0)),
+        out_specs=pl.BlockSpec((1, comp, nr, block), lambda i: (first + step * i, 0, 0, 0)),
         input_output_aliases=aliases,
         compiler_params=pltpu.CompilerParams(vmem_limit_bytes=VMEM_LIMIT),
         cost_estimate=pl.CostEstimate(
@@ -398,17 +399,15 @@
     own = own[:3] + own[5:]
     pieces_inner = swap(couple_radial(peers, order, inner, own, near, weights, in_r))
     pieces_outer = swap(couple_radial(peers, order, outer, own, near + far, weights, in_r))
-    low, high, *sent = axial(peers, order, inner, pieces_inner, in_m)
-    far = exchange(sent)
-    first, final, *sent = axial(peers, order, outer, pieces_outer, in_m)
-    near = exchange(sent)
+    low, high, *far = axial(peers, order, inner, pieces_inner, in_m)
+    first, final, *near = axial(peers, order, outer, pieces_outer, in_m)
+    near, far = lax.optimization_barrier((near, far))
+    near, far = exchange(near), exchange(far)
     own = [first, low, high, final]
-
-    halves = (modes[: count // 2], modes[count // 2 :])
-    pieces = [swap(couple_axial(peers, order, half, own, near + far, weights, out_m)) for half in halves]
-    result = None
-    for half, p in zip(halves, pieces):
-        result = radial_last(peers, half[0], count, p, out_r, result)
+    pieces_inner = swap(couple_axial(peers, order, inner, own, near, weights, out_m))
+    pieces_outer = swap(couple_axial(peers, order, outer, own, near + far, weights, out_m))
+    result = radial_last(peers, inner, count, pieces_inner, out_r, None)
+    result = radial_last(peers, outer, count, pieces_outer, out_r, result)
     return result
 
 

time: 135 us -> 131 us (0.970)
  starting transfers between devices: 58.6 us -> 53.6 us
    ppermute x8, starting transfers between devices: 33.1 us -> 28 us  [exchange(): lax.ppermute(p, ('mode', 'pencil'), pair)]
    ppermute x8, waiting for transfers between devices: 18.2 us -> 22.5 us  [exchange(): lax.ppermute(p, ('mode', 'pencil'), pair)]
    ppermute x18, waiting for transfers between devices: 30.9 us -> 27.2 us  [swap(): lax.ppermute(pieces[k], 'pencil', [(i, i ^ k) for i in range(peers)])]
  transfers between devices with their start and end apart: 26 -> 26, of which waited for: 9 -> 11; matrix products, arithmetic and copies ran while one was open for 0% -> 0% of each run, Pallas kernels for 15% -> 17%
where the time goes in v3:
time: 131 us; the launch traced here: 130 us
  starting transfers between devices  53.6 us (41%)
  waiting for transfers between devices  49.7 us (38%)
  Pallas kernels  25.3 us (19%)
  local copies, waits for them, and re-layouts  1.62 us (1%)
    ppermute x8, starting transfers between devices, exchange(): lax.ppermute(p, ('mode', 'pencil'), pair)  28 us
    ppermute x18, waiting for transfers between devices, swap(): lax.ppermute(pieces[k], 'pencil', [(i, i ^ k) for i in range(peers)])  27.2 us
    ppermute x18, starting transfers between devices, swap(): lax.ppermute(pieces[k], 'pencil', [(i, i ^ k) for i in range(peers)])  25.6 us
    ppermute x8, waiting for transfers between devices, exchange(): lax.ppermute(p, ('mode', 'pencil'), pair)  22.5 us
    pallas_call x9, Pallas kernels, call(): pl.pallas_call(kernel, out_shape=outs, in_specs=[pl.BlockSpec(memory_spac...  20.6 us
    pallas_call x2, Pallas kernels, radial_last(): pl.pallas_call(functools.partial(radial_last_kernel, peers), grid=(count,...  2.84 us
  transfers between devices with their start and end apart: 26, of which 11 were waited for; matrix products, arithmetic and copies ran while one was open for 0% of the time, Pallas kernels for 17%

profile of v3, /device:TPU:1, one launch (start us, length us, event | category | flops | bytes accessed | tf_op | source)
XLA Modules:
  0.0 130.5 jit_solution(12471364094321778764)
XLA Ops:
  0.0 0.1 pad_add_fusion.order_ref
  0.1 1.6 %copy-done = bf16[4,8,64,512]{3,2,1,0:T(8,128)(2,1)S(1)} copy-done((bf16[4,8,64,512]{3,2,1,0:T(8,128)(2,1)S(1)}, bf16[4,8,64,512]{3,2,1,0:T(8,128)(2,1)}, u32[]{:S(2)}) %copy-start) | copy-done | bytes 2097176
  1.7 0.9 split.3
  2.6 3.7 %collective-permute-start = (bf16[2,8,64,128]{3,2,1,0:T(8,128)(2,1)S(1)}, bf16[2,8,64,128]{3,2,1,0:T(8,128)(2,1)S(1)}, u32[]{:S(2)}, u32[]{:S(2)}) collective-permute-start(bf16[2,8,64,128]{3,2,1,0:T(8,128)(2,1)S(1)} %get-tuple-element.66), channel_id=1, source_target_pairs={{0,2},{1,3},{2,0},{3,1},{4,6},{5,7},{6,4},{7,5},{8,10},{9,11},{10,... | collective-permute-start | bytes 786440 | tf_op jit(solution)/shard_map/ppermute | solution.py:353
  6.3 1.0 collective-permute-start.1
  7.3 0.0 copy-start.5
  7.3 0.0 copy-start.6
  7.3 1.9 %collective-permute-start.2 = (bf16[2,8,64,128]{3,2,1,0:T(8,128)(2,1)S(1)}, bf16[2,8,64,128]{3,2,1,0:T(8,128)(2,1)S(1)}, u32[]{:S(2)}, u32[]{:S(2)}) collective-permute-start(bf16[2,8,64,128]{3,2,1,0:T(8,128)(2,1)S(1)} %get-tuple-element.71), channel_id=1, source_target_pairs={{0,3},{1,2},{2,1},{3,0},{4,7},{5,6},{6,5},{7,4},{8,11},{9,10},{10,... | collective-permute-start | bytes 786440 | tf_op jit(solution)/shard_map/ppermute | solution.py:353
  9.2 0.9 split.2
  10.2 6.6 %prepare.1 = (bf16[4,512,512]{2,1,0:T(8,128)(2,1)S(1)}, bf16[4,512,512]{2,1,0:T(8,128)(2,1)}, bf16[4,256,256]{2,1,0:T(8,128)(2,1)S(1)}, bf16[4,256,256]{2,1,0:T(8,128)(2,1)S(1)}, bf16[128,512]{1,0:T(8,128)(2,1)S(1)}) custom-call(s32[9]{0:T(128)S(1)} %pad_add_fusion.order_ref, s32[4]{0:T(128)S(1)} %copy-done.5, bf16[512,512]{1,0:T(8,128)(2,1)S(1)} %copy-done.6, ...), custom_call_target="tpu_custom_call" | custom-call | flops 4294967296 | bytes 6431284 | tf_op jit(solution)/shard_map/prepare/pallas_call | solution.py:32
  16.8 0.0 collective-permute-done.refs_2_
  16.8 0.5 collective-permute-start.3
  17.3 1.0 collective-permute-start.4
  18.3 2.1 %collective-permute-start.5 = (bf16[2,8,64,128]{3,2,1,0:T(8,128)(2,1)S(1)}, bf16[2,8,64,128]{3,2,1,0:T(8,128)(2,1)S(1)}, u32[]{:S(2)}, u32[]{:S(2)}) collective-permute-start(bf16[2,8,64,128]{3,2,1,0:T(8,128)(2,1)S(1)} %get-tuple-element.76), channel_id=1, source_target_pairs={{0,3},{1,2},{2,1},{3,0},{4,7},{5,6},{6,5},{7,4},{8,11},{9,10},{10,... | collective-permute-start | bytes 786440 | tf_op jit(solution)/shard_map/ppermute | solution.py:353
  20.5 0.0 collective-permute-done.1.refs_1_
  20.5 0.0 collective-permute-done.2.refs_3_
  20.5 0.7 assemble.2
  21.2 0.1 collective-permute-start.6
  21.3 9.2 %collective-permute-start.7 = (bf16[8,256,128]{2,1,0:T(8,128)(2,1)S(1)}, bf16[8,256,128]{2,1,0:T(8,128)(2,1)S(1)}, u32[]{:S(2)}, u32[]{:S(2)}) collective-permute-start(bf16[8,256,128]{2,1,0:T(8,128)(2,1)S(1)} %get-tuple-element.81), channel_id=1, source_target_pairs={{4,8},{8,4},{5,9},{9,5},{6,10},{10,6},{7,11},{11,7},{12,16},{16,12... | collective-permute-start | bytes 1572872 | tf_op jit(solution)/shard_map/ppermute | solution.py:377
  30.5 0.0 collective-permute-done.3.refs_1_
  30.5 0.0 collective-permute-done.4.refs_2_
  30.5 5.4 %collective-permute-done.5.refs_3_ = bf16[2,8,64,128]{3,2,1,0:T(8,128)(2,1)S(1)} collective-permute-done((bf16[2,8,64,128]{3,2,1,0:T(8,128)(2,1)S(1)}, bf16[2,8,64,128]{3,2,1,0:T(8,128)(2,1)S(1)}, u32[]{:S(2)}, u32[]{:S(2)}) %collective-permute-start.5) | collective-permute-done | bytes 262176 | tf_op jit(solution)/shard_map/ppermute | solution.py:353
  35.8 0.7 assemble.3
  36.5 0.1 collective-permute-start.8
  36.6 10.6 %collective-permute-start.9 = (bf16[8,256,128]{2,1,0:T(8,128)(2,1)S(1)}, bf16[8,256,128]{2,1,0:T(8,128)(2,1)S(1)}, u32[]{:S(2)}, u32[]{:S(2)}) collective-permute-start(bf16[8,256,128]{2,1,0:T(8,128)(2,1)S(1)} %get-tuple-element.83), channel_id=1, source_target_pairs={{4,8},{8,4},{5,9},{9,5},{6,10},{10,6},{7,11},{11,7},{12,16},{16,12... | collective-permute-start | bytes 1572872 | tf_op jit(solution)/shard_map/ppermute | solution.py:377
  47.2 0.0 collective-permute-done.6.refs_4_
  47.2 0.0 collective-permute-done.7.refs_5_
  47.2 2.0 %couple_radial.3 = (bf16[2,8,64,128]{3,2,1,0:T(8,128)(2,1)S(1)}, bf16[2,8,64,128]{3,2,1,0:T(8,128)(2,1)S(1)}, bf16[2,8,64,128]{3,2,1,0:T(8,128)(2,1)S(1)}, bf16[2,8,64,128]{3,2,1,0:T(8,128)(2,1)S(1)}) custom-call(s32[9]{0:T(128)S(1)} %pad_add_fusion.order_ref, bf16[8,256,128]{2,1,0:T(8,128)(2,1)S(1)} %get-tuple-element.72.refs_0_, ...), custom_call_target="tpu_custom_call" | custom-call | flops 805306368 | bytes 4849700 | tf_op jit(solution)/shard_map/couple_radial/pallas_call | solution.py:32
  49.2 0.3 collective-permute-start.13
  49.5 1.8 %collective-permute-start.14 = (bf16[2,8,64,128]{3,2,1,0:T(8,128)(2,1)S(1)}, bf16[2,8,64,128]{3,2,1,0:T(8,128)(2,1)S(1)}, u32[]{:S(2)}, u32[]{:S(2)}) collective-permute-start(bf16[2,8,64,128]{3,2,1,0:T(8,128)(2,1)S(1)} %get-tuple-element.94), channel_id=1, source_target_pairs={{0,2},{1,3},{2,0},{3,1},{4,6},{5,7},{6,4},{7,5},{8,10},{9,11},{10,... | collective-permute-start | bytes 786440 | tf_op jit(solution)/shard_map/ppermute | solution.py:353
  51.3 1.6 %collective-permute-start.15 = (bf16[2,8,64,128]{3,2,1,0:T(8,128)(2,1)S(1)}, bf16[2,8,64,128]{3,2,1,0:T(8,128)(2,1)S(1)}, u32[]{:S(2)}, u32[]{:S(2)}) collective-permute-start(bf16[2,8,64,128]{3,2,1,0:T(8,128)(2,1)S(1)} %get-tuple-element.95), channel_id=1, source_target_pairs={{0,3},{1,2},{2,1},{3,0},{4,7},{5,6},{6,5},{7,4},{8,11},{9,10},{10,... | collective-permute-start | bytes 786440 | tf_op jit(solution)/shard_map/ppermute | solution.py:353
  52.9 6.4 %collective-permute-done.9.refs_7_ = bf16[8,256,128]{2,1,0:T(8,128)(2,1)S(1)} collective-permute-done((bf16[8,256,128]{2,1,0:T(8,128)(2,1)S(1)}, bf16[8,256,128]{2,1,0:T(8,128)(2,1)S(1)}, u32[]{:S(2)}, u32[]{:S(2)}) %collective-permute-start.9) | collective-permute-done | bytes 524320 | tf_op jit(solution)/shard_map/ppermute | solution.py:377
  59.3 2.0 %couple_radial.2 = (bf16[2,8,64,128]{3,2,1,0:T(8,128)(2,1)S(1)}, bf16[2,8,64,128]{3,2,1,0:T(8,128)(2,1)S(1)}, bf16[2,8,64,128]{3,2,1,0:T(8,128)(2,1)S(1)}, bf16[2,8,64,128]{3,2,1,0:T(8,128)(2,1)S(1)}) custom-call(s32[9]{0:T(128)S(1)} %pad_add_fusion.order_ref, bf16[8,256,128]{2,1,0:T(8,128)(2,1)S(1)} %get-tuple-element.72.refs_0_, ...), custom_call_target="tpu_custom_call" | custom-call | flops 805306368 | bytes 5898276 | tf_op jit(solution)/shard_map/couple_radial/pallas_call | solution.py:32
  61.4 0.9 collective-permute-start.10
  62.3 1.5 %collective-permute-start.11 = (bf16[2,8,64,128]{3,2,1,0:T(8,128)(2,1)S(1)}, bf16[2,8,64,128]{3,2,1,0:T(8,128)(2,1)S(1)}, u32[]{:S(2)}, u32[]{:S(2)}) collective-permute-start(bf16[2,8,64,128]{3,2,1,0:T(8,128)(2,1)S(1)} %get-tuple-element.88), channel_id=1, source_target_pairs={{0,2},{1,3},{2,0},{3,1},{4,6},{5,7},{6,4},{7,5},{8,10},{9,11},{10,... | collective-permute-start | bytes 786440 | tf_op jit(solution)/shard_map/ppermute | solution.py:353
  63.8 0.0 collective-permute-done.13.refs_1_
  63.8 1.7 %collective-permute-start.12 = (bf16[2,8,64,128]{3,2,1,0:T(8,128)(2,1)S(1)}, bf16[2,8,64,128]{3,2,1,0:T(8,128)(2,1)S(1)}, u32[]{:S(2)}, u32[]{:S(2)}) collective-permute-start(bf16[2,8,64,128]{3,2,1,0:T(8,128)(2,1)S(1)} %get-tuple-element.89), channel_id=1, source_target_pairs={{0,3},{1,2},{2,1},{3,0},{4,7},{5,6},{6,5},{7,4},{8,11},{9,10},{10,... | collective-permute-start | bytes 786440 | tf_op jit(solution)/shard_map/ppermute | solution.py:353
  65.5 0.0 collective-permute-done.14.refs_2_
  65.5 1.3 %collective-permute-done.15.refs_3_ = bf16[2,8,64,128]{3,2,1,0:T(8,128)(2,1)S(1)} collective-permute-done((bf16[2,8,64,128]{3,2,1,0:T(8,128)(2,1)S(1)}, bf16[2,8,64,128]{3,2,1,0:T(8,128)(2,1)S(1)}, u32[]{:S(2)}, u32[]{:S(2)}) %collective-permute-start.15) | collective-permute-done | bytes 262176 | tf_op jit(solution)/shard_map/ppermute | solution.py:353
  66.8 1.3 %axial.3 = (bf16[8,64,512]{2,1,0:T(8,128)(2,1)S(1)}, bf16[8,64,512]{2,1,0:T(8,128)(2,1)S(1)}, bf16[8,64,512]{2,1,0:T(8,128)(2,1)S(1)}, bf16[8,64,512]{2,1,0:T(8,128)(2,1)S(1)}) custom-call(s32[9]{0:T(128)S(1)} %pad_add_fusion.order_ref, bf16[2,8,64,128]{3,2,1,0:T(8,128)(2,1)S(1)} %get-tuple-element.92.refs_0_, ...), custom_call_target="tpu_custom_call" | custom-call | flops 536870912 | bytes 5242916 | tf_op jit(solution)/shard_map/axial/pallas_call | solution.py:32
  68.2 4.0 %collective-permute-done.11.refs_2_ = bf16[2,8,64,128]{3,2,1,0:T(8,128)(2,1)S(1)} collective-permute-done((bf16[2,8,64,128]{3,2,1,0:T(8,128)(2,1)S(1)}, bf16[2,8,64,128]{3,2,1,0:T(8,128)(2,1)S(1)}, u32[]{:S(2)}, u32[]{:S(2)}) %collective-permute-start.11) | collective-permute-done | bytes 262176 | tf_op jit(solution)/shard_map/ppermute | solution.py:353
  72.2 5.6 %collective-permute-done.12.refs_3_ = bf16[2,8,64,128]{3,2,1,0:T(8,128)(2,1)S(1)} collective-permute-done((bf16[2,8,64,128]{3,2,1,0:T(8,128)(2,1)S(1)}, bf16[2,8,64,128]{3,2,1,0:T(8,128)(2,1)S(1)}, u32[]{:S(2)}, u32[]{:S(2)}) %collective-permute-start.12) | collective-permute-done | bytes 262176 | tf_op jit(solution)/shard_map/ppermute | solution.py:353
  77.8 1.3 %axial.2 = (bf16[8,64,512]{2,1,0:T(8,128)(2,1)S(1)}, bf16[8,64,512]{2,1,0:T(8,128)(2,1)S(1)}, bf16[8,64,512]{2,1,0:T(8,128)(2,1)S(1)}, bf16[8,64,512]{2,1,0:T(8,128)(2,1)S(1)}) custom-call(s32[9]{0:T(128)S(1)} %pad_add_fusion.order_ref, bf16[2,8,64,128]{3,2,1,0:T(8,128)(2,1)S(1)} %get-tuple-element.86.refs_0_, ...), custom_call_target="tpu_custom_call" | custom-call | flops 536870912 | bytes 5242916 | tf_op jit(solution)/shard_map/axial/pallas_call | solution.py:32
  79.1 0.1 collective-permute-start.16
  79.2 6.5 %collective-permute-start.17 = (bf16[8,64,512]{2,1,0:T(8,128)(2,1)S(1)}, bf16[8,64,512]{2,1,0:T(8,128)(2,1)S(1)}, u32[]{:S(2)}, u32[]{:S(2)}) collective-permute-start(bf16[8,64,512]{2,1,0:T(8,128)(2,1)S(1)} %get-tuple-element.104), channel_id=1, source_target_pairs={{4,8},{8,4},{5,9},{9,5},{6,10},{10,6},{7,11},{11,7},{12,16},{16,12... | collective-permute-start | bytes 1572872 | tf_op jit(solution)/shard_map/ppermute | solution.py:377
  85.8 0.0 collective-permute-start.18
  85.8 1.4 %collective-permute-start.19 = (bf16[8,64,512]{2,1,0:T(8,128)(2,1)S(1)}, bf16[8,64,512]{2,1,0:T(8,128)(2,1)S(1)}, u32[]{:S(2)}, u32[]{:S(2)}) collective-permute-start(bf16[8,64,512]{2,1,0:T(8,128)(2,1)S(1)} %get-tuple-element.106), channel_id=1, source_target_pairs={{4,8},{8,4},{5,9},{9,5},{6,10},{10,6},{7,11},{11,7},{12,16},{16,12... | collective-permute-start | bytes 1572872 | tf_op jit(solution)/shard_map/ppermute | solution.py:377
  87.2 5.2 %collective-permute-done.16.refs_4_ = bf16[8,64,512]{2,1,0:T(8,128)(2,1)S(1)} collective-permute-done((bf16[8,64,512]{2,1,0:T(8,128)(2,1)S(1)}, bf16[8,64,512]{2,1,0:T(8,128)(2,1)S(1)}, u32[]{:S(2)}, u32[]{:S(2)}) %collective-permute-start.16) | collective-permute-done | bytes 524320 | tf_op jit(solution)/shard_map/ppermute | solution.py:377
  92.3 6.0 %collective-permute-done.17.refs_5_ = bf16[8,64,512]{2,1,0:T(8,128)(2,1)S(1)} collective-permute-done((bf16[8,64,512]{2,1,0:T(8,128)(2,1)S(1)}, bf16[8,64,512]{2,1,0:T(8,128)(2,1)S(1)}, u32[]{:S(2)}, u32[]{:S(2)}) %collective-permute-start.17) | collective-permute-done | bytes 524320 | tf_op jit(solution)/shard_map/ppermute | solution.py:377
  98.4 3.0 %couple_axial.3 = (bf16[2,8,64,128]{3,2,1,0:T(8,128)(2,1)S(1)}, bf16[2,8,64,128]{3,2,1,0:T(8,128)(2,1)S(1)}, bf16[2,8,64,128]{3,2,1,0:T(8,128)(2,1)S(1)}, bf16[2,8,64,128]{3,2,1,0:T(8,128)(2,1)S(1)}) custom-call(s32[9]{0:T(128)S(1)} %pad_add_fusion.order_ref, bf16[8,64,512]{2,1,0:T(8,128)(2,1)S(1)} %get-tuple-element.91.refs_0_, ...), custom_call_target="tpu_custom_call" | custom-call | flops 1073741824 | bytes 6422564 | tf_op jit(solution)/shard_map/couple_axial/pallas_call | solution.py:32
  101.3 0.5 collective-permute-start.23
  101.8 1.3 collective-permute-start.24
  103.1 2.0 %collective-permute-start.25 = (bf16[2,8,64,128]{3,2,1,0:T(8,128)(2,1)S(1)}, bf16[2,8,64,128]{3,2,1,0:T(8,128)(2,1)S(1)}, u32[]{:S(2)}, u32[]{:S(2)}) collective-permute-start(bf16[2,8,64,128]{3,2,1,0:T(8,128)(2,1)S(1)} %get-tuple-element.116), channel_id=1, source_target_pairs={{0,3},{1,2},{2,1},{3,0},{4,7},{5,6},{6,5},{7,4},{8,11},{9,10},{10,... | collective-permute-start | bytes 786440 | tf_op jit(solution)/shard_map/ppermute | solution.py:353
  105.1 4.9 %collective-permute-done.19.refs_7_ = bf16[8,64,512]{2,1,0:T(8,128)(2,1)S(1)} collective-permute-done((bf16[8,64,512]{2,1,0:T(8,128)(2,1)S(1)}, bf16[8,64,512]{2,1,0:T(8,128)(2,1)S(1)}, u32[]{:S(2)}, u32[]{:S(2)}) %collective-permute-start.19) | collective-permute-done | bytes 524320 | tf_op jit(solution)/shard_map/ppermute | solution.py:377
  110.0 3.0 %couple_axial.2 = (bf16[2,8,64,128]{3,2,1,0:T(8,128)(2,1)S(1)}, bf16[2,8,64,128]{3,2,1,0:T(8,128)(2,1)S(1)}, bf16[2,8,64,128]{3,2,1,0:T(8,128)(2,1)S(1)}, bf16[2,8,64,128]{3,2,1,0:T(8,128)(2,1)S(1)}) custom-call(s32[9]{0:T(128)S(1)} %pad_add_fusion.order_ref, bf16[8,64,512]{2,1,0:T(8,128)(2,1)S(1)} %get-tuple-element.91.refs_0_, ...), custom_call_target="tpu_custom_call" | custom-call | flops 1073741824 | bytes 7471140 | tf_op jit(solution)/shard_map/couple_axial/pallas_call | solution.py:32
  113.0 0.1 collective-permute-start.20
  113.1 1.0 collective-permute-start.21
  114.1 2.6 %collective-permute-start.22 = (bf16[2,8,64,128]{3,2,1,0:T(8,128)(2,1)S(1)}, bf16[2,8,64,128]{3,2,1,0:T(8,128)(2,1)S(1)}, u32[]{:S(2)}, u32[]{:S(2)}) collective-permute-start(bf16[2,8,64,128]{3,2,1,0:T(8,128)(2,1)S(1)} %get-tuple-element.111), channel_id=1, source_target_pairs={{0,3},{1,2},{2,1},{3,0},{4,7},{5,6},{6,5},{7,4},{8,11},{9,10},{10,... | collective-permute-start | bytes 786440 | tf_op jit(solution)/shard_map/ppermute | solution.py:353
  116.7 0.0 collective-permute-done.24.refs_2_
  116.7 1.6 %collective-permute-done.25.refs_3_ = bf16[2,8,64,128]{3,2,1,0:T(8,128)(2,1)S(1)} collective-permute-done((bf16[2,8,64,128]{3,2,1,0:T(8,128)(2,1)S(1)}, bf16[2,8,64,128]{3,2,1,0:T(8,128)(2,1)S(1)}, u32[]{:S(2)}, u32[]{:S(2)}) %collective-permute-start.25) | collective-permute-done | bytes 262176 | tf_op jit(solution)/shard_map/ppermute | solution.py:353
  118.3 1.4 %radial_last.2.refs_5_ = bf16[4,8,256,128]{3,2,1,0:T(8,128)(2,1)} custom-call(bf16[2,8,64,128]{3,2,1,0:T(8,128)(2,1)S(1)} %get-tuple-element.113.refs_0_, bf16[2,8,64,128]{3,2,1,0:T(8,128)(2,1)S(1)} %collective-permute-done.23.refs_1_, bf16[2,8,64,128]{3,2,1,0:T(8,128)(2,1)S(1)} %collective-permute-done.24.refs_2_, ...), custom_call_target="tpu_custom_call" | custom-call | flops 268435456 | bytes 2097152 | tf_op jit(solution)/shard_map/radial_last/pallas_call | solution.py:260
  119.8 3.3 %collective-permute-done.21.refs_2_ = bf16[2,8,64,128]{3,2,1,0:T(8,128)(2,1)S(1)} collective-permute-done((bf16[2,8,64,128]{3,2,1,0:T(8,128)(2,1)S(1)}, bf16[2,8,64,128]{3,2,1,0:T(8,128)(2,1)S(1)}, u32[]{:S(2)}, u32[]{:S(2)}) %collective-permute-start.21) | collective-permute-done | bytes 262176 | tf_op jit(solution)/shard_map/ppermute | solution.py:353
  123.1 5.9 %collective-permute-done.22.refs_3_ = bf16[2,8,64,128]{3,2,1,0:T(8,128)(2,1)S(1)} collective-permute-done((bf16[2,8,64,128]{3,2,1,0:T(8,128)(2,1)S(1)}, bf16[2,8,64,128]{3,2,1,0:T(8,128)(2,1)S(1)}, u32[]{:S(2)}, u32[]{:S(2)}) %collective-permute-start.22) | collective-permute-done | bytes 262176 | tf_op jit(solution)/shard_map/ppermute | solution.py:353
  129.0 1.4 %radial_last.3 = bf16[4,8,256,128]{3,2,1,0:T(8,128)(2,1)} custom-call(bf16[2,8,64,128]{3,2,1,0:T(8,128)(2,1)S(1)} %get-tuple-element.108.refs_0_, bf16[2,8,64,128]{3,2,1,0:T(8,128)(2,1)S(1)} %collective-permute-done.20.refs_1_, bf16[2,8,64,128]{3,2,1,0:T(8,128)(2,1)S(1)} %collective-permute-done.21.refs_2_, ...), custom_call_target="tpu_custom_call", output_to_operand_aliasing={{}: (5, {})} | custom-call | flops 268435456 | bytes 2097152 | tf_op jit(solution)/shard_map/radial_last/pallas_call | solution.py:260
  (17 shorter events, 0.0 us)
Async XLA Ops:
  0.1 1.6 %copy-start = (bf16[4,8,64,512]{3,2,1,0:T(8,128)(2,1)S(1)}, bf16[4,8,64,512]{3,2,1,0:T(8,128)(2,1)}, u32[]{:S(2)}) copy-start(bf16[4,8,64,512]{3,2,1,0:T(8,128)(2,1)} %refs_3_.3) | copy-start | bytes 6291460
  2.6 14.2 %collective-permute-start = (bf16[2,8,64,128]{3,2,1,0:T(8,128)(2,1)S(1)}, bf16[2,8,64,128]{3,2,1,0:T(8,128)(2,1)S(1)}, u32[]{:S(2)}, u32[]{:S(2)}) collective-permute-start(bf16[2,8,64,128]{3,2,1,0:T(8,128)(2,1)S(1)} %get-tuple-element.66), channel_id=1, source_target_pairs={{0,2},{1,3},{2,0},{3,1},{4,6},{5,7},{6,4},{7,5},{8,10},{9,11},{10,... | collective-permute-start | bytes 786440 | tf_op jit(solution)/shard_map/ppermute | solution.py:353
  6.3 14.2 %collective-permute-start.1 = (bf16[2,8,64,128]{3,2,1,0:T(8,128)(2,1)S(1)}, bf16[2,8,64,128]{3,2,1,0:T(8,128)(2,1)S(1)}, u32[]{:S(2)}, u32[]{:S(2)}) collective-permute-start(bf16[2,8,64,128]{3,2,1,0:T(8,128)(2,1)S(1)} %get-tuple-element.69), channel_id=1, source_target_pairs={{0,1},{1,0},{2,3},{3,2},{4,5},{5,4},{6,7},{7,6},{8,9},{9,8},{10,11... | collective-permute-start | bytes 786440 | tf_op jit(solution)/shard_map/ppermute | solution.py:353
  7.2 2.9 %copy-start.1 = (bf16[4,256,256]{2,1,0:T(8,128)(2,1)S(1)}, bf16[4,256,256]{2,1,0:T(8,128)(2,1)}, u32[]{:S(2)}) copy-start(bf16[4,256,256]{2,1,0:T(8,128)(2,1)} %rad_ref.1) | copy-start | bytes 1572868
  7.2 2.9 %copy-start.2 = (f32[4,512]{1,0:T(4,128)S(1)}, f32[4,512]{1,0:T(4,128)}, u32[]{:S(2)}) copy-start(f32[4,512]{1,0:T(4,128)} %damp_ref.1) | copy-start | bytes 24580
  7.2 2.9 %copy-start.3 = (f32[8,8]{1,0:T(8,128)S(1)}, f32[8,8]{1,0:T(8,128)}, u32[]{:S(2)}) copy-start(f32[8,8]{1,0:T(8,128)} %one_ref.1) | copy-start | bytes 772
  7.2 3.0 %copy-start.4 = (f32[8,8]{1,0:T(8,128)S(1)}, f32[8,8]{1,0:T(8,128)}, u32[]{:S(2)}) copy-start(f32[8,8]{1,0:T(8,128)} %two_ref.1) | copy-start | bytes 772
  7.3 3.0 %copy-start.5 = (s32[4]{0:T(128)S(1)}, s32[4]{0:T(128)}, u32[]{:S(2)}) copy-start(s32[4]{0:T(128)} %len_ref.1) | copy-start | bytes 52
  7.3 3.0 %copy-start.6 = (bf16[512,512]{1,0:T(8,128)(2,1)S(1)}, bf16[512,512]{1,0:T(8,128)(2,1)}, u32[]{:S(2)}) copy-start(bf16[512,512]{1,0:T(8,128)(2,1)} %constant.51.clone.q_ref) | copy-start | bytes 1572868
  7.3 13.2 %collective-permute-start.2 = (bf16[2,8,64,128]{3,2,1,0:T(8,128)(2,1)S(1)}, bf16[2,8,64,128]{3,2,1,0:T(8,128)(2,1)S(1)}, u32[]{:S(2)}, u32[]{:S(2)}) collective-permute-start(bf16[2,8,64,128]{3,2,1,0:T(8,128)(2,1)S(1)} %get-tuple-element.71), channel_id=1, source_target_pairs={{0,3},{1,2},{2,1},{3,0},{4,7},{5,6},{6,5},{7,4},{8,11},{9,10},{10,... | collective-permute-start | bytes 786440 | tf_op jit(solution)/shard_map/ppermute | solution.py:353
  16.8 13.7 %collective-permute-start.3 = (bf16[2,8,64,128]{3,2,1,0:T(8,128)(2,1)S(1)}, bf16[2,8,64,128]{3,2,1,0:T(8,128)(2,1)S(1)}, u32[]{:S(2)}, u32[]{:S(2)}) collective-permute-start(bf16[2,8,64,128]{3,2,1,0:T(8,128)(2,1)S(1)} %get-tuple-element.74), channel_id=1, source_target_pairs={{0,1},{1,0},{2,3},{3,2},{4,5},{5,4},{6,7},{7,6},{8,9},{9,8},{10,11... | collective-permute-start | bytes 786440 | tf_op jit(solution)/shard_map/ppermute | solution.py:353
  17.3 13.2 %collective-permute-start.4 = (bf16[2,8,64,128]{3,2,1,0:T(8,128)(2,1)S(1)}, bf16[2,8,64,128]{3,2,1,0:T(8,128)(2,1)S(1)}, u32[]{:S(2)}, u32[]{:S(2)}) collective-permute-start(bf16[2,8,64,128]{3,2,1,0:T(8,128)(2,1)S(1)} %get-tuple-element.75), channel_id=1, source_target_pairs={{0,2},{1,3},{2,0},{3,1},{4,6},{5,7},{6,4},{7,5},{8,10},{9,11},{10,... | collective-permute-start | bytes 786440 | tf_op jit(solution)/shard_map/ppermute | solution.py:353
  18.3 17.5 %collective-permute-start.5 = (bf16[2,8,64,128]{3,2,1,0:T(8,128)(2,1)S(1)}, bf16[2,8,64,128]{3,2,1,0:T(8,128)(2,1)S(1)}, u32[]{:S(2)}, u32[]{:S(2)}) collective-permute-start(bf16[2,8,64,128]{3,2,1,0:T(8,128)(2,1)S(1)} %get-tuple-element.76), channel_id=1, source_target_pairs={{0,3},{1,2},{2,1},{3,0},{4,7},{5,6},{6,5},{7,4},{8,11},{9,10},{10,... | collective-permute-start | bytes 786440 | tf_op jit(solution)/shard_map/ppermute | solution.py:353
  21.2 26.0 %collective-permute-start.6 = (bf16[8,256,128]{2,1,0:T(8,128)(2,1)S(1)}, bf16[8,256,128]{2,1,0:T(8,128)(2,1)S(1)}, u32[]{:S(2)}, u32[]{:S(2)}) collective-permute-start(bf16[8,256,128]{2,1,0:T(8,128)(2,1)S(1)} %get-tuple-element.80), channel_id=1, source_target_pairs={{0,4},{4,0},{1,5},{5,1},{2,6},{6,2},{3,7},{7,3},{8,12},{12,8},{9,1... | collective-permute-start | bytes 1572872 | tf_op jit(solution)/shard_map/ppermute | solution.py:377
  21.3 26.0 %collective-permute-start.7 = (bf16[8,256,128]{2,1,0:T(8,128)(2,1)S(1)}, bf16[8,256,128]{2,1,0:T(8,128)(2,1)S(1)}, u32[]{:S(2)}, u32[]{:S(2)}) collective-permute-start(bf16[8,256,128]{2,1,0:T(8,128)(2,1)S(1)} %get-tuple-element.81), channel_id=1, source_target_pairs={{4,8},{8,4},{5,9},{9,5},{6,10},{10,6},{7,11},{11,7},{12,16},{16,12... | collective-permute-start | bytes 1572872 | tf_op jit(solution)/shard_map/ppermute | solution.py:377
  36.5 16.4 %collective-permute-start.8 = (bf16[8,256,128]{2,1,0:T(8,128)(2,1)S(1)}, bf16[8,256,128]{2,1,0:T(8,128)(2,1)S(1)}, u32[]{:S(2)}, u32[]{:S(2)}) collective-permute-start(bf16[8,256,128]{2,1,0:T(8,128)(2,1)S(1)} %get-tuple-element.82), channel_id=1, source_target_pairs={{0,4},{4,0},{1,5},{5,1},{2,6},{6,2},{3,7},{7,3},{8,12},{12,8},{9,1... | collective-permute-start | bytes 1572872 | tf_op jit(solution)/shard_map/ppermute | solution.py:377
  36.6 22.7 %collective-permute-start.9 = (bf16[8,256,128]{2,1,0:T(8,128)(2,1)S(1)}, bf16[8,256,128]{2,1,0:T(8,128)(2,1)S(1)}, u32[]{:S(2)}, u32[]{:S(2)}) collective-permute-start(bf16[8,256,128]{2,1,0:T(8,128)(2,1)S(1)} %get-tuple-element.83), channel_id=1, source_target_pairs={{4,8},{8,4},{5,9},{9,5},{6,10},{10,6},{7,11},{11,7},{12,16},{16,12... | collective-permute-start | bytes 1572872 | tf_op jit(solution)/shard_map/ppermute | solution.py:377
  49.2 14.6 %collective-permute-start.13 = (bf16[2,8,64,128]{3,2,1,0:T(8,128)(2,1)S(1)}, bf16[2,8,64,128]{3,2,1,0:T(8,128)(2,1)S(1)}, u32[]{:S(2)}, u32[]{:S(2)}) collective-permute-start(bf16[2,8,64,128]{3,2,1,0:T(8,128)(2,1)S(1)} %get-tuple-element.93), channel_id=1, source_target_pairs={{0,1},{1,0},{2,3},{3,2},{4,5},{5,4},{6,7},{7,6},{8,9},{9,8},{10,11... | collective-permute-start | bytes 786440 | tf_op jit(solution)/shard_map/ppermute | solution.py:353
  49.5 16.0 %collective-permute-start.14 = (bf16[2,8,64,128]{3,2,1,0:T(8,128)(2,1)S(1)}, bf16[2,8,64,128]{3,2,1,0:T(8,128)(2,1)S(1)}, u32[]{:S(2)}, u32[]{:S(2)}) collective-permute-start(bf16[2,8,64,128]{3,2,1,0:T(8,128)(2,1)S(1)} %get-tuple-element.94), channel_id=1, source_target_pairs={{0,2},{1,3},{2,0},{3,1},{4,6},{5,7},{6,4},{7,5},{8,10},{9,11},{10,... | collective-permute-start | bytes 786440 | tf_op jit(solution)/shard_map/ppermute | solution.py:353
  51.3 15.6 %collective-permute-start.15 = (bf16[2,8,64,128]{3,2,1,0:T(8,128)(2,1)S(1)}, bf16[2,8,64,128]{3,2,1,0:T(8,128)(2,1)S(1)}, u32[]{:S(2)}, u32[]{:S(2)}) collective-permute-start(bf16[2,8,64,128]{3,2,1,0:T(8,128)(2,1)S(1)} %get-tuple-element.95), channel_id=1, source_target_pairs={{0,3},{1,2},{2,1},{3,0},{4,7},{5,6},{6,5},{7,4},{8,11},{9,10},{10,... | collective-permute-start | bytes 786440 | tf_op jit(solution)/shard_map/ppermute | solution.py:353
  61.4 6.8 %collective-permute-start.10 = (bf16[2,8,64,128]{3,2,1,0:T(8,128)(2,1)S(1)}, bf16[2,8,64,128]{3,2,1,0:T(8,128)(2,1)S(1)}, u32[]{:S(2)}, u32[]{:S(2)}) collective-permute-start(bf16[2,8,64,128]{3,2,1,0:T(8,128)(2,1)S(1)} %get-tuple-element.87), channel_id=1, source_target_pairs={{0,1},{1,0},{2,3},{3,2},{4,5},{5,4},{6,7},{7,6},{8,9},{9,8},{10,11... | collective-permute-start | bytes 786440 | tf_op jit(solution)/shard_map/ppermute | solution.py:353
  62.3 9.9 %collective-permute-start.11 = (bf16[2,8,64,128]{3,2,1,0:T(8,128)(2,1)S(1)}, bf16[2,8,64,128]{3,2,1,0:T(8,128)(2,1)S(1)}, u32[]{:S(2)}, u32[]{:S(2)}) collective-permute-start(bf16[2,8,64,128]{3,2,1,0:T(8,128)(2,1)S(1)} %get-tuple-element.88), channel_id=1, source_target_pairs={{0,2},{1,3},{2,0},{3,1},{4,6},{5,7},{6,4},{7,5},{8,10},{9,11},{10,... | collective-permute-start | bytes 786440 | tf_op jit(solution)/shard_map/ppermute | solution.py:353
  63.8 14.0 %collective-permute-start.12 = (bf16[2,8,64,128]{3,2,1,0:T(8,128)(2,1)S(1)}, bf16[2,8,64,128]{3,2,1,0:T(8,128)(2,1)S(1)}, u32[]{:S(2)}, u32[]{:S(2)}) collective-permute-start(bf16[2,8,64,128]{3,2,1,0:T(8,128)(2,1)S(1)} %get-tuple-element.89), channel_id=1, source_target_pairs={{0,3},{1,2},{2,1},{3,0},{4,7},{5,6},{6,5},{7,4},{8,11},{9,10},{10,... | collective-permute-start | bytes 786440 | tf_op jit(solution)/shard_map/ppermute | solution.py:353
  79.1 13.2 %collective-permute-start.16 = (bf16[8,64,512]{2,1,0:T(8,128)(2,1)S(1)}, bf16[8,64,512]{2,1,0:T(8,128)(2,1)S(1)}, u32[]{:S(2)}, u32[]{:S(2)}) collective-permute-start(bf16[8,64,512]{2,1,0:T(8,128)(2,1)S(1)} %get-tuple-element.103), channel_id=1, source_target_pairs={{0,4},{4,0},{1,5},{5,1},{2,6},{6,2},{3,7},{7,3},{8,12},{12,8},{9,1... | collective-permute-start | bytes 1572872 | tf_op jit(solution)/shard_map/ppermute | solution.py:377
  79.2 19.1 %collective-permute-start.17 = (bf16[8,64,512]{2,1,0:T(8,128)(2,1)S(1)}, bf16[8,64,512]{2,1,0:T(8,128)(2,1)S(1)}, u32[]{:S(2)}, u32[]{:S(2)}) collective-permute-start(bf16[8,64,512]{2,1,0:T(8,128)(2,1)S(1)} %get-tuple-element.104), channel_id=1, source_target_pairs={{4,8},{8,4},{5,9},{9,5},{6,10},{10,6},{7,11},{11,7},{12,16},{16,12... | collective-permute-start | bytes 1572872 | tf_op jit(solution)/shard_map/ppermute | solution.py:377
  85.8 19.3 %collective-permute-start.18 = (bf16[8,64,512]{2,1,0:T(8,128)(2,1)S(1)}, bf16[8,64,512]{2,1,0:T(8,128)(2,1)S(1)}, u32[]{:S(2)}, u32[]{:S(2)}) collective-permute-start(bf16[8,64,512]{2,1,0:T(8,128)(2,1)S(1)} %get-tuple-element.105), channel_id=1, source_target_pairs={{0,4},{4,0},{1,5},{5,1},{2,6},{6,2},{3,7},{7,3},{8,12},{12,8},{9,1... | collective-permute-start | bytes 1572872 | tf_op jit(solution)/shard_map/ppermute | solution.py:377
  85.8 24.2 %collective-permute-start.19 = (bf16[8,64,512]{2,1,0:T(8,128)(2,1)S(1)}, bf16[8,64,512]{2,1,0:T(8,128)(2,1)S(1)}, u32[]{:S(2)}, u32[]{:S(2)}) collective-permute-start(bf16[8,64,512]{2,1,0:T(8,128)(2,1)S(1)} %get-tuple-element.106), channel_id=1, source_target_pairs={{4,8},{8,4},{5,9},{9,5},{6,10},{10,6},{7,11},{11,7},{12,16},{16,12... | collective-permute-start | bytes 1572872 | tf_op jit(solution)/shard_map/ppermute | solution.py:377
  101.3 12.8 %collective-permute-start.23 = (bf16[2,8,64,128]{3,2,1,0:T(8,128)(2,1)S(1)}, bf16[2,8,64,128]{3,2,1,0:T(8,128)(2,1)S(1)}, u32[]{:S(2)}, u32[]{:S(2)}) collective-permute-start(bf16[2,8,64,128]{3,2,1,0:T(8,128)(2,1)S(1)} %get-tuple-element.114), channel_id=1, source_target_pairs={{0,1},{1,0},{2,3},{3,2},{4,5},{5,4},{6,7},{7,6},{8,9},{9,8},{10,11... | collective-permute-start | bytes 786440 | tf_op jit(solution)/shard_map/ppermute | solution.py:353
  101.8 14.9 %collective-permute-start.24 = (bf16[2,8,64,128]{3,2,1,0:T(8,128)(2,1)S(1)}, bf16[2,8,64,128]{3,2,1,0:T(8,128)(2,1)S(1)}, u32[]{:S(2)}, u32[]{:S(2)}) collective-permute-start(bf16[2,8,64,128]{3,2,1,0:T(8,128)(2,1)S(1)} %get-tuple-element.115), channel_id=1, source_target_pairs={{0,2},{1,3},{2,0},{3,1},{4,6},{5,7},{6,4},{7,5},{8,10},{9,11},{10,... | collective-permute-start | bytes 786440 | tf_op jit(solution)/shard_map/ppermute | solution.py:353
  103.1 15.3 %collective-permute-start.25 = (bf16[2,8,64,128]{3,2,1,0:T(8,128)(2,1)S(1)}, bf16[2,8,64,128]{3,2,1,0:T(8,128)(2,1)S(1)}, u32[]{:S(2)}, u32[]{:S(2)}) collective-permute-start(bf16[2,8,64,128]{3,2,1,0:T(8,128)(2,1)S(1)} %get-tuple-element.116), channel_id=1, source_target_pairs={{0,3},{1,2},{2,1},{3,0},{4,7},{5,6},{6,5},{7,4},{8,11},{9,10},{10,... | collective-permute-start | bytes 786440 | tf_op jit(solution)/shard_map/ppermute | solution.py:353
  113.0 6.8 %collective-permute-start.20 = (bf16[2,8,64,128]{3,2,1,0:T(8,128)(2,1)S(1)}, bf16[2,8,64,128]{3,2,1,0:T(8,128)(2,1)S(1)}, u32[]{:S(2)}, u32[]{:S(2)}) collective-permute-start(bf16[2,8,64,128]{3,2,1,0:T(8,128)(2,1)S(1)} %get-tuple-element.109), channel_id=1, source_target_pairs={{0,1},{1,0},{2,3},{3,2},{4,5},{5,4},{6,7},{7,6},{8,9},{9,8},{10,11... | collective-permute-start | bytes 786440 | tf_op jit(solution)/shard_map/ppermute | solution.py:353
  113.1 10.0 %collective-permute-start.21 = (bf16[2,8,64,128]{3,2,1,0:T(8,128)(2,1)S(1)}, bf16[2,8,64,128]{3,2,1,0:T(8,128)(2,1)S(1)}, u32[]{:S(2)}, u32[]{:S(2)}) collective-permute-start(bf16[2,8,64,128]{3,2,1,0:T(8,128)(2,1)S(1)} %get-tuple-element.110), channel_id=1, source_target_pairs={{0,2},{1,3},{2,0},{3,1},{4,6},{5,7},{6,4},{7,5},{8,10},{9,11},{10,... | collective-permute-start | bytes 786440 | tf_op jit(solution)/shard_map/ppermute | solution.py:353
  114.1 14.9 %collective-permute-start.22 = (bf16[2,8,64,128]{3,2,1,0:T(8,128)(2,1)S(1)}, bf16[2,8,64,128]{3,2,1,0:T(8,128)(2,1)S(1)}, u32[]{:S(2)}, u32[]{:S(2)}) collective-permute-start(bf16[2,8,64,128]{3,2,1,0:T(8,128)(2,1)S(1)} %get-tuple-element.111), channel_id=1, source_target_pairs={{0,3},{1,2},{2,1},{3,0},{4,7},{5,6},{6,5},{7,4},{8,11},{9,10},{10,... | collective-permute-start | bytes 786440 | tf_op jit(solution)/shard_map/ppermute | solution.py:353

commit v4 on v3

--- a/solution.py
+++ b/solution.py
@@ -12,7 +12,7 @@
 BF = jnp.bfloat16
 F32 = jnp.float32
 SUB = 16
-VMEM_LIMIT = 48 * 1024 * 1024
+VMEM_LIMIT = 16 * 1024 * 1024
 
 
 def cosine_table(count):
@@ -181,6 +181,14 @@
     )
 
 
+class Chosen:
+    def __init__(self, flag, one, other):
+        self.flag, self.one, self.other = flag, one, other
+
+    def __getitem__(self, at):
+        return jnp.where(self.flag, self.one[at], self.other[at])
+
+
 def around(own, before, after, m):
     count = len(own)
 
@@ -195,10 +203,9 @@
 def couple_axial_kernel(peers, modes, count, depth, order_ref, *refs):
     own, refs = refs[:count], refs[count:]
     halos, refs = refs[: 2 * depth], refs[2 * depth :]
-    sides = refs[3 + peers :]
-    for i in range(0, 2 * depth, 2):
-        by_parity(order_ref[2 * peers], halos[i : i + 2], sides[i : i + 2])
-    before, after = sides[0::2], sides[1::2]
+    odd = order_ref[2 * peers] == 1
+    before = [Chosen(odd, *halos[i : i + 2]) for i in range(0, 2 * depth, 2)]
+    after = [Chosen(odd, *halos[i : i + 2][::-1]) for i in range(0, 2 * depth, 2)]
     w_ref, m_ref = refs[:2]
     outs, a_ref = refs[2 : 2 + peers], refs[2 + peers]
     comp, rows, nz = own[0].shape
@@ -227,7 +234,7 @@
         (order, *own, *halos, weights, matrices),
         [shape(len(modes), comp, rows, nz // peers)] * peers,
         len(modes) * comp * rows * nz * 2 * (nz + 4 * comp * SUB),
-        scratch=[pltpu.VMEM((comp * rows, nz), BF)] + [pltpu.VMEM((comp, rows, nz), BF)] * len(halos),
+        scratch=[pltpu.VMEM((comp * rows, nz), BF)],
         smem=1,
     )
 
@@ -277,10 +284,9 @@
 def couple_radial_kernel(peers, modes, count, depth, order_ref, *refs):
     own, refs = refs[:count], refs[count:]
     halos, refs = refs[: 2 * depth], refs[2 * depth :]
-    sides = refs[3 + peers :]
-    for i in range(0, 2 * depth, 2):
-        by_parity(order_ref[2 * peers], halos[i : i + 2], sides[i : i + 2])
-    before, after = sides[0::2], sides[1::2]
+    odd = order_ref[2 * peers] == 1
+    before = [Chosen(odd, *halos[i : i + 2]) for i in range(0, 2 * depth, 2)]
+    after = [Chosen(odd, *halos[i : i + 2][::-1]) for i in range(0, 2 * depth, 2)]
     w_ref, r_ref = refs[:2]
     outs, a_ref = refs[2 : 2 + peers], refs[2 + peers]
     comp, nr, block = own[0].shape
@@ -319,7 +325,7 @@
         (order, *own, *halos, weights, matrices),
         [shape(len(modes), comp, nr // peers, block)] * peers,
         len(modes) * comp * nr * block * 2 * (4 * comp * SUB + nr),
-        scratch=[pltpu.VMEM((comp, nr, block), BF)] * (1 + len(halos)),
+        scratch=[pltpu.VMEM((comp, nr, block), BF)],
         smem=1,
     )
 

time: 131 us -> 130 us (level)
  Pallas kernels: 25.3 us -> 21.5 us
  starting transfers between devices: 53.6 us -> 55.6 us
    pallas_call x9, Pallas kernels: 20.6 us -> 16.8 us  [call(): pl.pallas_call(kernel, out_shape=outs, in_specs=[pl.BlockSpec(memory_spac...]
    ppermute x8, starting transfers between devices: 28 us -> 30.3 us  [exchange(): lax.ppermute(p, ('mode', 'pencil'), pair)]
  transfers between devices with their start and end apart: 26 -> 26, of which waited for: 11 -> 11; matrix products, arithmetic and copies ran while one was open for 0% -> 0% of each run, Pallas kernels for 17% -> 14%
where the time goes in v4:
time: 130 us
  starting transfers between devices  55.6 us (43%)
  waiting for transfers between devices  50.6 us (39%)
  Pallas kernels  21.5 us (17%)
  local copies, waits for them, and re-layouts  1.62 us (1%)
    ppermute x8, starting transfers between devices, exchange(): lax.ppermute(p, ('mode', 'pencil'), pair)  30.3 us
    ppermute x18, waiting for transfers between devices, swap(): lax.ppermute(pieces[k], 'pencil', [(i, i ^ k) for i in range(peers)])  26.9 us
    ppermute x18, starting transfers between devices, swap(): lax.ppermute(pieces[k], 'pencil', [(i, i ^ k) for i in range(peers)])  25.3 us
    ppermute x8, waiting for transfers between devices, exchange(): lax.ppermute(p, ('mode', 'pencil'), pair)  23.7 us
    pallas_call x9, Pallas kernels, call(): pl.pallas_call(kernel, out_shape=outs, in_specs=[pl.BlockSpec(memory_spac...  16.8 us
    pallas_call x2, Pallas kernels, radial_last(): pl.pallas_call(functools.partial(radial_last_kernel, peers), grid=(count,...  2.84 us
  transfers between devices with their start and end apart: 26, of which 11 were waited for; matrix products, arithmetic and copies ran while one was open for 0% of the time, Pallas kernels for 14%

profile of v4, /device:TPU:1, one launch (start us, length us, event | category | flops | bytes accessed | tf_op | source)
XLA Modules:
  0.0 129.7 jit_solution(10797980937323317699)
XLA Ops:
  0.0 0.1 pad_add_fusion.order_ref
  0.1 1.6 %copy-done = bf16[4,8,64,512]{3,2,1,0:T(8,128)(2,1)S(1)} copy-done((bf16[4,8,64,512]{3,2,1,0:T(8,128)(2,1)S(1)}, bf16[4,8,64,512]{3,2,1,0:T(8,128)(2,1)}, u32[]{:S(2)}) %copy-start) | copy-done | bytes 2097176
  1.7 0.9 split.3
  2.6 3.7 %collective-permute-start = (bf16[2,8,64,128]{3,2,1,0:T(8,128)(2,1)S(1)}, bf16[2,8,64,128]{3,2,1,0:T(8,128)(2,1)S(1)}, u32[]{:S(2)}, u32[]{:S(2)}) collective-permute-start(bf16[2,8,64,128]{3,2,1,0:T(8,128)(2,1)S(1)} %get-tuple-element.66), channel_id=1, source_target_pairs={{0,2},{1,3},{2,0},{3,1},{4,6},{5,7},{6,4},{7,5},{8,10},{9,11},{10,... | collective-permute-start | bytes 786440 | tf_op jit(solution)/shard_map/ppermute | solution.py:359
  6.3 1.0 collective-permute-start.1
  7.3 0.0 copy-start.5
  7.3 0.0 copy-start.6
  7.3 1.9 %collective-permute-start.2 = (bf16[2,8,64,128]{3,2,1,0:T(8,128)(2,1)S(1)}, bf16[2,8,64,128]{3,2,1,0:T(8,128)(2,1)S(1)}, u32[]{:S(2)}, u32[]{:S(2)}) collective-permute-start(bf16[2,8,64,128]{3,2,1,0:T(8,128)(2,1)S(1)} %get-tuple-element.71), channel_id=1, source_target_pairs={{0,3},{1,2},{2,1},{3,0},{4,7},{5,6},{6,5},{7,4},{8,11},{9,10},{10,... | collective-permute-start | bytes 786440 | tf_op jit(solution)/shard_map/ppermute | solution.py:359
  9.2 0.9 split.2
  10.2 5.4 %prepare.1 = (bf16[4,512,512]{2,1,0:T(8,128)(2,1)S(1)}, bf16[4,512,512]{2,1,0:T(8,128)(2,1)S(1)}, bf16[4,256,256]{2,1,0:T(8,128)(2,1)S(1)}, bf16[4,256,256]{2,1,0:T(8,128)(2,1)S(1)}, bf16[128,512]{1,0:T(8,128)(2,1)S(1)}) custom-call(s32[9]{0:T(128)S(1)} %pad_add_fusion.order_ref, s32[4]{0:T(128)S(1)} %copy-done.5, bf16[512,512]{1,0:T(8,128)(2,1)S(1)} %copy-done.6, ...), custom_call_target="tpu_custom_call" | custom-call | flops 4294967296 | bytes 6431284 | tf_op jit(solution)/shard_map/prepare/pallas_call | solution.py:32
  15.6 0.0 collective-permute-done.refs_2_
  15.6 0.6 collective-permute-start.3
  16.2 1.5 %collective-permute-start.4 = (bf16[2,8,64,128]{3,2,1,0:T(8,128)(2,1)S(1)}, bf16[2,8,64,128]{3,2,1,0:T(8,128)(2,1)S(1)}, u32[]{:S(2)}, u32[]{:S(2)}) collective-permute-start(bf16[2,8,64,128]{3,2,1,0:T(8,128)(2,1)S(1)} %get-tuple-element.75), channel_id=1, source_target_pairs={{0,2},{1,3},{2,0},{3,1},{4,6},{5,7},{6,4},{7,5},{8,10},{9,11},{10,... | collective-permute-start | bytes 786440 | tf_op jit(solution)/shard_map/ppermute | solution.py:359
  17.7 1.8 %collective-permute-start.5 = (bf16[2,8,64,128]{3,2,1,0:T(8,128)(2,1)S(1)}, bf16[2,8,64,128]{3,2,1,0:T(8,128)(2,1)S(1)}, u32[]{:S(2)}, u32[]{:S(2)}) collective-permute-start(bf16[2,8,64,128]{3,2,1,0:T(8,128)(2,1)S(1)} %get-tuple-element.76), channel_id=1, source_target_pairs={{0,3},{1,2},{2,1},{3,0},{4,7},{5,6},{6,5},{7,4},{8,11},{9,10},{10,... | collective-permute-start | bytes 786440 | tf_op jit(solution)/shard_map/ppermute | solution.py:359
  19.4 0.0 collective-permute-done.1.refs_1_
  19.4 0.0 collective-permute-done.2.refs_3_
  19.4 0.7 assemble.2
  20.1 1.0 collective-permute-start.6
  21.1 9.3 %collective-permute-start.7 = (bf16[8,256,128]{2,1,0:T(8,128)(2,1)S(1)}, bf16[8,256,128]{2,1,0:T(8,128)(2,1)S(1)}, u32[]{:S(2)}, u32[]{:S(2)}) collective-permute-start(bf16[8,256,128]{2,1,0:T(8,128)(2,1)S(1)} %get-tuple-element.81), channel_id=1, source_target_pairs={{4,8},{8,4},{5,9},{9,5},{6,10},{10,6},{7,11},{11,7},{12,16},{16,12... | collective-permute-start | bytes 1572872 | tf_op jit(solution)/shard_map/ppermute | solution.py:383
  30.4 0.0 collective-permute-done.3.refs_1_
  30.4 0.0 collective-permute-done.4.refs_2_
  30.4 3.3 %collective-permute-done.5.refs_3_ = bf16[2,8,64,128]{3,2,1,0:T(8,128)(2,1)S(1)} collective-permute-done((bf16[2,8,64,128]{3,2,1,0:T(8,128)(2,1)S(1)}, bf16[2,8,64,128]{3,2,1,0:T(8,128)(2,1)S(1)}, u32[]{:S(2)}, u32[]{:S(2)}) %collective-permute-start.5) | collective-permute-done | bytes 262176 | tf_op jit(solution)/shard_map/ppermute | solution.py:359
  33.8 0.7 assemble.3
  34.5 0.1 collective-permute-start.8
  34.6 12.3 %collective-permute-start.9 = (bf16[8,256,128]{2,1,0:T(8,128)(2,1)S(1)}, bf16[8,256,128]{2,1,0:T(8,128)(2,1)S(1)}, u32[]{:S(2)}, u32[]{:S(2)}) collective-permute-start(bf16[8,256,128]{2,1,0:T(8,128)(2,1)S(1)} %get-tuple-element.83), channel_id=1, source_target_pairs={{4,8},{8,4},{5,9},{9,5},{6,10},{10,6},{7,11},{11,7},{12,16},{16,12... | collective-permute-start | bytes 1572872 | tf_op jit(solution)/shard_map/ppermute | solution.py:383
  46.8 0.0 collective-permute-done.6.refs_4_
  46.8 0.0 collective-permute-done.7.refs_5_
  46.8 1.9 %couple_radial.3 = (bf16[2,8,64,128]{3,2,1,0:T(8,128)(2,1)S(1)}, bf16[2,8,64,128]{3,2,1,0:T(8,128)(2,1)S(1)}, bf16[2,8,64,128]{3,2,1,0:T(8,128)(2,1)S(1)}, bf16[2,8,64,128]{3,2,1,0:T(8,128)(2,1)S(1)}) custom-call(s32[9]{0:T(128)S(1)} %pad_add_fusion.order_ref, bf16[8,256,128]{2,1,0:T(8,128)(2,1)S(1)} %get-tuple-element.72.refs_0_, ...), custom_call_target="tpu_custom_call" | custom-call | flops 805306368 | bytes 4849700 | tf_op jit(solution)/shard_map/couple_radial/pallas_call | solution.py:32
  48.7 0.1 collective-permute-start.13
  48.8 1.1 collective-permute-start.14
  49.9 2.6 %collective-permute-start.15 = (bf16[2,8,64,128]{3,2,1,0:T(8,128)(2,1)S(1)}, bf16[2,8,64,128]{3,2,1,0:T(8,128)(2,1)S(1)}, u32[]{:S(2)}, u32[]{:S(2)}) collective-permute-start(bf16[2,8,64,128]{3,2,1,0:T(8,128)(2,1)S(1)} %get-tuple-element.95), channel_id=1, source_target_pairs={{0,3},{1,2},{2,1},{3,0},{4,7},{5,6},{6,5},{7,4},{8,11},{9,10},{10,... | collective-permute-start | bytes 786440 | tf_op jit(solution)/shard_map/ppermute | solution.py:359
  52.5 0.0 collective-permute-done.8.refs_6_
  52.5 6.5 %collective-permute-done.9.refs_7_ = bf16[8,256,128]{2,1,0:T(8,128)(2,1)S(1)} collective-permute-done((bf16[8,256,128]{2,1,0:T(8,128)(2,1)S(1)}, bf16[8,256,128]{2,1,0:T(8,128)(2,1)S(1)}, u32[]{:S(2)}, u32[]{:S(2)}) %collective-permute-start.9) | collective-permute-done | bytes 524320 | tf_op jit(solution)/shard_map/ppermute | solution.py:383
  58.9 1.9 %couple_radial.2 = (bf16[2,8,64,128]{3,2,1,0:T(8,128)(2,1)S(1)}, bf16[2,8,64,128]{3,2,1,0:T(8,128)(2,1)S(1)}, bf16[2,8,64,128]{3,2,1,0:T(8,128)(2,1)S(1)}, bf16[2,8,64,128]{3,2,1,0:T(8,128)(2,1)S(1)}) custom-call(s32[9]{0:T(128)S(1)} %pad_add_fusion.order_ref, bf16[8,256,128]{2,1,0:T(8,128)(2,1)S(1)} %get-tuple-element.72.refs_0_, ...), custom_call_target="tpu_custom_call" | custom-call | flops 805306368 | bytes 5898276 | tf_op jit(solution)/shard_map/couple_radial/pallas_call | solution.py:32
  60.8 0.1 collective-permute-start.10
  60.9 1.6 %collective-permute-start.11 = (bf16[2,8,64,128]{3,2,1,0:T(8,128)(2,1)S(1)}, bf16[2,8,64,128]{3,2,1,0:T(8,128)(2,1)S(1)}, u32[]{:S(2)}, u32[]{:S(2)}) collective-permute-start(bf16[2,8,64,128]{3,2,1,0:T(8,128)(2,1)S(1)} %get-tuple-element.88), channel_id=1, source_target_pairs={{0,2},{1,3},{2,0},{3,1},{4,6},{5,7},{6,4},{7,5},{8,10},{9,11},{10,... | collective-permute-start | bytes 786440 | tf_op jit(solution)/shard_map/ppermute | solution.py:359
  62.5 0.0 collective-permute-done.13.refs_1_
  62.5 2.0 %collective-permute-start.12 = (bf16[2,8,64,128]{3,2,1,0:T(8,128)(2,1)S(1)}, bf16[2,8,64,128]{3,2,1,0:T(8,128)(2,1)S(1)}, u32[]{:S(2)}, u32[]{:S(2)}) collective-permute-start(bf16[2,8,64,128]{3,2,1,0:T(8,128)(2,1)S(1)} %get-tuple-element.89), channel_id=1, source_target_pairs={{0,3},{1,2},{2,1},{3,0},{4,7},{5,6},{6,5},{7,4},{8,11},{9,10},{10,... | collective-permute-start | bytes 786440 | tf_op jit(solution)/shard_map/ppermute | solution.py:359
  64.6 0.0 collective-permute-done.14.refs_2_
  64.6 1.8 %collective-permute-done.15.refs_3_ = bf16[2,8,64,128]{3,2,1,0:T(8,128)(2,1)S(1)} collective-permute-done((bf16[2,8,64,128]{3,2,1,0:T(8,128)(2,1)S(1)}, bf16[2,8,64,128]{3,2,1,0:T(8,128)(2,1)S(1)}, u32[]{:S(2)}, u32[]{:S(2)}) %collective-permute-start.15) | collective-permute-done | bytes 262176 | tf_op jit(solution)/shard_map/ppermute | solution.py:359
  66.4 1.3 %axial.3 = (bf16[8,64,512]{2,1,0:T(8,128)(2,1)S(1)}, bf16[8,64,512]{2,1,0:T(8,128)(2,1)S(1)}, bf16[8,64,512]{2,1,0:T(8,128)(2,1)S(1)}, bf16[8,64,512]{2,1,0:T(8,128)(2,1)S(1)}) custom-call(s32[9]{0:T(128)S(1)} %pad_add_fusion.order_ref, bf16[2,8,64,128]{3,2,1,0:T(8,128)(2,1)S(1)} %get-tuple-element.92.refs_0_, ...), custom_call_target="tpu_custom_call" | custom-call | flops 536870912 | bytes 5242916 | tf_op jit(solution)/shard_map/axial/pallas_call | solution.py:32
  67.7 0.0 collective-permute-done.10.refs_1_
  67.7 3.8 %collective-permute-done.11.refs_2_ = bf16[2,8,64,128]{3,2,1,0:T(8,128)(2,1)S(1)} collective-permute-done((bf16[2,8,64,128]{3,2,1,0:T(8,128)(2,1)S(1)}, bf16[2,8,64,128]{3,2,1,0:T(8,128)(2,1)S(1)}, u32[]{:S(2)}, u32[]{:S(2)}) %collective-permute-start.11) | collective-permute-done | bytes 262176 | tf_op jit(solution)/shard_map/ppermute | solution.py:359
  71.6 5.7 %collective-permute-done.12.refs_3_ = bf16[2,8,64,128]{3,2,1,0:T(8,128)(2,1)S(1)} collective-permute-done((bf16[2,8,64,128]{3,2,1,0:T(8,128)(2,1)S(1)}, bf16[2,8,64,128]{3,2,1,0:T(8,128)(2,1)S(1)}, u32[]{:S(2)}, u32[]{:S(2)}) %collective-permute-start.12) | collective-permute-done | bytes 262176 | tf_op jit(solution)/shard_map/ppermute | solution.py:359
  77.3 1.3 %axial.2 = (bf16[8,64,512]{2,1,0:T(8,128)(2,1)S(1)}, bf16[8,64,512]{2,1,0:T(8,128)(2,1)S(1)}, bf16[8,64,512]{2,1,0:T(8,128)(2,1)S(1)}, bf16[8,64,512]{2,1,0:T(8,128)(2,1)S(1)}) custom-call(s32[9]{0:T(128)S(1)} %pad_add_fusion.order_ref, bf16[2,8,64,128]{3,2,1,0:T(8,128)(2,1)S(1)} %get-tuple-element.86.refs_0_, ...), custom_call_target="tpu_custom_call" | custom-call | flops 536870912 | bytes 5242916 | tf_op jit(solution)/shard_map/axial/pallas_call | solution.py:32
  78.6 0.1 collective-permute-start.16
  78.7 6.2 %collective-permute-start.17 = (bf16[8,64,512]{2,1,0:T(8,128)(2,1)S(1)}, bf16[8,64,512]{2,1,0:T(8,128)(2,1)S(1)}, u32[]{:S(2)}, u32[]{:S(2)}) collective-permute-start(bf16[8,64,512]{2,1,0:T(8,128)(2,1)S(1)} %get-tuple-element.104), channel_id=1, source_target_pairs={{4,8},{8,4},{5,9},{9,5},{6,10},{10,6},{7,11},{11,7},{12,16},{16,12... | collective-permute-start | bytes 1572872 | tf_op jit(solution)/shard_map/ppermute | solution.py:383
  84.9 1.4 %collective-permute-start.19 = (bf16[8,64,512]{2,1,0:T(8,128)(2,1)S(1)}, bf16[8,64,512]{2,1,0:T(8,128)(2,1)S(1)}, u32[]{:S(2)}, u32[]{:S(2)}) collective-permute-start(bf16[8,64,512]{2,1,0:T(8,128)(2,1)S(1)} %get-tuple-element.106), channel_id=1, source_target_pairs={{4,8},{8,4},{5,9},{9,5},{6,10},{10,6},{7,11},{11,7},{12,16},{16,12... | collective-permute-start | bytes 1572872 | tf_op jit(solution)/shard_map/ppermute | solution.py:383
  86.3 5.6 %collective-permute-done.16.refs_4_ = bf16[8,64,512]{2,1,0:T(8,128)(2,1)S(1)} collective-permute-done((bf16[8,64,512]{2,1,0:T(8,128)(2,1)S(1)}, bf16[8,64,512]{2,1,0:T(8,128)(2,1)S(1)}, u32[]{:S(2)}, u32[]{:S(2)}) %collective-permute-start.16) | collective-permute-done | bytes 524320 | tf_op jit(solution)/shard_map/ppermute | solution.py:383
  91.9 6.0 %collective-permute-done.17.refs_5_ = bf16[8,64,512]{2,1,0:T(8,128)(2,1)S(1)} collective-permute-done((bf16[8,64,512]{2,1,0:T(8,128)(2,1)S(1)}, bf16[8,64,512]{2,1,0:T(8,128)(2,1)S(1)}, u32[]{:S(2)}, u32[]{:S(2)}) %collective-permute-start.17) | collective-permute-done | bytes 524320 | tf_op jit(solution)/shard_map/ppermute | solution.py:383
  97.9 1.8 %couple_axial.3 = (bf16[2,8,64,128]{3,2,1,0:T(8,128)(2,1)S(1)}, bf16[2,8,64,128]{3,2,1,0:T(8,128)(2,1)S(1)}, bf16[2,8,64,128]{3,2,1,0:T(8,128)(2,1)S(1)}, bf16[2,8,64,128]{3,2,1,0:T(8,128)(2,1)S(1)}) custom-call(s32[9]{0:T(128)S(1)} %pad_add_fusion.order_ref, bf16[8,64,512]{2,1,0:T(8,128)(2,1)S(1)} %get-tuple-element.91.refs_0_, ...), custom_call_target="tpu_custom_call" | custom-call | flops 1073741824 | bytes 6422564 | tf_op jit(solution)/shard_map/couple_axial/pallas_call | solution.py:32
  99.7 0.5 collective-permute-start.23
  100.1 0.9 collective-permute-start.24
  101.0 2.4 %collective-permute-start.25 = (bf16[2,8,64,128]{3,2,1,0:T(8,128)(2,1)S(1)}, bf16[2,8,64,128]{3,2,1,0:T(8,128)(2,1)S(1)}, u32[]{:S(2)}, u32[]{:S(2)}) collective-permute-start(bf16[2,8,64,128]{3,2,1,0:T(8,128)(2,1)S(1)} %get-tuple-element.116), channel_id=1, source_target_pairs={{0,3},{1,2},{2,1},{3,0},{4,7},{5,6},{6,5},{7,4},{8,11},{9,10},{10,... | collective-permute-start | bytes 786440 | tf_op jit(solution)/shard_map/ppermute | solution.py:359
  103.4 5.7 %collective-permute-done.19.refs_7_ = bf16[8,64,512]{2,1,0:T(8,128)(2,1)S(1)} collective-permute-done((bf16[8,64,512]{2,1,0:T(8,128)(2,1)S(1)}, bf16[8,64,512]{2,1,0:T(8,128)(2,1)S(1)}, u32[]{:S(2)}, u32[]{:S(2)}) %collective-permute-start.19) | collective-permute-done | bytes 524320 | tf_op jit(solution)/shard_map/ppermute | solution.py:383
  109.1 1.9 %couple_axial.2 = (bf16[2,8,64,128]{3,2,1,0:T(8,128)(2,1)S(1)}, bf16[2,8,64,128]{3,2,1,0:T(8,128)(2,1)S(1)}, bf16[2,8,64,128]{3,2,1,0:T(8,128)(2,1)S(1)}, bf16[2,8,64,128]{3,2,1,0:T(8,128)(2,1)S(1)}) custom-call(s32[9]{0:T(128)S(1)} %pad_add_fusion.order_ref, bf16[8,64,512]{2,1,0:T(8,128)(2,1)S(1)} %get-tuple-element.91.refs_0_, ...), custom_call_target="tpu_custom_call" | custom-call | flops 1073741824 | bytes 7471140 | tf_op jit(solution)/shard_map/couple_axial/pallas_call | solution.py:32
  110.9 0.1 collective-permute-start.20
  111.0 0.4 collective-permute-start.21
  111.5 3.2 %collective-permute-start.22 = (bf16[2,8,64,128]{3,2,1,0:T(8,128)(2,1)S(1)}, bf16[2,8,64,128]{3,2,1,0:T(8,128)(2,1)S(1)}, u32[]{:S(2)}, u32[]{:S(2)}) collective-permute-start(bf16[2,8,64,128]{3,2,1,0:T(8,128)(2,1)S(1)} %get-tuple-element.111), channel_id=1, source_target_pairs={{0,3},{1,2},{2,1},{3,0},{4,7},{5,6},{6,5},{7,4},{8,11},{9,10},{10,... | collective-permute-start | bytes 786440 | tf_op jit(solution)/shard_map/ppermute | solution.py:359
  114.7 2.5 %collective-permute-done.25.refs_3_ = bf16[2,8,64,128]{3,2,1,0:T(8,128)(2,1)S(1)} collective-permute-done((bf16[2,8,64,128]{3,2,1,0:T(8,128)(2,1)S(1)}, bf16[2,8,64,128]{3,2,1,0:T(8,128)(2,1)S(1)}, u32[]{:S(2)}, u32[]{:S(2)}) %collective-permute-start.25) | collective-permute-done | bytes 262176 | tf_op jit(solution)/shard_map/ppermute | solution.py:359
  117.2 1.4 %radial_last.2.refs_5_ = bf16[4,8,256,128]{3,2,1,0:T(8,128)(2,1)} custom-call(bf16[2,8,64,128]{3,2,1,0:T(8,128)(2,1)S(1)} %get-tuple-element.113.refs_0_, bf16[2,8,64,128]{3,2,1,0:T(8,128)(2,1)S(1)} %collective-permute-done.23.refs_1_, bf16[2,8,64,128]{3,2,1,0:T(8,128)(2,1)S(1)} %collective-permute-done.24.refs_2_, ...), custom_call_target="tpu_custom_call" | custom-call | flops 268435456 | bytes 2097152 | tf_op jit(solution)/shard_map/radial_last/pallas_call | solution.py:267
  118.6 4.0 %collective-permute-done.21.refs_2_ = bf16[2,8,64,128]{3,2,1,0:T(8,128)(2,1)S(1)} collective-permute-done((bf16[2,8,64,128]{3,2,1,0:T(8,128)(2,1)S(1)}, bf16[2,8,64,128]{3,2,1,0:T(8,128)(2,1)S(1)}, u32[]{:S(2)}, u32[]{:S(2)}) %collective-permute-start.21) | collective-permute-done | bytes 262176 | tf_op jit(solution)/shard_map/ppermute | solution.py:359
  122.6 5.6 %collective-permute-done.22.refs_3_ = bf16[2,8,64,128]{3,2,1,0:T(8,128)(2,1)S(1)} collective-permute-done((bf16[2,8,64,128]{3,2,1,0:T(8,128)(2,1)S(1)}, bf16[2,8,64,128]{3,2,1,0:T(8,128)(2,1)S(1)}, u32[]{:S(2)}, u32[]{:S(2)}) %collective-permute-start.22) | collective-permute-done | bytes 262176 | tf_op jit(solution)/shard_map/ppermute | solution.py:359
  128.2 1.4 %radial_last.3 = bf16[4,8,256,128]{3,2,1,0:T(8,128)(2,1)} custom-call(bf16[2,8,64,128]{3,2,1,0:T(8,128)(2,1)S(1)} %get-tuple-element.108.refs_0_, bf16[2,8,64,128]{3,2,1,0:T(8,128)(2,1)S(1)} %collective-permute-done.20.refs_1_, bf16[2,8,64,128]{3,2,1,0:T(8,128)(2,1)S(1)} %collective-permute-done.21.refs_2_, ...), custom_call_target="tpu_custom_call", output_to_operand_aliasing={{}: (5, {})} | custom-call | flops 268435456 | bytes 2097152 | tf_op jit(solution)/shard_map/radial_last/pallas_call | solution.py:267
  (17 shorter events, 0.0 us)
Async XLA Ops:
  0.1 1.6 %copy-start = (bf16[4,8,64,512]{3,2,1,0:T(8,128)(2,1)S(1)}, bf16[4,8,64,512]{3,2,1,0:T(8,128)(2,1)}, u32[]{:S(2)}) copy-start(bf16[4,8,64,512]{3,2,1,0:T(8,128)(2,1)} %refs_3_.3) | copy-start | bytes 6291460
  2.6 13.0 %collective-permute-start = (bf16[2,8,64,128]{3,2,1,0:T(8,128)(2,1)S(1)}, bf16[2,8,64,128]{3,2,1,0:T(8,128)(2,1)S(1)}, u32[]{:S(2)}, u32[]{:S(2)}) collective-permute-start(bf16[2,8,64,128]{3,2,1,0:T(8,128)(2,1)S(1)} %get-tuple-element.66), channel_id=1, source_target_pairs={{0,2},{1,3},{2,0},{3,1},{4,6},{5,7},{6,4},{7,5},{8,10},{9,11},{10,... | collective-permute-start | bytes 786440 | tf_op jit(solution)/shard_map/ppermute | solution.py:359
  6.3 13.1 %collective-permute-start.1 = (bf16[2,8,64,128]{3,2,1,0:T(8,128)(2,1)S(1)}, bf16[2,8,64,128]{3,2,1,0:T(8,128)(2,1)S(1)}, u32[]{:S(2)}, u32[]{:S(2)}) collective-permute-start(bf16[2,8,64,128]{3,2,1,0:T(8,128)(2,1)S(1)} %get-tuple-element.69), channel_id=1, source_target_pairs={{0,1},{1,0},{2,3},{3,2},{4,5},{5,4},{6,7},{7,6},{8,9},{9,8},{10,11... | collective-permute-start | bytes 786440 | tf_op jit(solution)/shard_map/ppermute | solution.py:359
  7.2 2.9 %copy-start.1 = (bf16[4,256,256]{2,1,0:T(8,128)(2,1)S(1)}, bf16[4,256,256]{2,1,0:T(8,128)(2,1)}, u32[]{:S(2)}) copy-start(bf16[4,256,256]{2,1,0:T(8,128)(2,1)} %rad_ref.1) | copy-start | bytes 1572868
  7.2 2.9 %copy-start.2 = (f32[4,512]{1,0:T(4,128)S(1)}, f32[4,512]{1,0:T(4,128)}, u32[]{:S(2)}) copy-start(f32[4,512]{1,0:T(4,128)} %damp_ref.1) | copy-start | bytes 24580
  7.2 2.9 %copy-start.3 = (f32[8,8]{1,0:T(8,128)S(1)}, f32[8,8]{1,0:T(8,128)}, u32[]{:S(2)}) copy-start(f32[8,8]{1,0:T(8,128)} %one_ref.1) | copy-start | bytes 772
  7.2 3.0 %copy-start.4 = (f32[8,8]{1,0:T(8,128)S(1)}, f32[8,8]{1,0:T(8,128)}, u32[]{:S(2)}) copy-start(f32[8,8]{1,0:T(8,128)} %two_ref.1) | copy-start | bytes 772
  7.3 3.0 %copy-start.5 = (s32[4]{0:T(128)S(1)}, s32[4]{0:T(128)}, u32[]{:S(2)}) copy-start(s32[4]{0:T(128)} %len_ref.1) | copy-start | bytes 52
  7.3 3.0 %copy-start.6 = (bf16[512,512]{1,0:T(8,128)(2,1)S(1)}, bf16[512,512]{1,0:T(8,128)(2,1)}, u32[]{:S(2)}) copy-start(bf16[512,512]{1,0:T(8,128)(2,1)} %constant.51.clone.q_ref) | copy-start | bytes 1572868
  7.3 12.2 %collective-permute-start.2 = (bf16[2,8,64,128]{3,2,1,0:T(8,128)(2,1)S(1)}, bf16[2,8,64,128]{3,2,1,0:T(8,128)(2,1)S(1)}, u32[]{:S(2)}, u32[]{:S(2)}) collective-permute-start(bf16[2,8,64,128]{3,2,1,0:T(8,128)(2,1)S(1)} %get-tuple-element.71), channel_id=1, source_target_pairs={{0,3},{1,2},{2,1},{3,0},{4,7},{5,6},{6,5},{7,4},{8,11},{9,10},{10,... | collective-permute-start | bytes 786440 | tf_op jit(solution)/shard_map/ppermute | solution.py:359
  15.6 14.8 %collective-permute-start.3 = (bf16[2,8,64,128]{3,2,1,0:T(8,128)(2,1)S(1)}, bf16[2,8,64,128]{3,2,1,0:T(8,128)(2,1)S(1)}, u32[]{:S(2)}, u32[]{:S(2)}) collective-permute-start(bf16[2,8,64,128]{3,2,1,0:T(8,128)(2,1)S(1)} %get-tuple-element.74), channel_id=1, source_target_pairs={{0,1},{1,0},{2,3},{3,2},{4,5},{5,4},{6,7},{7,6},{8,9},{9,8},{10,11... | collective-permute-start | bytes 786440 | tf_op jit(solution)/shard_map/ppermute | solution.py:359
  16.2 14.2 %collective-permute-start.4 = (bf16[2,8,64,128]{3,2,1,0:T(8,128)(2,1)S(1)}, bf16[2,8,64,128]{3,2,1,0:T(8,128)(2,1)S(1)}, u32[]{:S(2)}, u32[]{:S(2)}) collective-permute-start(bf16[2,8,64,128]{3,2,1,0:T(8,128)(2,1)S(1)} %get-tuple-element.75), channel_id=1, source_target_pairs={{0,2},{1,3},{2,0},{3,1},{4,6},{5,7},{6,4},{7,5},{8,10},{9,11},{10,... | collective-permute-start | bytes 786440 | tf_op jit(solution)/shard_map/ppermute | solution.py:359
  17.7 16.1 %collective-permute-start.5 = (bf16[2,8,64,128]{3,2,1,0:T(8,128)(2,1)S(1)}, bf16[2,8,64,128]{3,2,1,0:T(8,128)(2,1)S(1)}, u32[]{:S(2)}, u32[]{:S(2)}) collective-permute-start(bf16[2,8,64,128]{3,2,1,0:T(8,128)(2,1)S(1)} %get-tuple-element.76), channel_id=1, source_target_pairs={{0,3},{1,2},{2,1},{3,0},{4,7},{5,6},{6,5},{7,4},{8,11},{9,10},{10,... | collective-permute-start | bytes 786440 | tf_op jit(solution)/shard_map/ppermute | solution.py:359
  20.1 26.7 %collective-permute-start.6 = (bf16[8,256,128]{2,1,0:T(8,128)(2,1)S(1)}, bf16[8,256,128]{2,1,0:T(8,128)(2,1)S(1)}, u32[]{:S(2)}, u32[]{:S(2)}) collective-permute-start(bf16[8,256,128]{2,1,0:T(8,128)(2,1)S(1)} %get-tuple-element.80), channel_id=1, source_target_pairs={{0,4},{4,0},{1,5},{5,1},{2,6},{6,2},{3,7},{7,3},{8,12},{12,8},{9,1... | collective-permute-start | bytes 1572872 | tf_op jit(solution)/shard_map/ppermute | solution.py:383
  21.1 25.7 %collective-permute-start.7 = (bf16[8,256,128]{2,1,0:T(8,128)(2,1)S(1)}, bf16[8,256,128]{2,1,0:T(8,128)(2,1)S(1)}, u32[]{:S(2)}, u32[]{:S(2)}) collective-permute-start(bf16[8,256,128]{2,1,0:T(8,128)(2,1)S(1)} %get-tuple-element.81), channel_id=1, source_target_pairs={{4,8},{8,4},{5,9},{9,5},{6,10},{10,6},{7,11},{11,7},{12,16},{16,12... | collective-permute-start | bytes 1572872 | tf_op jit(solution)/shard_map/ppermute | solution.py:383
  34.5 18.0 %collective-permute-start.8 = (bf16[8,256,128]{2,1,0:T(8,128)(2,1)S(1)}, bf16[8,256,128]{2,1,0:T(8,128)(2,1)S(1)}, u32[]{:S(2)}, u32[]{:S(2)}) collective-permute-start(bf16[8,256,128]{2,1,0:T(8,128)(2,1)S(1)} %get-tuple-element.82), channel_id=1, source_target_pairs={{0,4},{4,0},{1,5},{5,1},{2,6},{6,2},{3,7},{7,3},{8,12},{12,8},{9,1... | collective-permute-start | bytes 1572872 | tf_op jit(solution)/shard_map/ppermute | solution.py:383
  34.6 24.4 %collective-permute-start.9 = (bf16[8,256,128]{2,1,0:T(8,128)(2,1)S(1)}, bf16[8,256,128]{2,1,0:T(8,128)(2,1)S(1)}, u32[]{:S(2)}, u32[]{:S(2)}) collective-permute-start(bf16[8,256,128]{2,1,0:T(8,128)(2,1)S(1)} %get-tuple-element.83), channel_id=1, source_target_pairs={{4,8},{8,4},{5,9},{9,5},{6,10},{10,6},{7,11},{11,7},{12,16},{16,12... | collective-permute-start | bytes 1572872 | tf_op jit(solution)/shard_map/ppermute | solution.py:383
  48.7 13.8 %collective-permute-start.13 = (bf16[2,8,64,128]{3,2,1,0:T(8,128)(2,1)S(1)}, bf16[2,8,64,128]{3,2,1,0:T(8,128)(2,1)S(1)}, u32[]{:S(2)}, u32[]{:S(2)}) collective-permute-start(bf16[2,8,64,128]{3,2,1,0:T(8,128)(2,1)S(1)} %get-tuple-element.93), channel_id=1, source_target_pairs={{0,1},{1,0},{2,3},{3,2},{4,5},{5,4},{6,7},{7,6},{8,9},{9,8},{10,11... | collective-permute-start | bytes 786440 | tf_op jit(solution)/shard_map/ppermute | solution.py:359
  48.8 15.7 %collective-permute-start.14 = (bf16[2,8,64,128]{3,2,1,0:T(8,128)(2,1)S(1)}, bf16[2,8,64,128]{3,2,1,0:T(8,128)(2,1)S(1)}, u32[]{:S(2)}, u32[]{:S(2)}) collective-permute-start(bf16[2,8,64,128]{3,2,1,0:T(8,128)(2,1)S(1)} %get-tuple-element.94), channel_id=1, source_target_pairs={{0,2},{1,3},{2,0},{3,1},{4,6},{5,7},{6,4},{7,5},{8,10},{9,11},{10,... | collective-permute-start | bytes 786440 | tf_op jit(solution)/shard_map/ppermute | solution.py:359
  49.9 16.5 %collective-permute-start.15 = (bf16[2,8,64,128]{3,2,1,0:T(8,128)(2,1)S(1)}, bf16[2,8,64,128]{3,2,1,0:T(8,128)(2,1)S(1)}, u32[]{:S(2)}, u32[]{:S(2)}) collective-permute-start(bf16[2,8,64,128]{3,2,1,0:T(8,128)(2,1)S(1)} %get-tuple-element.95), channel_id=1, source_target_pairs={{0,3},{1,2},{2,1},{3,0},{4,7},{5,6},{6,5},{7,4},{8,11},{9,10},{10,... | collective-permute-start | bytes 786440 | tf_op jit(solution)/shard_map/ppermute | solution.py:359
  60.8 6.9 %collective-permute-start.10 = (bf16[2,8,64,128]{3,2,1,0:T(8,128)(2,1)S(1)}, bf16[2,8,64,128]{3,2,1,0:T(8,128)(2,1)S(1)}, u32[]{:S(2)}, u32[]{:S(2)}) collective-permute-start(bf16[2,8,64,128]{3,2,1,0:T(8,128)(2,1)S(1)} %get-tuple-element.87), channel_id=1, source_target_pairs={{0,1},{1,0},{2,3},{3,2},{4,5},{5,4},{6,7},{7,6},{8,9},{9,8},{10,11... | collective-permute-start | bytes 786440 | tf_op jit(solution)/shard_map/ppermute | solution.py:359
  60.9 10.6 %collective-permute-start.11 = (bf16[2,8,64,128]{3,2,1,0:T(8,128)(2,1)S(1)}, bf16[2,8,64,128]{3,2,1,0:T(8,128)(2,1)S(1)}, u32[]{:S(2)}, u32[]{:S(2)}) collective-permute-start(bf16[2,8,64,128]{3,2,1,0:T(8,128)(2,1)S(1)} %get-tuple-element.88), channel_id=1, source_target_pairs={{0,2},{1,3},{2,0},{3,1},{4,6},{5,7},{6,4},{7,5},{8,10},{9,11},{10,... | collective-permute-start | bytes 786440 | tf_op jit(solution)/shard_map/ppermute | solution.py:359
  62.5 14.8 %collective-permute-start.12 = (bf16[2,8,64,128]{3,2,1,0:T(8,128)(2,1)S(1)}, bf16[2,8,64,128]{3,2,1,0:T(8,128)(2,1)S(1)}, u32[]{:S(2)}, u32[]{:S(2)}) collective-permute-start(bf16[2,8,64,128]{3,2,1,0:T(8,128)(2,1)S(1)} %get-tuple-element.89), channel_id=1, source_target_pairs={{0,3},{1,2},{2,1},{3,0},{4,7},{5,6},{6,5},{7,4},{8,11},{9,10},{10,... | collective-permute-start | bytes 786440 | tf_op jit(solution)/shard_map/ppermute | solution.py:359
  78.6 13.3 %collective-permute-start.16 = (bf16[8,64,512]{2,1,0:T(8,128)(2,1)S(1)}, bf16[8,64,512]{2,1,0:T(8,128)(2,1)S(1)}, u32[]{:S(2)}, u32[]{:S(2)}) collective-permute-start(bf16[8,64,512]{2,1,0:T(8,128)(2,1)S(1)} %get-tuple-element.103), channel_id=1, source_target_pairs={{0,4},{4,0},{1,5},{5,1},{2,6},{6,2},{3,7},{7,3},{8,12},{12,8},{9,1... | collective-permute-start | bytes 1572872 | tf_op jit(solution)/shard_map/ppermute | solution.py:383
  78.7 19.1 %collective-permute-start.17 = (bf16[8,64,512]{2,1,0:T(8,128)(2,1)S(1)}, bf16[8,64,512]{2,1,0:T(8,128)(2,1)S(1)}, u32[]{:S(2)}, u32[]{:S(2)}) collective-permute-start(bf16[8,64,512]{2,1,0:T(8,128)(2,1)S(1)} %get-tuple-element.104), channel_id=1, source_target_pairs={{4,8},{8,4},{5,9},{9,5},{6,10},{10,6},{7,11},{11,7},{12,16},{16,12... | collective-permute-start | bytes 1572872 | tf_op jit(solution)/shard_map/ppermute | solution.py:383
  84.9 18.5 %collective-permute-start.18 = (bf16[8,64,512]{2,1,0:T(8,128)(2,1)S(1)}, bf16[8,64,512]{2,1,0:T(8,128)(2,1)S(1)}, u32[]{:S(2)}, u32[]{:S(2)}) collective-permute-start(bf16[8,64,512]{2,1,0:T(8,128)(2,1)S(1)} %get-tuple-element.105), channel_id=1, source_target_pairs={{0,4},{4,0},{1,5},{5,1},{2,6},{6,2},{3,7},{7,3},{8,12},{12,8},{9,1... | collective-permute-start | bytes 1572872 | tf_op jit(solution)/shard_map/ppermute | solution.py:383
  84.9 24.2 %collective-permute-start.19 = (bf16[8,64,512]{2,1,0:T(8,128)(2,1)S(1)}, bf16[8,64,512]{2,1,0:T(8,128)(2,1)S(1)}, u32[]{:S(2)}, u32[]{:S(2)}) collective-permute-start(bf16[8,64,512]{2,1,0:T(8,128)(2,1)S(1)} %get-tuple-element.106), channel_id=1, source_target_pairs={{4,8},{8,4},{5,9},{9,5},{6,10},{10,6},{7,11},{11,7},{12,16},{16,12... | collective-permute-start | bytes 1572872 | tf_op jit(solution)/shard_map/ppermute | solution.py:383
  99.7 11.8 %collective-permute-start.23 = (bf16[2,8,64,128]{3,2,1,0:T(8,128)(2,1)S(1)}, bf16[2,8,64,128]{3,2,1,0:T(8,128)(2,1)S(1)}, u32[]{:S(2)}, u32[]{:S(2)}) collective-permute-start(bf16[2,8,64,128]{3,2,1,0:T(8,128)(2,1)S(1)} %get-tuple-element.114), channel_id=1, source_target_pairs={{0,1},{1,0},{2,3},{3,2},{4,5},{5,4},{6,7},{7,6},{8,9},{9,8},{10,11... | collective-permute-start | bytes 786440 | tf_op jit(solution)/shard_map/ppermute | solution.py:359
  100.1 14.5 %collective-permute-start.24 = (bf16[2,8,64,128]{3,2,1,0:T(8,128)(2,1)S(1)}, bf16[2,8,64,128]{3,2,1,0:T(8,128)(2,1)S(1)}, u32[]{:S(2)}, u32[]{:S(2)}) collective-permute-start(bf16[2,8,64,128]{3,2,1,0:T(8,128)(2,1)S(1)} %get-tuple-element.115), channel_id=1, source_target_pairs={{0,2},{1,3},{2,0},{3,1},{4,6},{5,7},{6,4},{7,5},{8,10},{9,11},{10,... | collective-permute-start | bytes 786440 | tf_op jit(solution)/shard_map/ppermute | solution.py:359
  101.0 16.1 %collective-permute-start.25 = (bf16[2,8,64,128]{3,2,1,0:T(8,128)(2,1)S(1)}, bf16[2,8,64,128]{3,2,1,0:T(8,128)(2,1)S(1)}, u32[]{:S(2)}, u32[]{:S(2)}) collective-permute-start(bf16[2,8,64,128]{3,2,1,0:T(8,128)(2,1)S(1)} %get-tuple-element.116), channel_id=1, source_target_pairs={{0,3},{1,2},{2,1},{3,0},{4,7},{5,6},{6,5},{7,4},{8,11},{9,10},{10,... | collective-permute-start | bytes 786440 | tf_op jit(solution)/shard_map/ppermute | solution.py:359
  110.9 7.6 %collective-permute-start.20 = (bf16[2,8,64,128]{3,2,1,0:T(8,128)(2,1)S(1)}, bf16[2,8,64,128]{3,2,1,0:T(8,128)(2,1)S(1)}, u32[]{:S(2)}, u32[]{:S(2)}) collective-permute-start(bf16[2,8,64,128]{3,2,1,0:T(8,128)(2,1)S(1)} %get-tuple-element.109), channel_id=1, source_target_pairs={{0,1},{1,0},{2,3},{3,2},{4,5},{5,4},{6,7},{7,6},{8,9},{9,8},{10,11... | collective-permute-start | bytes 786440 | tf_op jit(solution)/shard_map/ppermute | solution.py:359
  111.0 11.6 %collective-permute-start.21 = (bf16[2,8,64,128]{3,2,1,0:T(8,128)(2,1)S(1)}, bf16[2,8,64,128]{3,2,1,0:T(8,128)(2,1)S(1)}, u32[]{:S(2)}, u32[]{:S(2)}) collective-permute-start(bf16[2,8,64,128]{3,2,1,0:T(8,128)(2,1)S(1)} %get-tuple-element.110), channel_id=1, source_target_pairs={{0,2},{1,3},{2,0},{3,1},{4,6},{5,7},{6,4},{7,5},{8,10},{9,11},{10,... | collective-permute-start | bytes 786440 | tf_op jit(solution)/shard_map/ppermute | solution.py:359
  111.5 16.8 %collective-permute-start.22 = (bf16[2,8,64,128]{3,2,1,0:T(8,128)(2,1)S(1)}, bf16[2,8,64,128]{3,2,1,0:T(8,128)(2,1)S(1)}, u32[]{:S(2)}, u32[]{:S(2)}) collective-permute-start(bf16[2,8,64,128]{3,2,1,0:T(8,128)(2,1)S(1)} %get-tuple-element.111), channel_id=1, source_target_pairs={{0,3},{1,2},{2,1},{3,0},{4,7},{5,6},{6,5},{7,4},{8,11},{9,10},{10,... | collective-permute-start | bytes 786440 | tf_op jit(solution)/shard_map/ppermute | solution.py:359

commit v5 on v4

--- a/solution.py
+++ b/solution.py
@@ -116,35 +116,36 @@
     )
 
 
-def split_kernel(peers, order_ref, *refs):
+def split_kernel(peers, chosen, order_ref, x_ref, *refs):
+    outs, sems = refs[:peers], refs[peers]
+    block = outs[0].shape[3]
+    copies = []
     for k in range(peers):
-        refs[peers + k][...] = refs[k][...]
-
-
-def split(peers, order, x, first, step, number):
+        start = pl.multiple_of(order_ref[k] * block, block)
+        for at, m in enumerate(chosen):
+            source = x_ref.at[m, :, :, pl.ds(start, block)]
+            copies.append(pltpu.make_async_copy(source, outs[k].at[at], sems.at[k, at]))
+    for copy in copies:
+        copy.start()
+    for copy in copies:
+        copy.wait()
+
+
+def split(peers, order, x, chosen):
     _, comp, rows, nz = x.shape
-    block = nz // peers
+    number = len(chosen)
     return pl.pallas_call(
-        functools.partial(split_kernel, peers),
-        grid_spec=pltpu.PrefetchScalarGridSpec(
-            num_scalar_prefetch=1,
-            grid=(number,),
-            in_specs=[
-                pl.BlockSpec(
-                    (1, comp, rows, block),
-                    functools.partial(lambda k, i, order: (first + step * i, 0, 0, order[k]), k),
-                )
-                for k in range(peers)
-            ],
-            out_specs=[pl.BlockSpec((1, comp, rows, block), lambda i, order: (i, 0, 0, 0))] * peers,
-        ),
-        out_shape=[shape(number, comp, rows, block)] * peers,
+        functools.partial(split_kernel, peers, chosen),
+        in_specs=[pl.BlockSpec(memory_space=pltpu.SMEM), pl.BlockSpec(memory_space=pltpu.HBM)],
+        out_specs=vmem(peers),
+        out_shape=[shape(number, comp, rows, nz // peers)] * peers,
+        scratch_shapes=[pltpu.SemaphoreType.DMA((peers, number))],
         compiler_params=pltpu.CompilerParams(vmem_limit_bytes=VMEM_LIMIT),
         cost_estimate=pl.CostEstimate(
             flops=0, bytes_accessed=4 * number * comp * rows * nz, transcendentals=0
         ),
         name="split",
-    )(order, *[x] * peers)
+    )(order, x)
 
 
 def by_parity(odd, given, taken):
@@ -239,37 +240,48 @@
     )
 
 
-def radial_one(pieces, matrix, out):
-    comp, _, block = pieces[0].shape
-    for c in range(0, comp, 2):
-        field = jnp.concatenate([jnp.concatenate([p[c], p[c + 1]], axis=1) for p in pieces], axis=0)
-        result = dot(matrix, field).astype(BF)
-        out[c] = result[:, :block]
-        out[c + 1] = result[:, block:]
-
-
-def radial_last_kernel(peers, *refs):
-    radial_one([p.at[0] for p in refs[:peers]], refs[peers][0], refs[-1].at[0])
+def radial_last_kernel(peers, modes, *refs):
+    pieces, r_ref = refs[:peers], refs[peers]
+    out_ref, made_ref, sems = refs[-3:]
+    comp, _, block = pieces[0].shape[1:]
+    copies = []
+    for at, m in enumerate(modes):
+        for c in range(0, comp, 2):
+            field = jnp.concatenate(
+                [jnp.concatenate([p[at, c], p[at, c + 1]], axis=1) for p in pieces], axis=0
+            )
+            result = dot(r_ref[m], field).astype(BF)
+            made_ref[at, c] = result[:, :block]
+            made_ref[at, c + 1] = result[:, block:]
+            copies.append(
+                pltpu.make_async_copy(
+                    made_ref.at[at, c : c + 2], out_ref.at[m, c : c + 2], sems.at[at, c // 2]
+                )
+            )
+            copies[-1].start()
+    for copy in copies:
+        copy.wait()
 
 
 def radial_last(peers, modes, total, pieces, matrices, partial_result):
     count, comp, rows, block = pieces[0].shape
-    first, step = modes[0], modes[1] - modes[0]
     nr = rows * peers
-    specs = [pl.BlockSpec((1, comp, rows, block), lambda i: (i, 0, 0, 0))] * peers
-    specs.append(pl.BlockSpec((1, nr, nr), lambda i: (first + step * i, 0, 0)))
+    specs = vmem(peers + 1)
     args = [*pieces, matrices]
     aliases = {}
     if partial_result is not None:
-        specs.append(pl.BlockSpec(memory_space=pl.ANY))
+        specs.append(pl.BlockSpec(memory_space=pltpu.HBM))
         aliases = {len(args): 0}
         args.append(partial_result)
     return pl.pallas_call(
-        functools.partial(radial_last_kernel, peers),
-        grid=(count,),
+        functools.partial(radial_last_kernel, peers, modes),
         out_shape=shape(total, comp, nr, block),
         in_specs=specs,
-        out_specs=pl.BlockSpec((1, comp, nr, block), lambda i: (first + step * i, 0, 0, 0)),
+        out_specs=pl.BlockSpec(memory_space=pltpu.HBM),
+        scratch_shapes=[
+            pltpu.VMEM((count, comp, nr, block), BF),
+            pltpu.SemaphoreType.DMA((count, comp // 2)),
+        ],
         input_output_aliases=aliases,
         compiler_params=pltpu.CompilerParams(vmem_limit_bytes=VMEM_LIMIT),
         cost_estimate=pl.CostEstimate(
@@ -389,8 +401,9 @@
     last = count - 1
     inner, outer = (1, last - 1), (0, last)
 
-    pieces_outer = swap(split(peers, order, cotangent, 0, last, 2))
-    pieces_inner = split(peers, order, cotangent, 1, last - 2, 2)
+    cotangent = pltpu.with_memory_space_constraint(cotangent, pltpu.MemorySpace.HBM)
+    pieces_outer = swap(split(peers, order, cotangent, outer))
+    pieces_inner = split(peers, order, cotangent, inner)
     in_m, out_m, in_r, out_r, weights = prepare(
         peers, order, lengths, table, axial_damping, radial_ops, couple_one, couple_two
     )

time: 130 us -> 129 us (level)
  starting transfers between devices: 55.6 us -> 53.9 us
  Pallas kernels: 21.5 us -> 23.1 us
  local copies, waits for them, and re-layouts: 1.62 us -> 0.03 us
    pallas_call x4, Pallas kernels: 4.7 us -> 6.37 us  [the longest x2 3.85 us: split(): pl.pallas_call(functools.partial(split_kernel, peers, chosen), in_specs=[...]
    ppermute x8, starting transfers between devices: 30.3 us -> 28.6 us  [exchange(): lax.ppermute(p, ('mode', 'pencil'), pair)]
    unnamed x14 -> x12, local copies, waits for them, and re-layouts: 1.62 us -> 0.03 us
where the time goes in v5:
time: 129 us
  starting transfers between devices  53.9 us (42%)
  waiting for transfers between devices  51.7 us (40%)
  Pallas kernels  23.1 us (18%)
    ppermute x8, starting transfers between devices, exchange(): lax.ppermute(p, ('mode', 'pencil'), pair)  28.6 us
    ppermute x18, waiting for transfers between devices, swap(): lax.ppermute(pieces[k], 'pencil', [(i, i ^ k) for i in range(peers)])  28.1 us
    ppermute x18, starting transfers between devices, swap(): lax.ppermute(pieces[k], 'pencil', [(i, i ^ k) for i in range(peers)])  25.2 us
    ppermute x8, waiting for transfers between devices, exchange(): lax.ppermute(p, ('mode', 'pencil'), pair)  23.6 us
    pallas_call x9, Pallas kernels, call(): pl.pallas_call(kernel, out_shape=outs, in_specs=[pl.BlockSpec(memory_spac...  16.8 us
    pallas_call x2, Pallas kernels, split(): pl.pallas_call(functools.partial(split_kernel, peers, chosen), in_specs=[...  3.85 us
  transfers between devices with their start and end apart: 26, of which 11 were waited for; matrix products, arithmetic and copies ran while one was open for 0% of the time, Pallas kernels for 14%

profile of v5, /device:TPU:1, one launch (start us, length us, event | category | flops | bytes accessed | tf_op | source)
XLA Modules:
  0.0 129.3 jit_solution(350262805045625146)
XLA Ops:
  0.0 0.1 pad_add_fusion.order_ref
  0.1 0.0 copy-start.4
  0.1 0.0 copy-start.5
  0.1 1.9 %split.3 = (bf16[2,8,64,128]{3,2,1,0:T(8,128)(2,1)S(1)}, bf16[2,8,64,128]{3,2,1,0:T(8,128)(2,1)S(1)}, bf16[2,8,64,128]{3,2,1,0:T(8,128)(2,1)S(1)}, bf16[2,8,64,128]{3,2,1,0:T(8,128)(2,1)S(1)}) custom-call(s32[9]{0:T(128)S(1)} %pad_add_fusion.order_ref, bf16[4,8,64,512]{3,2,1,0:T(8,128)(2,1)} %x_ref.3), custom_call_target="tpu_custom_call" | custom-call | bytes 2097152 | tf_op jit(solution)/shard_map/split/pallas_call | solution.py:137
  2.1 3.7 %collective-permute-start = (bf16[2,8,64,128]{3,2,1,0:T(8,128)(2,1)S(1)}, bf16[2,8,64,128]{3,2,1,0:T(8,128)(2,1)S(1)}, u32[]{:S(2)}, u32[]{:S(2)}) collective-permute-start(bf16[2,8,64,128]{3,2,1,0:T(8,128)(2,1)S(1)} %get-tuple-element.66), channel_id=1, source_target_pairs={{0,2},{1,3},{2,0},{3,1},{4,6},{5,7},{6,4},{7,5},{8,10},{9,11},{10,... | collective-permute-start | bytes 786440 | tf_op jit(solution)/shard_map/ppermute | solution.py:371
  5.7 1.0 collective-permute-start.1
  6.7 1.9 %collective-permute-start.2 = (bf16[2,8,64,128]{3,2,1,0:T(8,128)(2,1)S(1)}, bf16[2,8,64,128]{3,2,1,0:T(8,128)(2,1)S(1)}, u32[]{:S(2)}, u32[]{:S(2)}) collective-permute-start(bf16[2,8,64,128]{3,2,1,0:T(8,128)(2,1)S(1)} %get-tuple-element.71), channel_id=1, source_target_pairs={{0,3},{1,2},{2,1},{3,0},{4,7},{5,6},{6,5},{7,4},{8,11},{9,10},{10,... | collective-permute-start | bytes 786440 | tf_op jit(solution)/shard_map/ppermute | solution.py:371
  8.5 1.9 %split.2 = (bf16[2,8,64,128]{3,2,1,0:T(8,128)(2,1)S(1)}, bf16[2,8,64,128]{3,2,1,0:T(8,128)(2,1)S(1)}, bf16[2,8,64,128]{3,2,1,0:T(8,128)(2,1)S(1)}, bf16[2,8,64,128]{3,2,1,0:T(8,128)(2,1)S(1)}) custom-call(s32[9]{0:T(128)S(1)} %pad_add_fusion.order_ref, bf16[4,8,64,512]{3,2,1,0:T(8,128)(2,1)} %x_ref.3), custom_call_target="tpu_custom_call" | custom-call | bytes 2097152 | tf_op jit(solution)/shard_map/split/pallas_call | solution.py:137
  10.5 5.3 %prepare.1 = (bf16[4,512,512]{2,1,0:T(8,128)(2,1)S(1)}, bf16[4,512,512]{2,1,0:T(8,128)(2,1)S(1)}, bf16[4,256,256]{2,1,0:T(8,128)(2,1)S(1)}, bf16[4,256,256]{2,1,0:T(8,128)(2,1)S(1)}, bf16[128,512]{1,0:T(8,128)(2,1)S(1)}) custom-call(s32[9]{0:T(128)S(1)} %pad_add_fusion.order_ref, s32[4]{0:T(128)S(1)} %copy-done.4, bf16[512,512]{1,0:T(8,128)(2,1)S(1)} %copy-done.5, ...), custom_call_target="tpu_custom_call" | custom-call | flops 4294967296 | bytes 6431284 | tf_op jit(solution)/shard_map/prepare/pallas_call | solution.py:32
  15.8 0.0 collective-permute-done.refs_2_
  15.9 0.6 collective-permute-start.3
  16.4 1.0 collective-permute-start.4
  17.5 2.2 %collective-permute-start.5 = (bf16[2,8,64,128]{3,2,1,0:T(8,128)(2,1)S(1)}, bf16[2,8,64,128]{3,2,1,0:T(8,128)(2,1)S(1)}, u32[]{:S(2)}, u32[]{:S(2)}) collective-permute-start(bf16[2,8,64,128]{3,2,1,0:T(8,128)(2,1)S(1)} %get-tuple-element.76), channel_id=1, source_target_pairs={{0,3},{1,2},{2,1},{3,0},{4,7},{5,6},{6,5},{7,4},{8,11},{9,10},{10,... | collective-permute-start | bytes 786440 | tf_op jit(solution)/shard_map/ppermute | solution.py:371
  19.7 0.0 collective-permute-done.1.refs_1_
  19.7 0.0 collective-permute-done.2.refs_3_
  19.7 0.7 assemble.2
  20.4 0.2 collective-permute-start.6
  20.6 9.3 %collective-permute-start.7 = (bf16[8,256,128]{2,1,0:T(8,128)(2,1)S(1)}, bf16[8,256,128]{2,1,0:T(8,128)(2,1)S(1)}, u32[]{:S(2)}, u32[]{:S(2)}) collective-permute-start(bf16[8,256,128]{2,1,0:T(8,128)(2,1)S(1)} %get-tuple-element.81), channel_id=1, source_target_pairs={{4,8},{8,4},{5,9},{9,5},{6,10},{10,6},{7,11},{11,7},{12,16},{16,12... | collective-permute-start | bytes 1572872 | tf_op jit(solution)/shard_map/ppermute | solution.py:395
  29.9 0.0 collective-permute-done.3.refs_1_
  29.9 0.0 collective-permute-done.4.refs_2_
  29.9 4.9 %collective-permute-done.5.refs_3_ = bf16[2,8,64,128]{3,2,1,0:T(8,128)(2,1)S(1)} collective-permute-done((bf16[2,8,64,128]{3,2,1,0:T(8,128)(2,1)S(1)}, bf16[2,8,64,128]{3,2,1,0:T(8,128)(2,1)S(1)}, u32[]{:S(2)}, u32[]{:S(2)}) %collective-permute-start.5) | collective-permute-done | bytes 262176 | tf_op jit(solution)/shard_map/ppermute | solution.py:371
  34.7 0.7 assemble.3
  35.4 0.1 collective-permute-start.8
  35.5 11.1 %collective-permute-start.9 = (bf16[8,256,128]{2,1,0:T(8,128)(2,1)S(1)}, bf16[8,256,128]{2,1,0:T(8,128)(2,1)S(1)}, u32[]{:S(2)}, u32[]{:S(2)}) collective-permute-start(bf16[8,256,128]{2,1,0:T(8,128)(2,1)S(1)} %get-tuple-element.83), channel_id=1, source_target_pairs={{4,8},{8,4},{5,9},{9,5},{6,10},{10,6},{7,11},{11,7},{12,16},{16,12... | collective-permute-start | bytes 1572872 | tf_op jit(solution)/shard_map/ppermute | solution.py:395
  46.6 1.9 %couple_radial.3 = (bf16[2,8,64,128]{3,2,1,0:T(8,128)(2,1)S(1)}, bf16[2,8,64,128]{3,2,1,0:T(8,128)(2,1)S(1)}, bf16[2,8,64,128]{3,2,1,0:T(8,128)(2,1)S(1)}, bf16[2,8,64,128]{3,2,1,0:T(8,128)(2,1)S(1)}) custom-call(s32[9]{0:T(128)S(1)} %pad_add_fusion.order_ref, bf16[8,256,128]{2,1,0:T(8,128)(2,1)S(1)} %get-tuple-element.72.refs_0_, ...), custom_call_target="tpu_custom_call" | custom-call | flops 805306368 | bytes 4849700 | tf_op jit(solution)/shard_map/couple_radial/pallas_call | solution.py:32
  48.5 0.1 collective-permute-start.13
  48.6 0.9 collective-permute-start.14
  49.5 2.7 %collective-permute-start.15 = (bf16[2,8,64,128]{3,2,1,0:T(8,128)(2,1)S(1)}, bf16[2,8,64,128]{3,2,1,0:T(8,128)(2,1)S(1)}, u32[]{:S(2)}, u32[]{:S(2)}) collective-permute-start(bf16[2,8,64,128]{3,2,1,0:T(8,128)(2,1)S(1)} %get-tuple-element.95), channel_id=1, source_target_pairs={{0,3},{1,2},{2,1},{3,0},{4,7},{5,6},{6,5},{7,4},{8,11},{9,10},{10,... | collective-permute-start | bytes 786440 | tf_op jit(solution)/shard_map/ppermute | solution.py:371
  52.2 0.0 collective-permute-done.8.refs_6_
  52.2 6.4 %collective-permute-done.9.refs_7_ = bf16[8,256,128]{2,1,0:T(8,128)(2,1)S(1)} collective-permute-done((bf16[8,256,128]{2,1,0:T(8,128)(2,1)S(1)}, bf16[8,256,128]{2,1,0:T(8,128)(2,1)S(1)}, u32[]{:S(2)}, u32[]{:S(2)}) %collective-permute-start.9) | collective-permute-done | bytes 524320 | tf_op jit(solution)/shard_map/ppermute | solution.py:395
  58.6 1.9 %couple_radial.2 = (bf16[2,8,64,128]{3,2,1,0:T(8,128)(2,1)S(1)}, bf16[2,8,64,128]{3,2,1,0:T(8,128)(2,1)S(1)}, bf16[2,8,64,128]{3,2,1,0:T(8,128)(2,1)S(1)}, bf16[2,8,64,128]{3,2,1,0:T(8,128)(2,1)S(1)}) custom-call(s32[9]{0:T(128)S(1)} %pad_add_fusion.order_ref, bf16[8,256,128]{2,1,0:T(8,128)(2,1)S(1)} %get-tuple-element.72.refs_0_, ...), custom_call_target="tpu_custom_call" | custom-call | flops 805306368 | bytes 5898276 | tf_op jit(solution)/shard_map/couple_radial/pallas_call | solution.py:32
  60.5 0.1 collective-permute-start.10
  60.6 1.4 %collective-permute-start.11 = (bf16[2,8,64,128]{3,2,1,0:T(8,128)(2,1)S(1)}, bf16[2,8,64,128]{3,2,1,0:T(8,128)(2,1)S(1)}, u32[]{:S(2)}, u32[]{:S(2)}) collective-permute-start(bf16[2,8,64,128]{3,2,1,0:T(8,128)(2,1)S(1)} %get-tuple-element.88), channel_id=1, source_target_pairs={{0,2},{1,3},{2,0},{3,1},{4,6},{5,7},{6,4},{7,5},{8,10},{9,11},{10,... | collective-permute-start | bytes 786440 | tf_op jit(solution)/shard_map/ppermute | solution.py:371
  62.0 2.3 %collective-permute-start.12 = (bf16[2,8,64,128]{3,2,1,0:T(8,128)(2,1)S(1)}, bf16[2,8,64,128]{3,2,1,0:T(8,128)(2,1)S(1)}, u32[]{:S(2)}, u32[]{:S(2)}) collective-permute-start(bf16[2,8,64,128]{3,2,1,0:T(8,128)(2,1)S(1)} %get-tuple-element.89), channel_id=1, source_target_pairs={{0,3},{1,2},{2,1},{3,0},{4,7},{5,6},{6,5},{7,4},{8,11},{9,10},{10,... | collective-permute-start | bytes 786440 | tf_op jit(solution)/shard_map/ppermute | solution.py:371
  64.3 1.8 %collective-permute-done.15.refs_3_ = bf16[2,8,64,128]{3,2,1,0:T(8,128)(2,1)S(1)} collective-permute-done((bf16[2,8,64,128]{3,2,1,0:T(8,128)(2,1)S(1)}, bf16[2,8,64,128]{3,2,1,0:T(8,128)(2,1)S(1)}, u32[]{:S(2)}, u32[]{:S(2)}) %collective-permute-start.15) | collective-permute-done | bytes 262176 | tf_op jit(solution)/shard_map/ppermute | solution.py:371
  66.1 1.3 %axial.3 = (bf16[8,64,512]{2,1,0:T(8,128)(2,1)S(1)}, bf16[8,64,512]{2,1,0:T(8,128)(2,1)S(1)}, bf16[8,64,512]{2,1,0:T(8,128)(2,1)S(1)}, bf16[8,64,512]{2,1,0:T(8,128)(2,1)S(1)}) custom-call(s32[9]{0:T(128)S(1)} %pad_add_fusion.order_ref, bf16[2,8,64,128]{3,2,1,0:T(8,128)(2,1)S(1)} %get-tuple-element.92.refs_0_, ...), custom_call_target="tpu_custom_call" | custom-call | flops 536870912 | bytes 5242916 | tf_op jit(solution)/shard_map/axial/pallas_call | solution.py:32
  67.4 0.0 collective-permute-done.10.refs_1_
  67.4 3.8 %collective-permute-done.11.refs_2_ = bf16[2,8,64,128]{3,2,1,0:T(8,128)(2,1)S(1)} collective-permute-done((bf16[2,8,64,128]{3,2,1,0:T(8,128)(2,1)S(1)}, bf16[2,8,64,128]{3,2,1,0:T(8,128)(2,1)S(1)}, u32[]{:S(2)}, u32[]{:S(2)}) %collective-permute-start.11) | collective-permute-done | bytes 262176 | tf_op jit(solution)/shard_map/ppermute | solution.py:371
  71.3 5.7 %collective-permute-done.12.refs_3_ = bf16[2,8,64,128]{3,2,1,0:T(8,128)(2,1)S(1)} collective-permute-done((bf16[2,8,64,128]{3,2,1,0:T(8,128)(2,1)S(1)}, bf16[2,8,64,128]{3,2,1,0:T(8,128)(2,1)S(1)}, u32[]{:S(2)}, u32[]{:S(2)}) %collective-permute-start.12) | collective-permute-done | bytes 262176 | tf_op jit(solution)/shard_map/ppermute | solution.py:371
  77.0 1.3 %axial.2 = (bf16[8,64,512]{2,1,0:T(8,128)(2,1)S(1)}, bf16[8,64,512]{2,1,0:T(8,128)(2,1)S(1)}, bf16[8,64,512]{2,1,0:T(8,128)(2,1)S(1)}, bf16[8,64,512]{2,1,0:T(8,128)(2,1)S(1)}) custom-call(s32[9]{0:T(128)S(1)} %pad_add_fusion.order_ref, bf16[2,8,64,128]{3,2,1,0:T(8,128)(2,1)S(1)} %get-tuple-element.86.refs_0_, ...), custom_call_target="tpu_custom_call" | custom-call | flops 536870912 | bytes 5242916 | tf_op jit(solution)/shard_map/axial/pallas_call | solution.py:32
  78.3 0.1 collective-permute-start.16
  78.4 6.5 %collective-permute-start.17 = (bf16[8,64,512]{2,1,0:T(8,128)(2,1)S(1)}, bf16[8,64,512]{2,1,0:T(8,128)(2,1)S(1)}, u32[]{:S(2)}, u32[]{:S(2)}) collective-permute-start(bf16[8,64,512]{2,1,0:T(8,128)(2,1)S(1)} %get-tuple-element.104), channel_id=1, source_target_pairs={{4,8},{8,4},{5,9},{9,5},{6,10},{10,6},{7,11},{11,7},{12,16},{16,12... | collective-permute-start | bytes 1572872 | tf_op jit(solution)/shard_map/ppermute | solution.py:395
  85.0 0.0 collective-permute-start.18
  85.0 1.4 %collective-permute-start.19 = (bf16[8,64,512]{2,1,0:T(8,128)(2,1)S(1)}, bf16[8,64,512]{2,1,0:T(8,128)(2,1)S(1)}, u32[]{:S(2)}, u32[]{:S(2)}) collective-permute-start(bf16[8,64,512]{2,1,0:T(8,128)(2,1)S(1)} %get-tuple-element.106), channel_id=1, source_target_pairs={{4,8},{8,4},{5,9},{9,5},{6,10},{10,6},{7,11},{11,7},{12,16},{16,12... | collective-permute-start | bytes 1572872 | tf_op jit(solution)/shard_map/ppermute | solution.py:395
  86.3 5.3 %collective-permute-done.16.refs_4_ = bf16[8,64,512]{2,1,0:T(8,128)(2,1)S(1)} collective-permute-done((bf16[8,64,512]{2,1,0:T(8,128)(2,1)S(1)}, bf16[8,64,512]{2,1,0:T(8,128)(2,1)S(1)}, u32[]{:S(2)}, u32[]{:S(2)}) %collective-permute-start.16) | collective-permute-done | bytes 524320 | tf_op jit(solution)/shard_map/ppermute | solution.py:395
  91.6 6.0 %collective-permute-done.17.refs_5_ = bf16[8,64,512]{2,1,0:T(8,128)(2,1)S(1)} collective-permute-done((bf16[8,64,512]{2,1,0:T(8,128)(2,1)S(1)}, bf16[8,64,512]{2,1,0:T(8,128)(2,1)S(1)}, u32[]{:S(2)}, u32[]{:S(2)}) %collective-permute-start.17) | collective-permute-done | bytes 524320 | tf_op jit(solution)/shard_map/ppermute | solution.py:395
  97.6 1.8 %couple_axial.3 = (bf16[2,8,64,128]{3,2,1,0:T(8,128)(2,1)S(1)}, bf16[2,8,64,128]{3,2,1,0:T(8,128)(2,1)S(1)}, bf16[2,8,64,128]{3,2,1,0:T(8,128)(2,1)S(1)}, bf16[2,8,64,128]{3,2,1,0:T(8,128)(2,1)S(1)}) custom-call(s32[9]{0:T(128)S(1)} %pad_add_fusion.order_ref, bf16[8,64,512]{2,1,0:T(8,128)(2,1)S(1)} %get-tuple-element.91.refs_0_, ...), custom_call_target="tpu_custom_call" | custom-call | flops 1073741824 | bytes 6422564 | tf_op jit(solution)/shard_map/couple_axial/pallas_call | solution.py:32
  99.4 0.5 collective-permute-start.23
  99.9 1.2 collective-permute-start.24
  101.1 2.0 %collective-permute-start.25 = (bf16[2,8,64,128]{3,2,1,0:T(8,128)(2,1)S(1)}, bf16[2,8,64,128]{3,2,1,0:T(8,128)(2,1)S(1)}, u32[]{:S(2)}, u32[]{:S(2)}) collective-permute-start(bf16[2,8,64,128]{3,2,1,0:T(8,128)(2,1)S(1)} %get-tuple-element.116), channel_id=1, source_target_pairs={{0,3},{1,2},{2,1},{3,0},{4,7},{5,6},{6,5},{7,4},{8,11},{9,10},{10,... | collective-permute-start | bytes 786440 | tf_op jit(solution)/shard_map/ppermute | solution.py:371
  103.1 0.0 collective-permute-done.18.refs_6_
  103.1 6.0 %collective-permute-done.19.refs_7_ = bf16[8,64,512]{2,1,0:T(8,128)(2,1)S(1)} collective-permute-done((bf16[8,64,512]{2,1,0:T(8,128)(2,1)S(1)}, bf16[8,64,512]{2,1,0:T(8,128)(2,1)S(1)}, u32[]{:S(2)}, u32[]{:S(2)}) %collective-permute-start.19) | collective-permute-done | bytes 524320 | tf_op jit(solution)/shard_map/ppermute | solution.py:395
  109.1 1.9 %couple_axial.2 = (bf16[2,8,64,128]{3,2,1,0:T(8,128)(2,1)S(1)}, bf16[2,8,64,128]{3,2,1,0:T(8,128)(2,1)S(1)}, bf16[2,8,64,128]{3,2,1,0:T(8,128)(2,1)S(1)}, bf16[2,8,64,128]{3,2,1,0:T(8,128)(2,1)S(1)}) custom-call(s32[9]{0:T(128)S(1)} %pad_add_fusion.order_ref, bf16[8,64,512]{2,1,0:T(8,128)(2,1)S(1)} %get-tuple-element.91.refs_0_, ...), custom_call_target="tpu_custom_call" | custom-call | flops 1073741824 | bytes 7471140 | tf_op jit(solution)/shard_map/couple_axial/pallas_call | solution.py:32
  111.0 0.1 collective-permute-start.20
  111.1 0.8 collective-permute-start.21
  111.9 0.0 collective-permute-done.23.refs_1_
  111.9 2.8 %collective-permute-start.22 = (bf16[2,8,64,128]{3,2,1,0:T(8,128)(2,1)S(1)}, bf16[2,8,64,128]{3,2,1,0:T(8,128)(2,1)S(1)}, u32[]{:S(2)}, u32[]{:S(2)}) collective-permute-start(bf16[2,8,64,128]{3,2,1,0:T(8,128)(2,1)S(1)} %get-tuple-element.111), channel_id=1, source_target_pairs={{0,3},{1,2},{2,1},{3,0},{4,7},{5,6},{6,5},{7,4},{8,11},{9,10},{10,... | collective-permute-start | bytes 786440 | tf_op jit(solution)/shard_map/ppermute | solution.py:371
  114.7 0.0 collective-permute-done.24.refs_2_
  114.7 2.0 %collective-permute-done.25.refs_3_ = bf16[2,8,64,128]{3,2,1,0:T(8,128)(2,1)S(1)} collective-permute-done((bf16[2,8,64,128]{3,2,1,0:T(8,128)(2,1)S(1)}, bf16[2,8,64,128]{3,2,1,0:T(8,128)(2,1)S(1)}, u32[]{:S(2)}, u32[]{:S(2)}) %collective-permute-start.25) | collective-permute-done | bytes 262176 | tf_op jit(solution)/shard_map/ppermute | solution.py:371
  116.8 1.3 radial_last.2.refs_5_
  118.0 0.0 collective-permute-done.20.refs_1_
  118.0 4.2 %collective-permute-done.21.refs_2_ = bf16[2,8,64,128]{3,2,1,0:T(8,128)(2,1)S(1)} collective-permute-done((bf16[2,8,64,128]{3,2,1,0:T(8,128)(2,1)S(1)}, bf16[2,8,64,128]{3,2,1,0:T(8,128)(2,1)S(1)}, u32[]{:S(2)}, u32[]{:S(2)}) %collective-permute-start.21) | collective-permute-done | bytes 262176 | tf_op jit(solution)/shard_map/ppermute | solution.py:371
  122.2 5.6 %collective-permute-done.22.refs_3_ = bf16[2,8,64,128]{3,2,1,0:T(8,128)(2,1)S(1)} collective-permute-done((bf16[2,8,64,128]{3,2,1,0:T(8,128)(2,1)S(1)}, bf16[2,8,64,128]{3,2,1,0:T(8,128)(2,1)S(1)}, u32[]{:S(2)}, u32[]{:S(2)}) %collective-permute-start.22) | collective-permute-done | bytes 262176 | tf_op jit(solution)/shard_map/ppermute | solution.py:371
  127.8 1.3 radial_last.3
  (15 shorter events, 0.0 us)
Async XLA Ops:
  0.1 10.4 %copy-start = (bf16[4,256,256]{2,1,0:T(8,128)(2,1)S(1)}, bf16[4,256,256]{2,1,0:T(8,128)(2,1)}, u32[]{:S(2)}) copy-start(bf16[4,256,256]{2,1,0:T(8,128)(2,1)} %rad_ref.1) | copy-start | bytes 1572868
  0.1 10.4 %copy-start.1 = (f32[4,512]{1,0:T(4,128)S(1)}, f32[4,512]{1,0:T(4,128)}, u32[]{:S(2)}) copy-start(f32[4,512]{1,0:T(4,128)} %damp_ref.1) | copy-start | bytes 24580
  0.1 10.4 %copy-start.2 = (f32[8,8]{1,0:T(8,128)S(1)}, f32[8,8]{1,0:T(8,128)}, u32[]{:S(2)}) copy-start(f32[8,8]{1,0:T(8,128)} %one_ref.1) | copy-start | bytes 772
  0.1 10.4 %copy-start.3 = (f32[8,8]{1,0:T(8,128)S(1)}, f32[8,8]{1,0:T(8,128)}, u32[]{:S(2)}) copy-start(f32[8,8]{1,0:T(8,128)} %two_ref.1) | copy-start | bytes 772
  0.1 10.4 %copy-start.4 = (s32[4]{0:T(128)S(1)}, s32[4]{0:T(128)}, u32[]{:S(2)}) copy-start(s32[4]{0:T(128)} %len_ref.1) | copy-start | bytes 52
  0.1 10.4 %copy-start.5 = (bf16[512,512]{1,0:T(8,128)(2,1)S(1)}, bf16[512,512]{1,0:T(8,128)(2,1)}, u32[]{:S(2)}) copy-start(bf16[512,512]{1,0:T(8,128)(2,1)} %constant.51.clone.q_ref) | copy-start | bytes 1572868
  2.1 13.8 %collective-permute-start = (bf16[2,8,64,128]{3,2,1,0:T(8,128)(2,1)S(1)}, bf16[2,8,64,128]{3,2,1,0:T(8,128)(2,1)S(1)}, u32[]{:S(2)}, u32[]{:S(2)}) collective-permute-start(bf16[2,8,64,128]{3,2,1,0:T(8,128)(2,1)S(1)} %get-tuple-element.66), channel_id=1, source_target_pairs={{0,2},{1,3},{2,0},{3,1},{4,6},{5,7},{6,4},{7,5},{8,10},{9,11},{10,... | collective-permute-start | bytes 786440 | tf_op jit(solution)/shard_map/ppermute | solution.py:371
  5.7 14.0 %collective-permute-start.1 = (bf16[2,8,64,128]{3,2,1,0:T(8,128)(2,1)S(1)}, bf16[2,8,64,128]{3,2,1,0:T(8,128)(2,1)S(1)}, u32[]{:S(2)}, u32[]{:S(2)}) collective-permute-start(bf16[2,8,64,128]{3,2,1,0:T(8,128)(2,1)S(1)} %get-tuple-element.69), channel_id=1, source_target_pairs={{0,1},{1,0},{2,3},{3,2},{4,5},{5,4},{6,7},{7,6},{8,9},{9,8},{10,11... | collective-permute-start | bytes 786440 | tf_op jit(solution)/shard_map/ppermute | solution.py:371
  6.7 13.0 %collective-permute-start.2 = (bf16[2,8,64,128]{3,2,1,0:T(8,128)(2,1)S(1)}, bf16[2,8,64,128]{3,2,1,0:T(8,128)(2,1)S(1)}, u32[]{:S(2)}, u32[]{:S(2)}) collective-permute-start(bf16[2,8,64,128]{3,2,1,0:T(8,128)(2,1)S(1)} %get-tuple-element.71), channel_id=1, source_target_pairs={{0,3},{1,2},{2,1},{3,0},{4,7},{5,6},{6,5},{7,4},{8,11},{9,10},{10,... | collective-permute-start | bytes 786440 | tf_op jit(solution)/shard_map/ppermute | solution.py:371
  15.9 14.0 %collective-permute-start.3 = (bf16[2,8,64,128]{3,2,1,0:T(8,128)(2,1)S(1)}, bf16[2,8,64,128]{3,2,1,0:T(8,128)(2,1)S(1)}, u32[]{:S(2)}, u32[]{:S(2)}) collective-permute-start(bf16[2,8,64,128]{3,2,1,0:T(8,128)(2,1)S(1)} %get-tuple-element.74), channel_id=1, source_target_pairs={{0,1},{1,0},{2,3},{3,2},{4,5},{5,4},{6,7},{7,6},{8,9},{9,8},{10,11... | collective-permute-start | bytes 786440 | tf_op jit(solution)/shard_map/ppermute | solution.py:371
  16.4 13.4 %collective-permute-start.4 = (bf16[2,8,64,128]{3,2,1,0:T(8,128)(2,1)S(1)}, bf16[2,8,64,128]{3,2,1,0:T(8,128)(2,1)S(1)}, u32[]{:S(2)}, u32[]{:S(2)}) collective-permute-start(bf16[2,8,64,128]{3,2,1,0:T(8,128)(2,1)S(1)} %get-tuple-element.75), channel_id=1, source_target_pairs={{0,2},{1,3},{2,0},{3,1},{4,6},{5,7},{6,4},{7,5},{8,10},{9,11},{10,... | collective-permute-start | bytes 786440 | tf_op jit(solution)/shard_map/ppermute | solution.py:371
  17.5 17.3 %collective-permute-start.5 = (bf16[2,8,64,128]{3,2,1,0:T(8,128)(2,1)S(1)}, bf16[2,8,64,128]{3,2,1,0:T(8,128)(2,1)S(1)}, u32[]{:S(2)}, u32[]{:S(2)}) collective-permute-start(bf16[2,8,64,128]{3,2,1,0:T(8,128)(2,1)S(1)} %get-tuple-element.76), channel_id=1, source_target_pairs={{0,3},{1,2},{2,1},{3,0},{4,7},{5,6},{6,5},{7,4},{8,11},{9,10},{10,... | collective-permute-start | bytes 786440 | tf_op jit(solution)/shard_map/ppermute | solution.py:371
  20.4 26.2 %collective-permute-start.6 = (bf16[8,256,128]{2,1,0:T(8,128)(2,1)S(1)}, bf16[8,256,128]{2,1,0:T(8,128)(2,1)S(1)}, u32[]{:S(2)}, u32[]{:S(2)}) collective-permute-start(bf16[8,256,128]{2,1,0:T(8,128)(2,1)S(1)} %get-tuple-element.80), channel_id=1, source_target_pairs={{0,4},{4,0},{1,5},{5,1},{2,6},{6,2},{3,7},{7,3},{8,12},{12,8},{9,1... | collective-permute-start | bytes 1572872 | tf_op jit(solution)/shard_map/ppermute | solution.py:395
  20.6 26.1 %collective-permute-start.7 = (bf16[8,256,128]{2,1,0:T(8,128)(2,1)S(1)}, bf16[8,256,128]{2,1,0:T(8,128)(2,1)S(1)}, u32[]{:S(2)}, u32[]{:S(2)}) collective-permute-start(bf16[8,256,128]{2,1,0:T(8,128)(2,1)S(1)} %get-tuple-element.81), channel_id=1, source_target_pairs={{4,8},{8,4},{5,9},{9,5},{6,10},{10,6},{7,11},{11,7},{12,16},{16,12... | collective-permute-start | bytes 1572872 | tf_op jit(solution)/shard_map/ppermute | solution.py:395
  35.4 16.8 %collective-permute-start.8 = (bf16[8,256,128]{2,1,0:T(8,128)(2,1)S(1)}, bf16[8,256,128]{2,1,0:T(8,128)(2,1)S(1)}, u32[]{:S(2)}, u32[]{:S(2)}) collective-permute-start(bf16[8,256,128]{2,1,0:T(8,128)(2,1)S(1)} %get-tuple-element.82), channel_id=1, source_target_pairs={{0,4},{4,0},{1,5},{5,1},{2,6},{6,2},{3,7},{7,3},{8,12},{12,8},{9,1... | collective-permute-start | bytes 1572872 | tf_op jit(solution)/shard_map/ppermute | solution.py:395
  35.5 23.1 %collective-permute-start.9 = (bf16[8,256,128]{2,1,0:T(8,128)(2,1)S(1)}, bf16[8,256,128]{2,1,0:T(8,128)(2,1)S(1)}, u32[]{:S(2)}, u32[]{:S(2)}) collective-permute-start(bf16[8,256,128]{2,1,0:T(8,128)(2,1)S(1)} %get-tuple-element.83), channel_id=1, source_target_pairs={{4,8},{8,4},{5,9},{9,5},{6,10},{10,6},{7,11},{11,7},{12,16},{16,12... | collective-permute-start | bytes 1572872 | tf_op jit(solution)/shard_map/ppermute | solution.py:395
  48.5 13.5 %collective-permute-start.13 = (bf16[2,8,64,128]{3,2,1,0:T(8,128)(2,1)S(1)}, bf16[2,8,64,128]{3,2,1,0:T(8,128)(2,1)S(1)}, u32[]{:S(2)}, u32[]{:S(2)}) collective-permute-start(bf16[2,8,64,128]{3,2,1,0:T(8,128)(2,1)S(1)} %get-tuple-element.93), channel_id=1, source_target_pairs={{0,1},{1,0},{2,3},{3,2},{4,5},{5,4},{6,7},{7,6},{8,9},{9,8},{10,11... | collective-permute-start | bytes 786440 | tf_op jit(solution)/shard_map/ppermute | solution.py:371
  48.6 15.7 %collective-permute-start.14 = (bf16[2,8,64,128]{3,2,1,0:T(8,128)(2,1)S(1)}, bf16[2,8,64,128]{3,2,1,0:T(8,128)(2,1)S(1)}, u32[]{:S(2)}, u32[]{:S(2)}) collective-permute-start(bf16[2,8,64,128]{3,2,1,0:T(8,128)(2,1)S(1)} %get-tuple-element.94), channel_id=1, source_target_pairs={{0,2},{1,3},{2,0},{3,1},{4,6},{5,7},{6,4},{7,5},{8,10},{9,11},{10,... | collective-permute-start | bytes 786440 | tf_op jit(solution)/shard_map/ppermute | solution.py:371
  49.5 16.6 %collective-permute-start.15 = (bf16[2,8,64,128]{3,2,1,0:T(8,128)(2,1)S(1)}, bf16[2,8,64,128]{3,2,1,0:T(8,128)(2,1)S(1)}, u32[]{:S(2)}, u32[]{:S(2)}) collective-permute-start(bf16[2,8,64,128]{3,2,1,0:T(8,128)(2,1)S(1)} %get-tuple-element.95), channel_id=1, source_target_pairs={{0,3},{1,2},{2,1},{3,0},{4,7},{5,6},{6,5},{7,4},{8,11},{9,10},{10,... | collective-permute-start | bytes 786440 | tf_op jit(solution)/shard_map/ppermute | solution.py:371
  60.5 6.9 %collective-permute-start.10 = (bf16[2,8,64,128]{3,2,1,0:T(8,128)(2,1)S(1)}, bf16[2,8,64,128]{3,2,1,0:T(8,128)(2,1)S(1)}, u32[]{:S(2)}, u32[]{:S(2)}) collective-permute-start(bf16[2,8,64,128]{3,2,1,0:T(8,128)(2,1)S(1)} %get-tuple-element.87), channel_id=1, source_target_pairs={{0,1},{1,0},{2,3},{3,2},{4,5},{5,4},{6,7},{7,6},{8,9},{9,8},{10,11... | collective-permute-start | bytes 786440 | tf_op jit(solution)/shard_map/ppermute | solution.py:371
  60.6 10.6 %collective-permute-start.11 = (bf16[2,8,64,128]{3,2,1,0:T(8,128)(2,1)S(1)}, bf16[2,8,64,128]{3,2,1,0:T(8,128)(2,1)S(1)}, u32[]{:S(2)}, u32[]{:S(2)}) collective-permute-start(bf16[2,8,64,128]{3,2,1,0:T(8,128)(2,1)S(1)} %get-tuple-element.88), channel_id=1, source_target_pairs={{0,2},{1,3},{2,0},{3,1},{4,6},{5,7},{6,4},{7,5},{8,10},{9,11},{10,... | collective-permute-start | bytes 786440 | tf_op jit(solution)/shard_map/ppermute | solution.py:371
  62.0 15.0 %collective-permute-start.12 = (bf16[2,8,64,128]{3,2,1,0:T(8,128)(2,1)S(1)}, bf16[2,8,64,128]{3,2,1,0:T(8,128)(2,1)S(1)}, u32[]{:S(2)}, u32[]{:S(2)}) collective-permute-start(bf16[2,8,64,128]{3,2,1,0:T(8,128)(2,1)S(1)} %get-tuple-element.89), channel_id=1, source_target_pairs={{0,3},{1,2},{2,1},{3,0},{4,7},{5,6},{6,5},{7,4},{8,11},{9,10},{10,... | collective-permute-start | bytes 786440 | tf_op jit(solution)/shard_map/ppermute | solution.py:371
  78.3 13.3 %collective-permute-start.16 = (bf16[8,64,512]{2,1,0:T(8,128)(2,1)S(1)}, bf16[8,64,512]{2,1,0:T(8,128)(2,1)S(1)}, u32[]{:S(2)}, u32[]{:S(2)}) collective-permute-start(bf16[8,64,512]{2,1,0:T(8,128)(2,1)S(1)} %get-tuple-element.103), channel_id=1, source_target_pairs={{0,4},{4,0},{1,5},{5,1},{2,6},{6,2},{3,7},{7,3},{8,12},{12,8},{9,1... | collective-permute-start | bytes 1572872 | tf_op jit(solution)/shard_map/ppermute | solution.py:395
  78.4 19.1 %collective-permute-start.17 = (bf16[8,64,512]{2,1,0:T(8,128)(2,1)S(1)}, bf16[8,64,512]{2,1,0:T(8,128)(2,1)S(1)}, u32[]{:S(2)}, u32[]{:S(2)}) collective-permute-start(bf16[8,64,512]{2,1,0:T(8,128)(2,1)S(1)} %get-tuple-element.104), channel_id=1, source_target_pairs={{4,8},{8,4},{5,9},{9,5},{6,10},{10,6},{7,11},{11,7},{12,16},{16,12... | collective-permute-start | bytes 1572872 | tf_op jit(solution)/shard_map/ppermute | solution.py:395
  85.0 18.2 %collective-permute-start.18 = (bf16[8,64,512]{2,1,0:T(8,128)(2,1)S(1)}, bf16[8,64,512]{2,1,0:T(8,128)(2,1)S(1)}, u32[]{:S(2)}, u32[]{:S(2)}) collective-permute-start(bf16[8,64,512]{2,1,0:T(8,128)(2,1)S(1)} %get-tuple-element.105), channel_id=1, source_target_pairs={{0,4},{4,0},{1,5},{5,1},{2,6},{6,2},{3,7},{7,3},{8,12},{12,8},{9,1... | collective-permute-start | bytes 1572872 | tf_op jit(solution)/shard_map/ppermute | solution.py:395
  85.0 24.2 %collective-permute-start.19 = (bf16[8,64,512]{2,1,0:T(8,128)(2,1)S(1)}, bf16[8,64,512]{2,1,0:T(8,128)(2,1)S(1)}, u32[]{:S(2)}, u32[]{:S(2)}) collective-permute-start(bf16[8,64,512]{2,1,0:T(8,128)(2,1)S(1)} %get-tuple-element.106), channel_id=1, source_target_pairs={{4,8},{8,4},{5,9},{9,5},{6,10},{10,6},{7,11},{11,7},{12,16},{16,12... | collective-permute-start | bytes 1572872 | tf_op jit(solution)/shard_map/ppermute | solution.py:395
  99.4 12.5 %collective-permute-start.23 = (bf16[2,8,64,128]{3,2,1,0:T(8,128)(2,1)S(1)}, bf16[2,8,64,128]{3,2,1,0:T(8,128)(2,1)S(1)}, u32[]{:S(2)}, u32[]{:S(2)}) collective-permute-start(bf16[2,8,64,128]{3,2,1,0:T(8,128)(2,1)S(1)} %get-tuple-element.114), channel_id=1, source_target_pairs={{0,1},{1,0},{2,3},{3,2},{4,5},{5,4},{6,7},{7,6},{8,9},{9,8},{10,11... | collective-permute-start | bytes 786440 | tf_op jit(solution)/shard_map/ppermute | solution.py:371
  99.9 14.9 %collective-permute-start.24 = (bf16[2,8,64,128]{3,2,1,0:T(8,128)(2,1)S(1)}, bf16[2,8,64,128]{3,2,1,0:T(8,128)(2,1)S(1)}, u32[]{:S(2)}, u32[]{:S(2)}) collective-permute-start(bf16[2,8,64,128]{3,2,1,0:T(8,128)(2,1)S(1)} %get-tuple-element.115), channel_id=1, source_target_pairs={{0,2},{1,3},{2,0},{3,1},{4,6},{5,7},{6,4},{7,5},{8,10},{9,11},{10,... | collective-permute-start | bytes 786440 | tf_op jit(solution)/shard_map/ppermute | solution.py:371
  101.1 15.6 %collective-permute-start.25 = (bf16[2,8,64,128]{3,2,1,0:T(8,128)(2,1)S(1)}, bf16[2,8,64,128]{3,2,1,0:T(8,128)(2,1)S(1)}, u32[]{:S(2)}, u32[]{:S(2)}) collective-permute-start(bf16[2,8,64,128]{3,2,1,0:T(8,128)(2,1)S(1)} %get-tuple-element.116), channel_id=1, source_target_pairs={{0,3},{1,2},{2,1},{3,0},{4,7},{5,6},{6,5},{7,4},{8,11},{9,10},{10,... | collective-permute-start | bytes 786440 | tf_op jit(solution)/shard_map/ppermute | solution.py:371
  111.0 7.0 %collective-permute-start.20 = (bf16[2,8,64,128]{3,2,1,0:T(8,128)(2,1)S(1)}, bf16[2,8,64,128]{3,2,1,0:T(8,128)(2,1)S(1)}, u32[]{:S(2)}, u32[]{:S(2)}) collective-permute-start(bf16[2,8,64,128]{3,2,1,0:T(8,128)(2,1)S(1)} %get-tuple-element.109), channel_id=1, source_target_pairs={{0,1},{1,0},{2,3},{3,2},{4,5},{5,4},{6,7},{7,6},{8,9},{9,8},{10,11... | collective-permute-start | bytes 786440 | tf_op jit(solution)/shard_map/ppermute | solution.py:371
  111.1 11.1 %collective-permute-start.21 = (bf16[2,8,64,128]{3,2,1,0:T(8,128)(2,1)S(1)}, bf16[2,8,64,128]{3,2,1,0:T(8,128)(2,1)S(1)}, u32[]{:S(2)}, u32[]{:S(2)}) collective-permute-start(bf16[2,8,64,128]{3,2,1,0:T(8,128)(2,1)S(1)} %get-tuple-element.110), channel_id=1, source_target_pairs={{0,2},{1,3},{2,0},{3,1},{4,6},{5,7},{6,4},{7,5},{8,10},{9,11},{10,... | collective-permute-start | bytes 786440 | tf_op jit(solution)/shard_map/ppermute | solution.py:371
  111.9 15.9 %collective-permute-start.22 = (bf16[2,8,64,128]{3,2,1,0:T(8,128)(2,1)S(1)}, bf16[2,8,64,128]{3,2,1,0:T(8,128)(2,1)S(1)}, u32[]{:S(2)}, u32[]{:S(2)}) collective-permute-start(bf16[2,8,64,128]{3,2,1,0:T(8,128)(2,1)S(1)} %get-tuple-element.111), channel_id=1, source_target_pairs={{0,3},{1,2},{2,1},{3,0},{4,7},{5,6},{6,5},{7,4},{8,11},{9,10},{10,... | collective-permute-start | bytes 786440 | tf_op jit(solution)/shard_map/ppermute | solution.py:371

commit v6 on v5

--- a/solution.py
+++ b/solution.py
@@ -12,7 +12,7 @@
 BF = jnp.bfloat16
 F32 = jnp.float32
 SUB = 16
-VMEM_LIMIT = 16 * 1024 * 1024
+VMEM_LIMIT = 11 * 1024 * 1024
 
 
 def cosine_table(count):

time: 129 us -> 129 us (level)
  no operation moved by 1% of the time
where the time goes in v6:
time: 129 us
  starting transfers between devices  53.9 us (42%)
  waiting for transfers between devices  51.7 us (40%)
  Pallas kernels  23.1 us (18%)
    ppermute x8, starting transfers between devices, exchange(): lax.ppermute(p, ('mode', 'pencil'), pair)  28.6 us
    ppermute x18, waiting for transfers between devices, swap(): lax.ppermute(pieces[k], 'pencil', [(i, i ^ k) for i in range(peers)])  28.1 us
    ppermute x18, starting transfers between devices, swap(): lax.ppermute(pieces[k], 'pencil', [(i, i ^ k) for i in range(peers)])  25.2 us
    ppermute x8, waiting for transfers between devices, exchange(): lax.ppermute(p, ('mode', 'pencil'), pair)  23.6 us
    pallas_call x9, Pallas kernels, call(): pl.pallas_call(kernel, out_shape=outs, in_specs=[pl.BlockSpec(memory_spac...  16.8 us
    pallas_call x2, Pallas kernels, split(): pl.pallas_call(functools.partial(split_kernel, peers, chosen), in_specs=[...  3.85 us
  transfers between devices with their start and end apart: 26, of which 11 were waited for; matrix products, arithmetic and copies ran while one was open for 0% of the time, Pallas kernels for 14%

profile of v6, /device:TPU:1, one launch (start us, length us, event | category | flops | bytes accessed | tf_op | source)
XLA Modules:
  0.0 129.3 jit_solution(16254939398463896798)
XLA Ops:
  0.0 0.1 pad_add_fusion.order_ref
  0.1 0.0 copy-start.4
  0.1 0.0 copy-start.5
  0.1 1.9 %split.3 = (bf16[2,8,64,128]{3,2,1,0:T(8,128)(2,1)S(1)}, bf16[2,8,64,128]{3,2,1,0:T(8,128)(2,1)S(1)}, bf16[2,8,64,128]{3,2,1,0:T(8,128)(2,1)S(1)}, bf16[2,8,64,128]{3,2,1,0:T(8,128)(2,1)S(1)}) custom-call(s32[9]{0:T(128)S(1)} %pad_add_fusion.order_ref, bf16[4,8,64,512]{3,2,1,0:T(8,128)(2,1)} %x_ref.3), custom_call_target="tpu_custom_call" | custom-call | bytes 2097152 | tf_op jit(solution)/shard_map/split/pallas_call | solution.py:137
  2.1 3.7 %collective-permute-start = (bf16[2,8,64,128]{3,2,1,0:T(8,128)(2,1)S(1)}, bf16[2,8,64,128]{3,2,1,0:T(8,128)(2,1)S(1)}, u32[]{:S(2)}, u32[]{:S(2)}) collective-permute-start(bf16[2,8,64,128]{3,2,1,0:T(8,128)(2,1)S(1)} %get-tuple-element.66), channel_id=1, source_target_pairs={{0,2},{1,3},{2,0},{3,1},{4,6},{5,7},{6,4},{7,5},{8,10},{9,11},{10,... | collective-permute-start | bytes 786440 | tf_op jit(solution)/shard_map/ppermute | solution.py:371
  5.7 1.0 collective-permute-start.1
  6.7 1.9 %collective-permute-start.2 = (bf16[2,8,64,128]{3,2,1,0:T(8,128)(2,1)S(1)}, bf16[2,8,64,128]{3,2,1,0:T(8,128)(2,1)S(1)}, u32[]{:S(2)}, u32[]{:S(2)}) collective-permute-start(bf16[2,8,64,128]{3,2,1,0:T(8,128)(2,1)S(1)} %get-tuple-element.71), channel_id=1, source_target_pairs={{0,3},{1,2},{2,1},{3,0},{4,7},{5,6},{6,5},{7,4},{8,11},{9,10},{10,... | collective-permute-start | bytes 786440 | tf_op jit(solution)/shard_map/ppermute | solution.py:371
  8.5 1.9 %split.2 = (bf16[2,8,64,128]{3,2,1,0:T(8,128)(2,1)S(1)}, bf16[2,8,64,128]{3,2,1,0:T(8,128)(2,1)S(1)}, bf16[2,8,64,128]{3,2,1,0:T(8,128)(2,1)S(1)}, bf16[2,8,64,128]{3,2,1,0:T(8,128)(2,1)S(1)}) custom-call(s32[9]{0:T(128)S(1)} %pad_add_fusion.order_ref, bf16[4,8,64,512]{3,2,1,0:T(8,128)(2,1)} %x_ref.3), custom_call_target="tpu_custom_call" | custom-call | bytes 2097152 | tf_op jit(solution)/shard_map/split/pallas_call | solution.py:137
  10.5 5.3 %prepare.1 = (bf16[4,512,512]{2,1,0:T(8,128)(2,1)S(1)}, bf16[4,512,512]{2,1,0:T(8,128)(2,1)S(1)}, bf16[4,256,256]{2,1,0:T(8,128)(2,1)S(1)}, bf16[4,256,256]{2,1,0:T(8,128)(2,1)S(1)}, bf16[128,512]{1,0:T(8,128)(2,1)S(1)}) custom-call(s32[9]{0:T(128)S(1)} %pad_add_fusion.order_ref, s32[4]{0:T(128)S(1)} %copy-done.4, bf16[512,512]{1,0:T(8,128)(2,1)S(1)} %copy-done.5, ...), custom_call_target="tpu_custom_call" | custom-call | flops 4294967296 | bytes 6431284 | tf_op jit(solution)/shard_map/prepare/pallas_call | solution.py:32
  15.8 0.0 collective-permute-done.refs_2_
  15.9 0.6 collective-permute-start.3
  16.4 1.0 collective-permute-start.4
  17.5 2.2 %collective-permute-start.5 = (bf16[2,8,64,128]{3,2,1,0:T(8,128)(2,1)S(1)}, bf16[2,8,64,128]{3,2,1,0:T(8,128)(2,1)S(1)}, u32[]{:S(2)}, u32[]{:S(2)}) collective-permute-start(bf16[2,8,64,128]{3,2,1,0:T(8,128)(2,1)S(1)} %get-tuple-element.76), channel_id=1, source_target_pairs={{0,3},{1,2},{2,1},{3,0},{4,7},{5,6},{6,5},{7,4},{8,11},{9,10},{10,... | collective-permute-start | bytes 786440 | tf_op jit(solution)/shard_map/ppermute | solution.py:371
  19.7 0.0 collective-permute-done.1.refs_1_
  19.7 0.0 collective-permute-done.2.refs_3_
  19.7 0.7 assemble.2
  20.4 0.2 collective-permute-start.6
  20.6 9.3 %collective-permute-start.7 = (bf16[8,256,128]{2,1,0:T(8,128)(2,1)S(1)}, bf16[8,256,128]{2,1,0:T(8,128)(2,1)S(1)}, u32[]{:S(2)}, u32[]{:S(2)}) collective-permute-start(bf16[8,256,128]{2,1,0:T(8,128)(2,1)S(1)} %get-tuple-element.81), channel_id=1, source_target_pairs={{4,8},{8,4},{5,9},{9,5},{6,10},{10,6},{7,11},{11,7},{12,16},{16,12... | collective-permute-start | bytes 1572872 | tf_op jit(solution)/shard_map/ppermute | solution.py:395
  29.9 0.0 collective-permute-done.3.refs_1_
  29.9 0.0 collective-permute-done.4.refs_2_
  29.9 4.9 %collective-permute-done.5.refs_3_ = bf16[2,8,64,128]{3,2,1,0:T(8,128)(2,1)S(1)} collective-permute-done((bf16[2,8,64,128]{3,2,1,0:T(8,128)(2,1)S(1)}, bf16[2,8,64,128]{3,2,1,0:T(8,128)(2,1)S(1)}, u32[]{:S(2)}, u32[]{:S(2)}) %collective-permute-start.5) | collective-permute-done | bytes 262176 | tf_op jit(solution)/shard_map/ppermute | solution.py:371
  34.7 0.7 assemble.3
  35.4 0.1 collective-permute-start.8
  35.5 11.1 %collective-permute-start.9 = (bf16[8,256,128]{2,1,0:T(8,128)(2,1)S(1)}, bf16[8,256,128]{2,1,0:T(8,128)(2,1)S(1)}, u32[]{:S(2)}, u32[]{:S(2)}) collective-permute-start(bf16[8,256,128]{2,1,0:T(8,128)(2,1)S(1)} %get-tuple-element.83), channel_id=1, source_target_pairs={{4,8},{8,4},{5,9},{9,5},{6,10},{10,6},{7,11},{11,7},{12,16},{16,12... | collective-permute-start | bytes 1572872 | tf_op jit(solution)/shard_map/ppermute | solution.py:395
  46.6 1.9 %couple_radial.3 = (bf16[2,8,64,128]{3,2,1,0:T(8,128)(2,1)S(1)}, bf16[2,8,64,128]{3,2,1,0:T(8,128)(2,1)S(1)}, bf16[2,8,64,128]{3,2,1,0:T(8,128)(2,1)S(1)}, bf16[2,8,64,128]{3,2,1,0:T(8,128)(2,1)S(1)}) custom-call(s32[9]{0:T(128)S(1)} %pad_add_fusion.order_ref, bf16[8,256,128]{2,1,0:T(8,128)(2,1)S(1)} %get-tuple-element.72.refs_0_, ...), custom_call_target="tpu_custom_call" | custom-call | flops 805306368 | bytes 4849700 | tf_op jit(solution)/shard_map/couple_radial/pallas_call | solution.py:32
  48.5 0.1 collective-permute-start.13
  48.6 0.9 collective-permute-start.14
  49.5 2.7 %collective-permute-start.15 = (bf16[2,8,64,128]{3,2,1,0:T(8,128)(2,1)S(1)}, bf16[2,8,64,128]{3,2,1,0:T(8,128)(2,1)S(1)}, u32[]{:S(2)}, u32[]{:S(2)}) collective-permute-start(bf16[2,8,64,128]{3,2,1,0:T(8,128)(2,1)S(1)} %get-tuple-element.95), channel_id=1, source_target_pairs={{0,3},{1,2},{2,1},{3,0},{4,7},{5,6},{6,5},{7,4},{8,11},{9,10},{10,... | collective-permute-start | bytes 786440 | tf_op jit(solution)/shard_map/ppermute | solution.py:371
  52.2 0.0 collective-permute-done.8.refs_6_
  52.2 6.4 %collective-permute-done.9.refs_7_ = bf16[8,256,128]{2,1,0:T(8,128)(2,1)S(1)} collective-permute-done((bf16[8,256,128]{2,1,0:T(8,128)(2,1)S(1)}, bf16[8,256,128]{2,1,0:T(8,128)(2,1)S(1)}, u32[]{:S(2)}, u32[]{:S(2)}) %collective-permute-start.9) | collective-permute-done | bytes 524320 | tf_op jit(solution)/shard_map/ppermute | solution.py:395
  58.6 1.9 %couple_radial.2 = (bf16[2,8,64,128]{3,2,1,0:T(8,128)(2,1)S(1)}, bf16[2,8,64,128]{3,2,1,0:T(8,128)(2,1)S(1)}, bf16[2,8,64,128]{3,2,1,0:T(8,128)(2,1)S(1)}, bf16[2,8,64,128]{3,2,1,0:T(8,128)(2,1)S(1)}) custom-call(s32[9]{0:T(128)S(1)} %pad_add_fusion.order_ref, bf16[8,256,128]{2,1,0:T(8,128)(2,1)S(1)} %get-tuple-element.72.refs_0_, ...), custom_call_target="tpu_custom_call" | custom-call | flops 805306368 | bytes 5898276 | tf_op jit(solution)/shard_map/couple_radial/pallas_call | solution.py:32
  60.5 0.1 collective-permute-start.10
  60.6 1.4 %collective-permute-start.11 = (bf16[2,8,64,128]{3,2,1,0:T(8,128)(2,1)S(1)}, bf16[2,8,64,128]{3,2,1,0:T(8,128)(2,1)S(1)}, u32[]{:S(2)}, u32[]{:S(2)}) collective-permute-start(bf16[2,8,64,128]{3,2,1,0:T(8,128)(2,1)S(1)} %get-tuple-element.88), channel_id=1, source_target_pairs={{0,2},{1,3},{2,0},{3,1},{4,6},{5,7},{6,4},{7,5},{8,10},{9,11},{10,... | collective-permute-start | bytes 786440 | tf_op jit(solution)/shard_map/ppermute | solution.py:371
  62.0 2.3 %collective-permute-start.12 = (bf16[2,8,64,128]{3,2,1,0:T(8,128)(2,1)S(1)}, bf16[2,8,64,128]{3,2,1,0:T(8,128)(2,1)S(1)}, u32[]{:S(2)}, u32[]{:S(2)}) collective-permute-start(bf16[2,8,64,128]{3,2,1,0:T(8,128)(2,1)S(1)} %get-tuple-element.89), channel_id=1, source_target_pairs={{0,3},{1,2},{2,1},{3,0},{4,7},{5,6},{6,5},{7,4},{8,11},{9,10},{10,... | collective-permute-start | bytes 786440 | tf_op jit(solution)/shard_map/ppermute | solution.py:371
  64.3 1.8 %collective-permute-done.15.refs_3_ = bf16[2,8,64,128]{3,2,1,0:T(8,128)(2,1)S(1)} collective-permute-done((bf16[2,8,64,128]{3,2,1,0:T(8,128)(2,1)S(1)}, bf16[2,8,64,128]{3,2,1,0:T(8,128)(2,1)S(1)}, u32[]{:S(2)}, u32[]{:S(2)}) %collective-permute-start.15) | collective-permute-done | bytes 262176 | tf_op jit(solution)/shard_map/ppermute | solution.py:371
  66.1 1.3 %axial.3 = (bf16[8,64,512]{2,1,0:T(8,128)(2,1)S(1)}, bf16[8,64,512]{2,1,0:T(8,128)(2,1)S(1)}, bf16[8,64,512]{2,1,0:T(8,128)(2,1)S(1)}, bf16[8,64,512]{2,1,0:T(8,128)(2,1)S(1)}) custom-call(s32[9]{0:T(128)S(1)} %pad_add_fusion.order_ref, bf16[2,8,64,128]{3,2,1,0:T(8,128)(2,1)S(1)} %get-tuple-element.92.refs_0_, ...), custom_call_target="tpu_custom_call" | custom-call | flops 536870912 | bytes 5242916 | tf_op jit(solution)/shard_map/axial/pallas_call | solution.py:32
  67.4 0.0 collective-permute-done.10.refs_1_
  67.4 3.8 %collective-permute-done.11.refs_2_ = bf16[2,8,64,128]{3,2,1,0:T(8,128)(2,1)S(1)} collective-permute-done((bf16[2,8,64,128]{3,2,1,0:T(8,128)(2,1)S(1)}, bf16[2,8,64,128]{3,2,1,0:T(8,128)(2,1)S(1)}, u32[]{:S(2)}, u32[]{:S(2)}) %collective-permute-start.11) | collective-permute-done | bytes 262176 | tf_op jit(solution)/shard_map/ppermute | solution.py:371
  71.3 5.7 %collective-permute-done.12.refs_3_ = bf16[2,8,64,128]{3,2,1,0:T(8,128)(2,1)S(1)} collective-permute-done((bf16[2,8,64,128]{3,2,1,0:T(8,128)(2,1)S(1)}, bf16[2,8,64,128]{3,2,1,0:T(8,128)(2,1)S(1)}, u32[]{:S(2)}, u32[]{:S(2)}) %collective-permute-start.12) | collective-permute-done | bytes 262176 | tf_op jit(solution)/shard_map/ppermute | solution.py:371
  77.0 1.3 %axial.2 = (bf16[8,64,512]{2,1,0:T(8,128)(2,1)S(1)}, bf16[8,64,512]{2,1,0:T(8,128)(2,1)S(1)}, bf16[8,64,512]{2,1,0:T(8,128)(2,1)S(1)}, bf16[8,64,512]{2,1,0:T(8,128)(2,1)S(1)}) custom-call(s32[9]{0:T(128)S(1)} %pad_add_fusion.order_ref, bf16[2,8,64,128]{3,2,1,0:T(8,128)(2,1)S(1)} %get-tuple-element.86.refs_0_, ...), custom_call_target="tpu_custom_call" | custom-call | flops 536870912 | bytes 5242916 | tf_op jit(solution)/shard_map/axial/pallas_call | solution.py:32
  78.3 0.1 collective-permute-start.16
  78.4 6.5 %collective-permute-start.17 = (bf16[8,64,512]{2,1,0:T(8,128)(2,1)S(1)}, bf16[8,64,512]{2,1,0:T(8,128)(2,1)S(1)}, u32[]{:S(2)}, u32[]{:S(2)}) collective-permute-start(bf16[8,64,512]{2,1,0:T(8,128)(2,1)S(1)} %get-tuple-element.104), channel_id=1, source_target_pairs={{4,8},{8,4},{5,9},{9,5},{6,10},{10,6},{7,11},{11,7},{12,16},{16,12... | collective-permute-start | bytes 1572872 | tf_op jit(solution)/shard_map/ppermute | solution.py:395
  85.0 0.0 collective-permute-start.18
  85.0 1.4 %collective-permute-start.19 = (bf16[8,64,512]{2,1,0:T(8,128)(2,1)S(1)}, bf16[8,64,512]{2,1,0:T(8,128)(2,1)S(1)}, u32[]{:S(2)}, u32[]{:S(2)}) collective-permute-start(bf16[8,64,512]{2,1,0:T(8,128)(2,1)S(1)} %get-tuple-element.106), channel_id=1, source_target_pairs={{4,8},{8,4},{5,9},{9,5},{6,10},{10,6},{7,11},{11,7},{12,16},{16,12... | collective-permute-start | bytes 1572872 | tf_op jit(solution)/shard_map/ppermute | solution.py:395
  86.3 5.3 %collective-permute-done.16.refs_4_ = bf16[8,64,512]{2,1,0:T(8,128)(2,1)S(1)} collective-permute-done((bf16[8,64,512]{2,1,0:T(8,128)(2,1)S(1)}, bf16[8,64,512]{2,1,0:T(8,128)(2,1)S(1)}, u32[]{:S(2)}, u32[]{:S(2)}) %collective-permute-start.16) | collective-permute-done | bytes 524320 | tf_op jit(solution)/shard_map/ppermute | solution.py:395
  91.6 6.0 %collective-permute-done.17.refs_5_ = bf16[8,64,512]{2,1,0:T(8,128)(2,1)S(1)} collective-permute-done((bf16[8,64,512]{2,1,0:T(8,128)(2,1)S(1)}, bf16[8,64,512]{2,1,0:T(8,128)(2,1)S(1)}, u32[]{:S(2)}, u32[]{:S(2)}) %collective-permute-start.17) | collective-permute-done | bytes 524320 | tf_op jit(solution)/shard_map/ppermute | solution.py:395
  97.6 1.8 %couple_axial.3 = (bf16[2,8,64,128]{3,2,1,0:T(8,128)(2,1)S(1)}, bf16[2,8,64,128]{3,2,1,0:T(8,128)(2,1)S(1)}, bf16[2,8,64,128]{3,2,1,0:T(8,128)(2,1)S(1)}, bf16[2,8,64,128]{3,2,1,0:T(8,128)(2,1)S(1)}) custom-call(s32[9]{0:T(128)S(1)} %pad_add_fusion.order_ref, bf16[8,64,512]{2,1,0:T(8,128)(2,1)S(1)} %get-tuple-element.91.refs_0_, ...), custom_call_target="tpu_custom_call" | custom-call | flops 1073741824 | bytes 6422564 | tf_op jit(solution)/shard_map/couple_axial/pallas_call | solution.py:32
  99.4 0.5 collective-permute-start.23
  99.9 1.2 collective-permute-start.24
  101.1 2.0 %collective-permute-start.25 = (bf16[2,8,64,128]{3,2,1,0:T(8,128)(2,1)S(1)}, bf16[2,8,64,128]{3,2,1,0:T(8,128)(2,1)S(1)}, u32[]{:S(2)}, u32[]{:S(2)}) collective-permute-start(bf16[2,8,64,128]{3,2,1,0:T(8,128)(2,1)S(1)} %get-tuple-element.116), channel_id=1, source_target_pairs={{0,3},{1,2},{2,1},{3,0},{4,7},{5,6},{6,5},{7,4},{8,11},{9,10},{10,... | collective-permute-start | bytes 786440 | tf_op jit(solution)/shard_map/ppermute | solution.py:371
  103.1 0.0 collective-permute-done.18.refs_6_
  103.1 6.0 %collective-permute-done.19.refs_7_ = bf16[8,64,512]{2,1,0:T(8,128)(2,1)S(1)} collective-permute-done((bf16[8,64,512]{2,1,0:T(8,128)(2,1)S(1)}, bf16[8,64,512]{2,1,0:T(8,128)(2,1)S(1)}, u32[]{:S(2)}, u32[]{:S(2)}) %collective-permute-start.19) | collective-permute-done | bytes 524320 | tf_op jit(solution)/shard_map/ppermute | solution.py:395
  109.1 1.9 %couple_axial.2 = (bf16[2,8,64,128]{3,2,1,0:T(8,128)(2,1)S(1)}, bf16[2,8,64,128]{3,2,1,0:T(8,128)(2,1)S(1)}, bf16[2,8,64,128]{3,2,1,0:T(8,128)(2,1)S(1)}, bf16[2,8,64,128]{3,2,1,0:T(8,128)(2,1)S(1)}) custom-call(s32[9]{0:T(128)S(1)} %pad_add_fusion.order_ref, bf16[8,64,512]{2,1,0:T(8,128)(2,1)S(1)} %get-tuple-element.91.refs_0_, ...), custom_call_target="tpu_custom_call" | custom-call | flops 1073741824 | bytes 7471140 | tf_op jit(solution)/shard_map/couple_axial/pallas_call | solution.py:32
  111.0 0.1 collective-permute-start.20
  111.1 0.8 collective-permute-start.21
  111.9 0.0 collective-permute-done.23.refs_1_
  111.9 2.8 %collective-permute-start.22 = (bf16[2,8,64,128]{3,2,1,0:T(8,128)(2,1)S(1)}, bf16[2,8,64,128]{3,2,1,0:T(8,128)(2,1)S(1)}, u32[]{:S(2)}, u32[]{:S(2)}) collective-permute-start(bf16[2,8,64,128]{3,2,1,0:T(8,128)(2,1)S(1)} %get-tuple-element.111), channel_id=1, source_target_pairs={{0,3},{1,2},{2,1},{3,0},{4,7},{5,6},{6,5},{7,4},{8,11},{9,10},{10,... | collective-permute-start | bytes 786440 | tf_op jit(solution)/shard_map/ppermute | solution.py:371
  114.7 0.0 collective-permute-done.24.refs_2_
  114.7 2.0 %collective-permute-done.25.refs_3_ = bf16[2,8,64,128]{3,2,1,0:T(8,128)(2,1)S(1)} collective-permute-done((bf16[2,8,64,128]{3,2,1,0:T(8,128)(2,1)S(1)}, bf16[2,8,64,128]{3,2,1,0:T(8,128)(2,1)S(1)}, u32[]{:S(2)}, u32[]{:S(2)}) %collective-permute-start.25) | collective-permute-done | bytes 262176 | tf_op jit(solution)/shard_map/ppermute | solution.py:371
  116.8 1.3 radial_last.2.refs_5_
  118.0 0.0 collective-permute-done.20.refs_1_
  118.0 4.2 %collective-permute-done.21.refs_2_ = bf16[2,8,64,128]{3,2,1,0:T(8,128)(2,1)S(1)} collective-permute-done((bf16[2,8,64,128]{3,2,1,0:T(8,128)(2,1)S(1)}, bf16[2,8,64,128]{3,2,1,0:T(8,128)(2,1)S(1)}, u32[]{:S(2)}, u32[]{:S(2)}) %collective-permute-start.21) | collective-permute-done | bytes 262176 | tf_op jit(solution)/shard_map/ppermute | solution.py:371
  122.2 5.6 %collective-permute-done.22.refs_3_ = bf16[2,8,64,128]{3,2,1,0:T(8,128)(2,1)S(1)} collective-permute-done((bf16[2,8,64,128]{3,2,1,0:T(8,128)(2,1)S(1)}, bf16[2,8,64,128]{3,2,1,0:T(8,128)(2,1)S(1)}, u32[]{:S(2)}, u32[]{:S(2)}) %collective-permute-start.22) | collective-permute-done | bytes 262176 | tf_op jit(solution)/shard_map/ppermute | solution.py:371
  127.8 1.3 radial_last.3
  (15 shorter events, 0.0 us)
Async XLA Ops:
  0.1 10.4 %copy-start = (bf16[4,256,256]{2,1,0:T(8,128)(2,1)S(1)}, bf16[4,256,256]{2,1,0:T(8,128)(2,1)}, u32[]{:S(2)}) copy-start(bf16[4,256,256]{2,1,0:T(8,128)(2,1)} %rad_ref.1) | copy-start | bytes 1572868
  0.1 10.4 %copy-start.1 = (f32[4,512]{1,0:T(4,128)S(1)}, f32[4,512]{1,0:T(4,128)}, u32[]{:S(2)}) copy-start(f32[4,512]{1,0:T(4,128)} %damp_ref.1) | copy-start | bytes 24580
  0.1 10.4 %copy-start.2 = (f32[8,8]{1,0:T(8,128)S(1)}, f32[8,8]{1,0:T(8,128)}, u32[]{:S(2)}) copy-start(f32[8,8]{1,0:T(8,128)} %one_ref.1) | copy-start | bytes 772
  0.1 10.4 %copy-start.3 = (f32[8,8]{1,0:T(8,128)S(1)}, f32[8,8]{1,0:T(8,128)}, u32[]{:S(2)}) copy-start(f32[8,8]{1,0:T(8,128)} %two_ref.1) | copy-start | bytes 772
  0.1 10.4 %copy-start.4 = (s32[4]{0:T(128)S(1)}, s32[4]{0:T(128)}, u32[]{:S(2)}) copy-start(s32[4]{0:T(128)} %len_ref.1) | copy-start | bytes 52
  0.1 10.4 %copy-start.5 = (bf16[512,512]{1,0:T(8,128)(2,1)S(1)}, bf16[512,512]{1,0:T(8,128)(2,1)}, u32[]{:S(2)}) copy-start(bf16[512,512]{1,0:T(8,128)(2,1)} %constant.51.clone.q_ref) | copy-start | bytes 1572868
  2.1 13.8 %collective-permute-start = (bf16[2,8,64,128]{3,2,1,0:T(8,128)(2,1)S(1)}, bf16[2,8,64,128]{3,2,1,0:T(8,128)(2,1)S(1)}, u32[]{:S(2)}, u32[]{:S(2)}) collective-permute-start(bf16[2,8,64,128]{3,2,1,0:T(8,128)(2,1)S(1)} %get-tuple-element.66), channel_id=1, source_target_pairs={{0,2},{1,3},{2,0},{3,1},{4,6},{5,7},{6,4},{7,5},{8,10},{9,11},{10,... | collective-permute-start | bytes 786440 | tf_op jit(solution)/shard_map/ppermute | solution.py:371
  5.7 14.0 %collective-permute-start.1 = (bf16[2,8,64,128]{3,2,1,0:T(8,128)(2,1)S(1)}, bf16[2,8,64,128]{3,2,1,0:T(8,128)(2,1)S(1)}, u32[]{:S(2)}, u32[]{:S(2)}) collective-permute-start(bf16[2,8,64,128]{3,2,1,0:T(8,128)(2,1)S(1)} %get-tuple-element.69), channel_id=1, source_target_pairs={{0,1},{1,0},{2,3},{3,2},{4,5},{5,4},{6,7},{7,6},{8,9},{9,8},{10,11... | collective-permute-start | bytes 786440 | tf_op jit(solution)/shard_map/ppermute | solution.py:371
  6.7 13.0 %collective-permute-start.2 = (bf16[2,8,64,128]{3,2,1,0:T(8,128)(2,1)S(1)}, bf16[2,8,64,128]{3,2,1,0:T(8,128)(2,1)S(1)}, u32[]{:S(2)}, u32[]{:S(2)}) collective-permute-start(bf16[2,8,64,128]{3,2,1,0:T(8,128)(2,1)S(1)} %get-tuple-element.71), channel_id=1, source_target_pairs={{0,3},{1,2},{2,1},{3,0},{4,7},{5,6},{6,5},{7,4},{8,11},{9,10},{10,... | collective-permute-start | bytes 786440 | tf_op jit(solution)/shard_map/ppermute | solution.py:371
  15.9 14.0 %collective-permute-start.3 = (bf16[2,8,64,128]{3,2,1,0:T(8,128)(2,1)S(1)}, bf16[2,8,64,128]{3,2,1,0:T(8,128)(2,1)S(1)}, u32[]{:S(2)}, u32[]{:S(2)}) collective-permute-start(bf16[2,8,64,128]{3,2,1,0:T(8,128)(2,1)S(1)} %get-tuple-element.74), channel_id=1, source_target_pairs={{0,1},{1,0},{2,3},{3,2},{4,5},{5,4},{6,7},{7,6},{8,9},{9,8},{10,11... | collective-permute-start | bytes 786440 | tf_op jit(solution)/shard_map/ppermute | solution.py:371
  16.4 13.4 %collective-permute-start.4 = (bf16[2,8,64,128]{3,2,1,0:T(8,128)(2,1)S(1)}, bf16[2,8,64,128]{3,2,1,0:T(8,128)(2,1)S(1)}, u32[]{:S(2)}, u32[]{:S(2)}) collective-permute-start(bf16[2,8,64,128]{3,2,1,0:T(8,128)(2,1)S(1)} %get-tuple-element.75), channel_id=1, source_target_pairs={{0,2},{1,3},{2,0},{3,1},{4,6},{5,7},{6,4},{7,5},{8,10},{9,11},{10,... | collective-permute-start | bytes 786440 | tf_op jit(solution)/shard_map/ppermute | solution.py:371
  17.5 17.3 %collective-permute-start.5 = (bf16[2,8,64,128]{3,2,1,0:T(8,128)(2,1)S(1)}, bf16[2,8,64,128]{3,2,1,0:T(8,128)(2,1)S(1)}, u32[]{:S(2)}, u32[]{:S(2)}) collective-permute-start(bf16[2,8,64,128]{3,2,1,0:T(8,128)(2,1)S(1)} %get-tuple-element.76), channel_id=1, source_target_pairs={{0,3},{1,2},{2,1},{3,0},{4,7},{5,6},{6,5},{7,4},{8,11},{9,10},{10,... | collective-permute-start | bytes 786440 | tf_op jit(solution)/shard_map/ppermute | solution.py:371
  20.4 26.2 %collective-permute-start.6 = (bf16[8,256,128]{2,1,0:T(8,128)(2,1)S(1)}, bf16[8,256,128]{2,1,0:T(8,128)(2,1)S(1)}, u32[]{:S(2)}, u32[]{:S(2)}) collective-permute-start(bf16[8,256,128]{2,1,0:T(8,128)(2,1)S(1)} %get-tuple-element.80), channel_id=1, source_target_pairs={{0,4},{4,0},{1,5},{5,1},{2,6},{6,2},{3,7},{7,3},{8,12},{12,8},{9,1... | collective-permute-start | bytes 1572872 | tf_op jit(solution)/shard_map/ppermute | solution.py:395
  20.6 26.1 %collective-permute-start.7 = (bf16[8,256,128]{2,1,0:T(8,128)(2,1)S(1)}, bf16[8,256,128]{2,1,0:T(8,128)(2,1)S(1)}, u32[]{:S(2)}, u32[]{:S(2)}) collective-permute-start(bf16[8,256,128]{2,1,0:T(8,128)(2,1)S(1)} %get-tuple-element.81), channel_id=1, source_target_pairs={{4,8},{8,4},{5,9},{9,5},{6,10},{10,6},{7,11},{11,7},{12,16},{16,12... | collective-permute-start | bytes 1572872 | tf_op jit(solution)/shard_map/ppermute | solution.py:395
  35.4 16.8 %collective-permute-start.8 = (bf16[8,256,128]{2,1,0:T(8,128)(2,1)S(1)}, bf16[8,256,128]{2,1,0:T(8,128)(2,1)S(1)}, u32[]{:S(2)}, u32[]{:S(2)}) collective-permute-start(bf16[8,256,128]{2,1,0:T(8,128)(2,1)S(1)} %get-tuple-element.82), channel_id=1, source_target_pairs={{0,4},{4,0},{1,5},{5,1},{2,6},{6,2},{3,7},{7,3},{8,12},{12,8},{9,1... | collective-permute-start | bytes 1572872 | tf_op jit(solution)/shard_map/ppermute | solution.py:395
  35.5 23.1 %collective-permute-start.9 = (bf16[8,256,128]{2,1,0:T(8,128)(2,1)S(1)}, bf16[8,256,128]{2,1,0:T(8,128)(2,1)S(1)}, u32[]{:S(2)}, u32[]{:S(2)}) collective-permute-start(bf16[8,256,128]{2,1,0:T(8,128)(2,1)S(1)} %get-tuple-element.83), channel_id=1, source_target_pairs={{4,8},{8,4},{5,9},{9,5},{6,10},{10,6},{7,11},{11,7},{12,16},{16,12... | collective-permute-start | bytes 1572872 | tf_op jit(solution)/shard_map/ppermute | solution.py:395
  48.5 13.5 %collective-permute-start.13 = (bf16[2,8,64,128]{3,2,1,0:T(8,128)(2,1)S(1)}, bf16[2,8,64,128]{3,2,1,0:T(8,128)(2,1)S(1)}, u32[]{:S(2)}, u32[]{:S(2)}) collective-permute-start(bf16[2,8,64,128]{3,2,1,0:T(8,128)(2,1)S(1)} %get-tuple-element.93), channel_id=1, source_target_pairs={{0,1},{1,0},{2,3},{3,2},{4,5},{5,4},{6,7},{7,6},{8,9},{9,8},{10,11... | collective-permute-start | bytes 786440 | tf_op jit(solution)/shard_map/ppermute | solution.py:371
  48.6 15.7 %collective-permute-start.14 = (bf16[2,8,64,128]{3,2,1,0:T(8,128)(2,1)S(1)}, bf16[2,8,64,128]{3,2,1,0:T(8,128)(2,1)S(1)}, u32[]{:S(2)}, u32[]{:S(2)}) collective-permute-start(bf16[2,8,64,128]{3,2,1,0:T(8,128)(2,1)S(1)} %get-tuple-element.94), channel_id=1, source_target_pairs={{0,2},{1,3},{2,0},{3,1},{4,6},{5,7},{6,4},{7,5},{8,10},{9,11},{10,... | collective-permute-start | bytes 786440 | tf_op jit(solution)/shard_map/ppermute | solution.py:371
  49.5 16.6 %collective-permute-start.15 = (bf16[2,8,64,128]{3,2,1,0:T(8,128)(2,1)S(1)}, bf16[2,8,64,128]{3,2,1,0:T(8,128)(2,1)S(1)}, u32[]{:S(2)}, u32[]{:S(2)}) collective-permute-start(bf16[2,8,64,128]{3,2,1,0:T(8,128)(2,1)S(1)} %get-tuple-element.95), channel_id=1, source_target_pairs={{0,3},{1,2},{2,1},{3,0},{4,7},{5,6},{6,5},{7,4},{8,11},{9,10},{10,... | collective-permute-start | bytes 786440 | tf_op jit(solution)/shard_map/ppermute | solution.py:371
  60.5 6.9 %collective-permute-start.10 = (bf16[2,8,64,128]{3,2,1,0:T(8,128)(2,1)S(1)}, bf16[2,8,64,128]{3,2,1,0:T(8,128)(2,1)S(1)}, u32[]{:S(2)}, u32[]{:S(2)}) collective-permute-start(bf16[2,8,64,128]{3,2,1,0:T(8,128)(2,1)S(1)} %get-tuple-element.87), channel_id=1, source_target_pairs={{0,1},{1,0},{2,3},{3,2},{4,5},{5,4},{6,7},{7,6},{8,9},{9,8},{10,11... | collective-permute-start | bytes 786440 | tf_op jit(solution)/shard_map/ppermute | solution.py:371
  60.6 10.6 %collective-permute-start.11 = (bf16[2,8,64,128]{3,2,1,0:T(8,128)(2,1)S(1)}, bf16[2,8,64,128]{3,2,1,0:T(8,128)(2,1)S(1)}, u32[]{:S(2)}, u32[]{:S(2)}) collective-permute-start(bf16[2,8,64,128]{3,2,1,0:T(8,128)(2,1)S(1)} %get-tuple-element.88), channel_id=1, source_target_pairs={{0,2},{1,3},{2,0},{3,1},{4,6},{5,7},{6,4},{7,5},{8,10},{9,11},{10,... | collective-permute-start | bytes 786440 | tf_op jit(solution)/shard_map/ppermute | solution.py:371
  62.0 15.0 %collective-permute-start.12 = (bf16[2,8,64,128]{3,2,1,0:T(8,128)(2,1)S(1)}, bf16[2,8,64,128]{3,2,1,0:T(8,128)(2,1)S(1)}, u32[]{:S(2)}, u32[]{:S(2)}) collective-permute-start(bf16[2,8,64,128]{3,2,1,0:T(8,128)(2,1)S(1)} %get-tuple-element.89), channel_id=1, source_target_pairs={{0,3},{1,2},{2,1},{3,0},{4,7},{5,6},{6,5},{7,4},{8,11},{9,10},{10,... | collective-permute-start | bytes 786440 | tf_op jit(solution)/shard_map/ppermute | solution.py:371
  78.3 13.3 %collective-permute-start.16 = (bf16[8,64,512]{2,1,0:T(8,128)(2,1)S(1)}, bf16[8,64,512]{2,1,0:T(8,128)(2,1)S(1)}, u32[]{:S(2)}, u32[]{:S(2)}) collective-permute-start(bf16[8,64,512]{2,1,0:T(8,128)(2,1)S(1)} %get-tuple-element.103), channel_id=1, source_target_pairs={{0,4},{4,0},{1,5},{5,1},{2,6},{6,2},{3,7},{7,3},{8,12},{12,8},{9,1... | collective-permute-start | bytes 1572872 | tf_op jit(solution)/shard_map/ppermute | solution.py:395
  78.4 19.1 %collective-permute-start.17 = (bf16[8,64,512]{2,1,0:T(8,128)(2,1)S(1)}, bf16[8,64,512]{2,1,0:T(8,128)(2,1)S(1)}, u32[]{:S(2)}, u32[]{:S(2)}) collective-permute-start(bf16[8,64,512]{2,1,0:T(8,128)(2,1)S(1)} %get-tuple-element.104), channel_id=1, source_target_pairs={{4,8},{8,4},{5,9},{9,5},{6,10},{10,6},{7,11},{11,7},{12,16},{16,12... | collective-permute-start | bytes 1572872 | tf_op jit(solution)/shard_map/ppermute | solution.py:395
  85.0 18.2 %collective-permute-start.18 = (bf16[8,64,512]{2,1,0:T(8,128)(2,1)S(1)}, bf16[8,64,512]{2,1,0:T(8,128)(2,1)S(1)}, u32[]{:S(2)}, u32[]{:S(2)}) collective-permute-start(bf16[8,64,512]{2,1,0:T(8,128)(2,1)S(1)} %get-tuple-element.105), channel_id=1, source_target_pairs={{0,4},{4,0},{1,5},{5,1},{2,6},{6,2},{3,7},{7,3},{8,12},{12,8},{9,1... | collective-permute-start | bytes 1572872 | tf_op jit(solution)/shard_map/ppermute | solution.py:395
  85.0 24.2 %collective-permute-start.19 = (bf16[8,64,512]{2,1,0:T(8,128)(2,1)S(1)}, bf16[8,64,512]{2,1,0:T(8,128)(2,1)S(1)}, u32[]{:S(2)}, u32[]{:S(2)}) collective-permute-start(bf16[8,64,512]{2,1,0:T(8,128)(2,1)S(1)} %get-tuple-element.106), channel_id=1, source_target_pairs={{4,8},{8,4},{5,9},{9,5},{6,10},{10,6},{7,11},{11,7},{12,16},{16,12... | collective-permute-start | bytes 1572872 | tf_op jit(solution)/shard_map/ppermute | solution.py:395
  99.4 12.5 %collective-permute-start.23 = (bf16[2,8,64,128]{3,2,1,0:T(8,128)(2,1)S(1)}, bf16[2,8,64,128]{3,2,1,0:T(8,128)(2,1)S(1)}, u32[]{:S(2)}, u32[]{:S(2)}) collective-permute-start(bf16[2,8,64,128]{3,2,1,0:T(8,128)(2,1)S(1)} %get-tuple-element.114), channel_id=1, source_target_pairs={{0,1},{1,0},{2,3},{3,2},{4,5},{5,4},{6,7},{7,6},{8,9},{9,8},{10,11... | collective-permute-start | bytes 786440 | tf_op jit(solution)/shard_map/ppermute | solution.py:371
  99.9 14.9 %collective-permute-start.24 = (bf16[2,8,64,128]{3,2,1,0:T(8,128)(2,1)S(1)}, bf16[2,8,64,128]{3,2,1,0:T(8,128)(2,1)S(1)}, u32[]{:S(2)}, u32[]{:S(2)}) collective-permute-start(bf16[2,8,64,128]{3,2,1,0:T(8,128)(2,1)S(1)} %get-tuple-element.115), channel_id=1, source_target_pairs={{0,2},{1,3},{2,0},{3,1},{4,6},{5,7},{6,4},{7,5},{8,10},{9,11},{10,... | collective-permute-start | bytes 786440 | tf_op jit(solution)/shard_map/ppermute | solution.py:371
  101.1 15.6 %collective-permute-start.25 = (bf16[2,8,64,128]{3,2,1,0:T(8,128)(2,1)S(1)}, bf16[2,8,64,128]{3,2,1,0:T(8,128)(2,1)S(1)}, u32[]{:S(2)}, u32[]{:S(2)}) collective-permute-start(bf16[2,8,64,128]{3,2,1,0:T(8,128)(2,1)S(1)} %get-tuple-element.116), channel_id=1, source_target_pairs={{0,3},{1,2},{2,1},{3,0},{4,7},{5,6},{6,5},{7,4},{8,11},{9,10},{10,... | collective-permute-start | bytes 786440 | tf_op jit(solution)/shard_map/ppermute | solution.py:371
  111.0 7.0 %collective-permute-start.20 = (bf16[2,8,64,128]{3,2,1,0:T(8,128)(2,1)S(1)}, bf16[2,8,64,128]{3,2,1,0:T(8,128)(2,1)S(1)}, u32[]{:S(2)}, u32[]{:S(2)}) collective-permute-start(bf16[2,8,64,128]{3,2,1,0:T(8,128)(2,1)S(1)} %get-tuple-element.109), channel_id=1, source_target_pairs={{0,1},{1,0},{2,3},{3,2},{4,5},{5,4},{6,7},{7,6},{8,9},{9,8},{10,11... | collective-permute-start | bytes 786440 | tf_op jit(solution)/shard_map/ppermute | solution.py:371
  111.1 11.1 %collective-permute-start.21 = (bf16[2,8,64,128]{3,2,1,0:T(8,128)(2,1)S(1)}, bf16[2,8,64,128]{3,2,1,0:T(8,128)(2,1)S(1)}, u32[]{:S(2)}, u32[]{:S(2)}) collective-permute-start(bf16[2,8,64,128]{3,2,1,0:T(8,128)(2,1)S(1)} %get-tuple-element.110), channel_id=1, source_target_pairs={{0,2},{1,3},{2,0},{3,1},{4,6},{5,7},{6,4},{7,5},{8,10},{9,11},{10,... | collective-permute-start | bytes 786440 | tf_op jit(solution)/shard_map/ppermute | solution.py:371
  111.9 15.9 %collective-permute-start.22 = (bf16[2,8,64,128]{3,2,1,0:T(8,128)(2,1)S(1)}, bf16[2,8,64,128]{3,2,1,0:T(8,128)(2,1)S(1)}, u32[]{:S(2)}, u32[]{:S(2)}) collective-permute-start(bf16[2,8,64,128]{3,2,1,0:T(8,128)(2,1)S(1)} %get-tuple-element.111), channel_id=1, source_target_pairs={{0,3},{1,2},{2,1},{3,0},{4,7},{5,6},{6,5},{7,4},{8,11},{9,10},{10,... | collective-permute-start | bytes 786440 | tf_op jit(solution)/shard_map/ppermute | solution.py:371
